TPU v7x, 32 devices: a whole 2x2x4 slice. The times are simulated.
32 devices in a mesh: dom: 8 (over y, x, core), sub: 4 (over z).
Axes of the slice: x: 2, y: 2, z: 4, core: 2. Of those that a mesh axis runs over, the one named last changes fastest.
Arguments:
- adjoint_rhs: float32 [384, 320], P(('dom', 'sub')), may hold values from -6 to 6
- adjoint_start: float32 [384, 320], P(('dom', 'sub')), may hold values from -6 to 6
- offdiag_blocks: bfloat16 [6, 384, 320, 320], P(None, ('dom', 'sub')), may hold values from -0.125 to 0.125
- diag_inverse: float32 [384, 320, 320], P(('dom', 'sub')), may hold values from -0.3125 to 0.3125
- geometry_jac: bfloat16 [384, 24, 320], P(('dom', 'sub')), may hold values from -0.125 to 0.125
- neighbor: int32 [384, 6], P(('dom', 'sub')), may hold values from -1 to 383, as said below
- corner_node: int32 [384, 8], P(('dom', 'sub')), may hold values from 0 to 566, as said below
- deform_place: int32 [567], replicated, may hold values from 0 to 575, as said below
- stiff_diag: float32 [3, 3, 576], P(None, None, ('dom', 'sub')), may hold values from -3.5 to 3.5
- stiff_upper: float32 [3, 3, 576], P(None, None, ('dom', 'sub')), may hold values from -3.5 to 3.5
- stiff_lower: float32 [3, 3, 576], P(None, None, ('dom', 'sub')), may hold values from -3.5 to 3.5
Outputs:
- adjoint: float32 [384, 320], P(('dom', 'sub'))
- shape_grad: float32 [3, 576], P(None, ('dom', 'sub'))
Inputs may be any that keep to these rules, and one draw needn't show every extreme that they name: Elements are numbered device by device in the order of dom then sub, 12 to a device. The relation is symmetric: neighbor[e, k] = f >= 0 implies neighbor[f, k xor 1] = e. A neighbour across face 0 or 1 lies on the same device or on the device one step up (face 0) or down (face 1) along dom with the same sub index; across face 2 or 3 on the same device or one step up (face 2) or down (face 3) along sub; across faces 4 and 5 on the same device. At most 12 faces 0 of one device, and as many faces 1, lead to another device, and at most 6 faces 2, and as many faces 3; these counts are reached. `corner_node`: elements that share a corner name the same node. `deform_place`: the positions are distinct.
All inputs are finite; a program needn't handle non-finite values.
Results may differ from a plain program's by a relative error of at most 0.0042.
Values sent between devices are 32-bit elements; how exact they have to be, the bound alone decides.
No kernel may reach another device: no remote copies, remote signals or barrier semaphores. Data moves between devices by JAX's collectives and lax.ppermute only.
A program may use at most 128 MiB of HBM per device.

v0:
```python
import jax
import jax.numpy as jnp
from jax import lax
from jax.sharding import PartitionSpec as P

NF = 6
BX = 1
BY = 2
BZ = 6
SWEEPS = 2


precise = lax.Precision.HIGHEST


def passed_along(value, axis, steps):
    count = lax.axis_size(axis)
    initial, last = (max(0, -steps), min(count, count - steps))
    return lax.ppermute(value, axis, [(source, source + steps) for source in range(initial, last)])


def padded_2(block, sides, width):
    for axis, dim in sides:
        count = lax.axis_size(axis)
        forward = [(i, i + 1) for i in range(count - 1)]
        backward = [(target, source) for source, target in forward]
        low = lax.ppermute(
            lax.slice_in_dim(block, block.shape[dim] - width, None, axis=dim), axis, forward
        )
        high = lax.ppermute(lax.slice_in_dim(block, 0, width, axis=dim), axis, backward)
        block = jnp.concatenate([low, block, high], axis=dim)
    return block


def dom_move(packed, offset):
    return passed_along(packed, "dom", offset)


def sub_move(packed, offset):
    return passed_along(packed, "sub", offset)


def slot_tables(neighbor, remote, capacity, face_index):
    face_ids = neighbor[:, face_index]
    chosen = remote[:, face_index]
    earlier = chosen[None, :] & (face_ids[None, :] < face_ids[:, None])
    send_rank = jnp.sum(earlier.astype(jnp.int32), 1)
    slot_range = jnp.arange(capacity, dtype=jnp.int32)
    send_table = (chosen[:, None] & (send_rank[:, None] == slot_range[None, :])).astype(jnp.float32)
    receive_rank = jnp.cumsum(chosen.astype(jnp.int32)) - 1
    receive_table = (chosen[:, None] & (receive_rank[:, None] == slot_range[None, :])).astype(
        jnp.float32
    )
    return (send_table, receive_table)


def on_device(
    adjoint_rhs,
    adjoint_start,
    offdiag_blocks,
    diag_inverse,
    geometry_jac,
    neighbor,
    corner_node,
    deform_place,
    stiff_diag,
    stiff_upper,
    stiff_lower,
):
    elem_count = adjoint_rhs.shape[0]
    block_size = adjoint_rhs.shape[1]
    device = lax.axis_index(("dom", "sub"))
    first_id = device * elem_count
    has_face = neighbor >= 0
    inside = has_face & (neighbor >= first_id) & (neighbor < first_id + elem_count)
    remote = has_face & jnp.logical_not(inside)
    target = jnp.where(inside, neighbor - first_id, elem_count)
    columns = jnp.arange(elem_count, dtype=jnp.int32)
    local_map = (
        (target.T[:, :, None] == columns[None, None, :])
        .astype(jnp.float32)
        .reshape(NF * elem_count, elem_count)
    )
    tables = [
        slot_tables(neighbor, remote, BY * BZ, 0),
        slot_tables(neighbor, remote, BY * BZ, 1),
        slot_tables(neighbor, remote, BX * BZ, 2),
        slot_tables(neighbor, remote, BX * BZ, 3),
    ]
    adjoint = adjoint_start
    for sweep_index in range(SWEEPS):
        rounded = adjoint.astype(jnp.bfloat16)
        face_terms = jnp.einsum(
            "keij,ei->kej", offdiag_blocks, rounded, preferred_element_type=jnp.float32
        )
        stacked_terms = face_terms.reshape(NF * elem_count, block_size)
        carried = jnp.dot(local_map.T, stacked_terms, precision=precise)
        for face_index in range(4):
            packed = jnp.dot(tables[face_index][0].T, face_terms[face_index], precision=precise)
            if face_index < 2:
                arrived = dom_move(packed, 1 - 2 * face_index)
            else:
                arrived = sub_move(packed, 5 - 2 * face_index)
            carried = carried + jnp.dot(tables[face_index ^ 1][1], arrived, precision=precise)
        adjoint = jnp.einsum("eij,ej->ei", diag_inverse, adjoint_rhs - carried, precision=precise)
    rounded = adjoint.astype(jnp.bfloat16)
    corner_terms = jnp.einsum(
        "emi,ei->em", geometry_jac, rounded, preferred_element_type=jnp.float32
    )
    values = corner_terms.reshape(elem_count, 8, 3).transpose(2, 0, 1).reshape(3, 8 * elem_count)
    places = deform_place[corner_node.reshape(-1)]
    node_count = stiff_diag.shape[2]
    every_value = lax.all_gather(values, ("dom", "sub"), axis=1, tiled=True)
    every_place = lax.all_gather(places, ("dom", "sub"), axis=0, tiled=True)
    node_slot = every_place - device * node_count
    owned = (node_slot >= 0) & (node_slot < node_count)
    node_slot = jnp.where(owned, node_slot, node_count)
    node_sens = jax.ops.segment_sum(every_value.T, node_slot, node_count + 1)[:node_count].T
    upper_term = jnp.einsum("abq,aq->bq", stiff_upper, node_sens, precision=precise)
    stacked = jnp.concatenate([upper_term, node_sens], 0)
    padded = padded_2(stacked, ((("dom", "sub"), 1),), 1)
    shape_grad = (
        jnp.einsum("abq,aq->bq", stiff_diag, node_sens, precision=precise) + padded[0:3, :-2]
    )
    shape_grad = shape_grad + jnp.einsum(
        "abq,aq->bq", stiff_lower, padded[3:6, 2:], precision=precise
    )
    return (adjoint, shape_grad)


def solution(mesh):
    placed = (
        P(("dom", "sub"), None),
        P(("dom", "sub"), None),
        P(None, ("dom", "sub"), None, None),
        P(("dom", "sub"), None, None),
        P(("dom", "sub"), None, None),
        P(("dom", "sub"), None),
        P(("dom", "sub"), None),
        P(),
        P(None, None, ("dom", "sub")),
        P(None, None, ("dom", "sub")),
        P(None, None, ("dom", "sub")),
    )
    return jax.shard_map(
        on_device,
        mesh=mesh,
        in_specs=placed,
        out_specs=(P(("dom", "sub"), None), P(None, ("dom", "sub"))),
        check_vma=False,
    )
```

profile of v0, /device:TPU:0, one launch (start us, length us, event | category | flops | bytes accessed | tf_op | source)
XLA Modules:
  0.0 203.5 jit_solution(1495273788116148652)
XLA Ops:
  0.7 0.8 slice_bitcast_fusion.24
  1.5 0.7 not_and_fusion
  2.2 0.7 convert_bitcast_fusion.1
  3.0 8.5 %fusion.2 = f32[12,1,6,320]{3,1,2,0:T(1,128)S(1)} fusion(bf16[6,12,320,320]{3,2,1,0:T(8,128)(2,1)} %param.13, bf16[12,320,1,1]{1,0,2,3:T(8,128)(2,1)S(1)} %convert_bitcast_fusion.1), kind=kOutput, calls=%fused_computation.4 | convolution fusion | flops 14745600 | bytes 14845440 | tf_op jit(solution)/shard_map/keij,ei->kej/dot_general | solution.py:93
  11.6 0.3 fusion.20
  11.9 1.3 collective-permute-start.1
  13.7 4.9 %collective-permute-start.2 = (f32[6,320]{1,0:T(8,128)S(1)}, f32[6,320]{1,0:T(8,128)S(1)}, u32[]{:S(2)}, u32[]{:S(2)}) collective-permute-start(f32[6,320]{1,0:T(8,128)S(1)} %fusion.19), channel_id=1, source_target_pairs={{0,1},{1,2},{2,3},{4,5},{5,6},{6,7},{8,9},{9,10},{10,11},{12,13},{... | collective-permute-start | bytes 23048 | tf_op jit(solution)/shard_map/ppermute | solution.py:19
  19.0 1.3 collective-permute-start.3
  20.5 0.3 fusion.21
  20.8 2.8 %collective-permute-start = (f32[12,320]{1,0:T(8,128)S(1)}, f32[12,320]{1,0:T(8,128)S(1)}, u32[]{:S(2)}, u32[]{:S(2)}) collective-permute-start(f32[12,320]{1,0:T(8,128)S(1)} %fusion.21), channel_id=1, source_target_pairs={{0,4},{4,8},{8,12},{12,16},{16,20},{20,24},{24,28},{1,5},{5,9},{9,... | collective-permute-start | bytes 46088 | tf_op jit(solution)/shard_map/ppermute | solution.py:19
  24.6 1.0 gather_fusion
  25.5 0.3 dynamic-update-slice
  25.8 42.5 %all-reduce = s32[3072]{0:T(1024)S(1)} all-reduce(s32[3072]{0:T(1024)S(1)} %dynamic-update-slice), channel_id=2, replica_groups=mesh['dom'=8,'sub'=4] {'dom','sub'}, use_global_device_ids=true, to_apply=%add | all-reduce | flops 3072 | bytes 24576
  69.4 7.5 %fusion.29 = bf16[12,1,320]{2,1,0:T(2,128)(2,1)S(1)} fusion(f32[12,320,320]{2,1,0:T(8,128)} %param.14, f32[12,320,1]{1,0,2:T(8,128)S(1)} %fusion.13), kind=kOutput, calls=%fused_computation.48 | convolution fusion | flops 14745600 | bytes 4938240 | tf_op jit(solution)/shard_map/eij,ej->ei/dot_general | solution.py:105
  77.0 8.6 %fusion = f32[12,1,6,320]{3,1,2,0:T(1,128)S(1)} fusion(bf16[6,12,320,320]{3,2,1,0:T(8,128)(2,1)} %param.13, bf16[12,320,1,1]{1,0,2,3:T(8,128)(2,1)S(1)} %bitcast.130), kind=kOutput, calls=%fused_computation.2 | convolution fusion | flops 14745600 | bytes 14845440 | tf_op jit(solution)/shard_map/keij,ei->kej/dot_general | solution.py:93
  85.9 0.3 fusion.15
  86.1 0.3 fusion.17
  86.4 0.3 fusion.14
  86.7 3.4 %collective-permute-start.6 = (f32[6,320]{1,0:T(8,128)S(1)}, f32[6,320]{1,0:T(8,128)S(1)}, u32[]{:S(2)}, u32[]{:S(2)}) collective-permute-start(f32[6,320]{1,0:T(8,128)S(1)} %fusion.15), channel_id=1, source_target_pairs={{0,1},{1,2},{2,3},{4,5},{5,6},{6,7},{8,9},{9,10},{10,11},{12,13},{... | collective-permute-start | bytes 23048 | tf_op jit(solution)/shard_map/ppermute | solution.py:19
  90.3 1.3 collective-permute-start.5
  91.6 3.0 %collective-permute-start.4 = (f32[12,320]{1,0:T(8,128)S(1)}, f32[12,320]{1,0:T(8,128)S(1)}, u32[]{:S(2)}, u32[]{:S(2)}) collective-permute-start(f32[12,320]{1,0:T(8,128)S(1)} %fusion.17), channel_id=1, source_target_pairs={{0,4},{4,8},{8,12},{12,16},{16,20},{20,24},{24,28},{1,5},{5,9},{9,... | collective-permute-start | bytes 46088 | tf_op jit(solution)/shard_map/ppermute | solution.py:19
  94.7 1.5 collective-permute-start.7
  96.3 3.9 %collective-permute-done.7 = f32[6,320]{1,0:T(8,128)S(1)} collective-permute-done((f32[6,320]{1,0:T(8,128)S(1)}, f32[6,320]{1,0:T(8,128)S(1)}, u32[]{:S(2)}, u32[]{:S(2)}) %collective-permute-start.7) | collective-permute-done | bytes 7712 | tf_op jit(solution)/shard_map/ppermute | solution.py:19
  100.9 5.2 %fusion.26 = f32[12,1,320]{2,1,0:T(1,128)S(1)} fusion(f32[12,320,320]{2,1,0:T(8,128)S(1)} %bitcast.128, f32[12,320,1]{1,0,2:T(8,128)S(1)} %fusion.8), kind=kOutput, calls=%fused_computation.45 | convolution fusion | flops 14745600 | bytes 4945920 | tf_op jit(solution)/shard_map/eij,ej->ei/dot_general | solution.py:105
  106.1 0.6 convert_bitcast_fusion
  107.2 65.2 %all-gather.1 = f32[32,96,3]{1,2,0:T(4,128)S(1)} all-gather(f32[1,96,3]{1,2,0:T(4,128)S(1)} %bitcast.143), channel_id=1, replica_groups=mesh['dom'=8,'sub'=4] {'dom','sub'}, dimensions={0}, use_global_device_ids=true | all-gather | bytes 38016 | tf_op jit(solution)/shard_map/all_gather | solution.py:113
  172.4 0.5 copy.66
  173.0 21.1 %scatter_custom_fusion = f32[19,3]{1,0:T(8,128)S(1)} fusion(s32[3072]{0:T(1024)S(1)} %and_select_fusion, f32[3072,3]{1,0:T(8,128)S(1)} %bitcast.129, f32[]{:T(128)} %constant.34.clone.1), kind=kCustom, calls=%fused_computation.84 | custom fusion | flops 9216 | bytes 232 | tf_op jit(solution)/shard_map/scatter-add | solution.py:118
  194.3 2.9 %collective-permute-start.8 = (f32[6,1]{1,0:T(8,128)S(1)}, f32[6,1]{1,0:T(8,128)S(1)}, u32[]{:S(2)}, u32[]{:S(2)}) collective-permute-start(f32[6,1]{1,0:T(8,128)S(1)} %get-tuple-element.18), channel_id=1, source_target_pairs={{0,1},{1,2},{2,3},{3,4},{4,5},{5,6},{6,7},{7,8},{8,9},{9,10},{10,1... | collective-permute-start | bytes 80 | tf_op jit(solution)/shard_map/ppermute | solution.py:27
  197.2 1.3 collective-permute-start.9
  198.5 4.2 %collective-permute-done.9 = f32[6,1]{1,0:T(8,128)S(1)} collective-permute-done((f32[6,1]{1,0:T(8,128)S(1)}, f32[6,1]{1,0:T(8,128)S(1)}, u32[]{:S(2)}, u32[]{:S(2)}) %collective-permute-start.9) | collective-permute-done | bytes 56 | tf_op jit(solution)/shard_map/ppermute | solution.py:30
  202.9 0.6 bitcast_add_fusion
  (79 shorter events, 5.6 us)
Async XLA Ops:
  0.6 106.1 %copy-start = (bf16[12,24,320]{2,1,0:T(8,128)(2,1)S(1)}, bf16[12,24,320]{2,1,0:T(8,128)(2,1)}, u32[]{:S(2)}) copy-start(bf16[12,24,320]{2,1,0:T(8,128)(2,1)} %param.15) | copy-start | bytes 552964
  2.9 20.6 %copy-start.3 = (s32[12,6]{0,1:T(8,128)S(1)}, s32[12,6]{0,1:T(8,128)}, u32[]{:S(2)}) copy-start(s32[12,6]{0,1:T(8,128)} %param.16) | copy-start | bytes 868
  2.9 21.4 %copy-start.7 = (s32[12,8]{0,1:T(8,128)S(1)}, s32[12,8]{0,1:T(8,128)}, u32[]{:S(2)}) copy-start(s32[12,8]{0,1:T(8,128)} %param.17) | copy-start | bytes 1156
  2.9 21.6 %copy-start.1 = (s32[567]{0:T(1024)S(1)}, s32[567]{0:T(1024)}, u32[]{:S(2)}) copy-start(s32[567]{0:T(1024)} %param.18) | copy-start | bytes 6808
  3.0 66.2 %copy-start.2 = (f32[12,320]{1,0:T(8,128)S(1)}, f32[12,320]{1,0:T(8,128)}, u32[]{:S(2)}) copy-start(f32[12,320]{1,0:T(8,128)} %param.11) | copy-start | bytes 46084
  11.9 57.1 %collective-permute-start.1 = (f32[12,320]{1,0:T(8,128)S(1)}, f32[12,320]{1,0:T(8,128)S(1)}, u32[]{:S(2)}, u32[]{:S(2)}) collective-permute-start(f32[12,320]{1,0:T(8,128)S(1)} %fusion.20), channel_id=1, source_target_pairs={{4,0},{8,4},{12,8},{16,12},{20,16},{24,20},{28,24},{5,1},{9,5},{13... | collective-permute-start | bytes 46088 | tf_op jit(solution)/shard_map/ppermute | solution.py:19
  13.7 54.9 %collective-permute-start.2 = (f32[6,320]{1,0:T(8,128)S(1)}, f32[6,320]{1,0:T(8,128)S(1)}, u32[]{:S(2)}, u32[]{:S(2)}) collective-permute-start(f32[6,320]{1,0:T(8,128)S(1)} %fusion.19), channel_id=1, source_target_pairs={{0,1},{1,2},{2,3},{4,5},{5,6},{6,7},{8,9},{9,10},{10,11},{12,13},{... | collective-permute-start | bytes 23048 | tf_op jit(solution)/shard_map/ppermute | solution.py:19
  19.0 49.7 %collective-permute-start.3 = (f32[6,320]{1,0:T(8,128)S(1)}, f32[6,320]{1,0:T(8,128)S(1)}, u32[]{:S(2)}, u32[]{:S(2)}) collective-permute-start(f32[6,320]{1,0:T(8,128)S(1)} %fusion.18), channel_id=1, source_target_pairs={{1,0},{2,1},{3,2},{5,4},{6,5},{7,6},{9,8},{10,9},{11,10},{13,12},{... | collective-permute-start | bytes 23048 | tf_op jit(solution)/shard_map/ppermute | solution.py:19
  20.8 48.4 %collective-permute-start = (f32[12,320]{1,0:T(8,128)S(1)}, f32[12,320]{1,0:T(8,128)S(1)}, u32[]{:S(2)}, u32[]{:S(2)}) collective-permute-start(f32[12,320]{1,0:T(8,128)S(1)} %fusion.21), channel_id=1, source_target_pairs={{0,4},{4,8},{8,12},{12,16},{16,20},{20,24},{24,28},{1,5},{5,9},{9,... | collective-permute-start | bytes 46088 | tf_op jit(solution)/shard_map/ppermute | solution.py:19
  69.4 31.5 %slice-start = ((s8[5898240]{0:T(1024)(128)(4,1)}), s8[4194304]{0:T(1024)(128)(4,1)S(1)}, s32[]{:S(2)}) async-start(s8[5898240]{0:T(1024)(128)(4,1)} %bitcast.127), calls=%async_computation | async-start | bytes 8388608
  77.0 23.9 %slice-start.1 = ((s8[5898240]{0:T(1024)(128)(4,1)}), s8[1703936]{0:T(1024)(128)(4,1)S(1)}, s32[]{:S(2)}) async-start(s8[5898240]{0:T(1024)(128)(4,1)} %bitcast.127), calls=%async_computation.1 | async-start | bytes 3407872
  85.6 108.7 %copy-start.5 = (f32[3,3,18]{2,1,0:T(4,128)S(1)}, f32[3,3,18]{2,1,0:T(4,128)}, u32[]{:S(2)}) copy-start(f32[3,3,18]{2,1,0:T(4,128)} %param.19) | copy-start | bytes 1948
  85.6 108.7 %copy-start.6 = (f32[3,3,18]{2,1,0:T(4,128)S(1)}, f32[3,3,18]{2,1,0:T(4,128)}, u32[]{:S(2)}) copy-start(f32[3,3,18]{2,1,0:T(4,128)} %param.20) | copy-start | bytes 1948
  85.6 117.3 %copy-start.4 = (f32[3,3,18]{2,1,0:T(4,128)S(1)}, f32[3,3,18]{2,1,0:T(4,128)}, u32[]{:S(2)}) copy-start(f32[3,3,18]{2,1,0:T(4,128)} %param.21) | copy-start | bytes 1948
  86.7 9.5 %collective-permute-start.6 = (f32[6,320]{1,0:T(8,128)S(1)}, f32[6,320]{1,0:T(8,128)S(1)}, u32[]{:S(2)}, u32[]{:S(2)}) collective-permute-start(f32[6,320]{1,0:T(8,128)S(1)} %fusion.15), channel_id=1, source_target_pairs={{0,1},{1,2},{2,3},{4,5},{5,6},{6,7},{8,9},{9,10},{10,11},{12,13},{... | collective-permute-start | bytes 23048 | tf_op jit(solution)/shard_map/ppermute | solution.py:19
  90.3 10.1 %collective-permute-start.5 = (f32[12,320]{1,0:T(8,128)S(1)}, f32[12,320]{1,0:T(8,128)S(1)}, u32[]{:S(2)}, u32[]{:S(2)}) collective-permute-start(f32[12,320]{1,0:T(8,128)S(1)} %fusion.16), channel_id=1, source_target_pairs={{4,0},{8,4},{12,8},{16,12},{20,16},{24,20},{28,24},{5,1},{9,5},{13... | collective-permute-start | bytes 46088 | tf_op jit(solution)/shard_map/ppermute | solution.py:19
  91.6 9.0 %collective-permute-start.4 = (f32[12,320]{1,0:T(8,128)S(1)}, f32[12,320]{1,0:T(8,128)S(1)}, u32[]{:S(2)}, u32[]{:S(2)}) collective-permute-start(f32[12,320]{1,0:T(8,128)S(1)} %fusion.17), channel_id=1, source_target_pairs={{0,4},{4,8},{8,12},{12,16},{16,20},{20,24},{24,28},{1,5},{5,9},{9,... | collective-permute-start | bytes 46088 | tf_op jit(solution)/shard_map/ppermute | solution.py:19
  94.7 5.6 %collective-permute-start.7 = (f32[6,320]{1,0:T(8,128)S(1)}, f32[6,320]{1,0:T(8,128)S(1)}, u32[]{:S(2)}, u32[]{:S(2)}) collective-permute-start(f32[6,320]{1,0:T(8,128)S(1)} %fusion.14), channel_id=1, source_target_pairs={{1,0},{2,1},{3,2},{5,4},{6,5},{7,6},{9,8},{10,9},{11,10},{13,12},{... | collective-permute-start | bytes 23048 | tf_op jit(solution)/shard_map/ppermute | solution.py:19
  194.3 4.2 %collective-permute-start.8 = (f32[6,1]{1,0:T(8,128)S(1)}, f32[6,1]{1,0:T(8,128)S(1)}, u32[]{:S(2)}, u32[]{:S(2)}) collective-permute-start(f32[6,1]{1,0:T(8,128)S(1)} %get-tuple-element.18), channel_id=1, source_target_pairs={{0,1},{1,2},{2,3},{3,4},{4,5},{5,6},{6,7},{7,8},{8,9},{9,10},{10,1... | collective-permute-start | bytes 80 | tf_op jit(solution)/shard_map/ppermute | solution.py:27
  197.2 5.5 %collective-permute-start.9 = (f32[6,1]{1,0:T(8,128)S(1)}, f32[6,1]{1,0:T(8,128)S(1)}, u32[]{:S(2)}, u32[]{:S(2)}) collective-permute-start(f32[6,1]{1,0:T(8,128)S(1)} %get-tuple-element.19), channel_id=1, source_target_pairs={{1,0},{2,1},{3,2},{4,3},{5,4},{6,5},{7,6},{8,7},{9,8},{10,9},{11,1... | collective-permute-start | bytes 80 | tf_op jit(solution)/shard_map/ppermute | solution.py:30
where the time goes:
time: 207 us; the launch traced here: 203 us
  blocking collectives  108 us (52%)
  matrix products  34.2 us (17%)
  other arithmetic  25.4 us (12%)
  starting transfers between devices  23.6 us (11%)
  waiting for transfers between devices  8.12 us (4%)
  local copies, waits for them, and re-layouts  3.49 us (2%)
    all_gather x1, blocking collectives, on_device(): every_value = lax.all_gather(values, ('dom', 'sub'), axis=1, tiled=True)  65.2 us
    unnamed x1, blocking collectives  42.5 us
    scatter-add x1, other arithmetic, on_device(): jax.ops.segment_sum(every_value.T, node_slot, node_count + 1)[:node_count]  21.1 us
    ppermute x8, starting transfers between devices, passed_along(): lax.ppermute(value, axis, [(source, source + steps) for source in range(i...  19.5 us
    dot_general x2, matrix products, on_device(): jnp.einsum('keij,ei->kej', offdiag_blocks, rounded, preferred_element_typ...  17 us
    dot_general x2, matrix products, on_device(): jnp.einsum('eij,ej->ei', diag_inverse, adjoint_rhs - carried, precision=p...  12.8 us
    ppermute x1, waiting for transfers between devices, padded_2(): lax.ppermute(lax.slice_in_dim(block, 0, width, axis=dim), axis, backward)  4.19 us
  transfers between devices with their start and end apart: 10, of which 2 were waited for; matrix products, arithmetic and copies ran while one was open for 3% of the time, Pallas kernels for 0%

commit v1 on v0

v1 whole, which is shorter than its diff:
```python
import jax
import jax.numpy as jnp
from jax import lax
from jax.experimental import pallas as pl
from jax.experimental.pallas import tpu as pltpu
from jax.sharding import PartitionSpec as P

NF = 6
CORNERS = 8
AXES = ("dom", "sub")
ROWS = 16

f32 = jnp.float32
bf16 = jnp.bfloat16
i32 = jnp.int32

IN_HBM = pl.BlockSpec(memory_space=pltpu.HBM)
IN_VMEM = pl.BlockSpec(memory_space=pltpu.VMEM)


def iota(shape, dim):
    return lax.broadcasted_iota(i32, shape, dim)


def up_to(count, multiple):
    return -(-count // multiple) * multiple


def in_three(value):
    first = value.astype(bf16)
    rest = value - first.astype(f32)
    second = rest.astype(bf16)
    return first, second, (rest - second.astype(f32)).astype(bf16)


def one_hot_dot(chooser, value):
    return sum(jnp.dot(chooser, part, preferred_element_type=f32) for part in in_three(value))


def dot_nt(a, b):
    return lax.dot_general(a, b, (((1,), (1,)), ((), ())), preferred_element_type=f32)


def pair_swaps(n_dom, n_sub):
    def at(d, s):
        return d * n_sub + s

    swaps = []
    for first in (0, 1):
        pairs = []
        for s in range(n_sub):
            for d in range(first, n_dom - 1, 2):
                pairs += [(at(d, s), at(d + 1, s)), (at(d + 1, s), at(d, s))]
        swaps.append(pairs)
    for first in (0, 1):
        pairs = []
        for d in range(n_dom):
            for s in range(first, n_sub - 1, 2):
                pairs += [(at(d, s), at(d, s + 1)), (at(d, s + 1), at(d, s))]
        swaps.append(pairs)
    for index in (1, 3):
        used = {source for source, _ in swaps[index]}
        for d in range(n_dom):
            for s in range(n_sub):
                other = (d, s ^ 1) if index == 1 else (d ^ 1, s)
                if at(d, s) in used or other[0] >= n_dom or other[1] >= n_sub:
                    continue
                if at(*other) not in used:
                    swaps[index].append((at(d, s), at(*other)))
    return swaps


def face_products(elem_count, adj_rows, blocks, faces, before=None):
    def one_element(e, _):
        if before is not None:
            before(e)
        row = adj_rows[pl.ds(e, 1), :].astype(bf16)
        for k in range(NF):
            faces[k, pl.ds(e, 1), :] = jnp.dot(row, blocks[k, e], preferred_element_type=f32)
        return 0

    lax.fori_loop(0, elem_count, one_element, 0)


def fill_sends(faces, sends):
    dom_even = lax.axis_index("dom") % 2 == 0
    sub_even = lax.axis_index("sub") % 2 == 0
    sends[0][...] = jnp.where(dom_even, faces[0], faces[1])
    sends[1][...] = jnp.where(dom_even, faces[1], faces[0])
    sends[2][...] = jnp.where(sub_even, faces[2], faces[3])
    sends[3][...] = jnp.where(sub_even, faces[3], faces[2])


def sum_chooser(elem_count, n_sub, neighbor_rows, square):
    dom, sub = lax.axis_index("dom"), lax.axis_index("sub")
    device = dom * n_sub + sub
    first = device * elem_count
    square[...] = jnp.zeros(square.shape, i32)
    square[0:NF, 0:elem_count] = neighbor_rows
    by_element = square[...].T[0:ROWS, :]
    dom_odd, sub_odd = dom % 2, sub % 2
    slots = (dom_odd, 1 - dom_odd, 2 + sub_odd, 3 - sub_odd)
    offsets = (n_sub, -n_sub, 1, -1)
    columns = iota((ROWS, (NF + 4) * ROWS), 1)
    live = iota((ROWS, 1), 0) < elem_count
    total = jnp.zeros(columns.shape, f32)
    for k in range(NF):
        ids = by_element[:, k : k + 1]
        inside = (ids >= first) & (ids < first + elem_count)
        column = (k ^ 1) * ROWS + ids - first
        if k < 4:
            away = (NF + slots[k]) * ROWS + ids - first - offsets[k] * elem_count
            column = jnp.where(inside, column, away)
        column = jnp.where(live & (ids >= 0), column, -1)
        total = total + jnp.where(columns == column, 1.0, 0.0)
    return total


def corner_lanes(elem_count, node_count, corner_rows, place_row):
    width = 3 * CORNERS * elem_count
    lane = iota((CORNERS, width), 1)
    inner = lane - 3 * CORNERS * jnp.floor((lane.astype(f32) + 0.5) / (3 * CORNERS)).astype(i32)
    mine = inner - 3 * iota((CORNERS, width), 0)
    mine = (mine >= 0) & (mine < 3)
    offset = iota((elem_count, width), 1) - 3 * CORNERS * iota((elem_count, width), 0)
    spread = jnp.where((offset >= 0) & (offset < 3 * CORNERS), 1.0, 0.0).astype(bf16)
    corners = corner_rows.astype(f32)
    high = jnp.floor(corners / 128.0)
    low = corners - 128.0 * high
    nodes = 128.0 * jnp.dot(high.astype(bf16), spread, preferred_element_type=f32)
    nodes = nodes + jnp.dot(low.astype(bf16), spread, preferred_element_type=f32)
    nodes = jnp.sum(jnp.where(mine, nodes, 0.0), axis=0, keepdims=True).astype(i32)
    count = place_row.shape[1]
    found = jnp.where(iota((count, width), 0) == nodes, 1.0, 0.0).astype(bf16)
    place = jnp.broadcast_to(place_row.astype(f32), (8, count))
    owner = jnp.floor((place + 0.5) / node_count)
    slot = place - node_count * owner
    pair = jnp.where(iota((8, count), 0) == 0, owner, slot).astype(bf16)
    return jnp.dot(pair, found, preferred_element_type=f32)


def first_sweep(elem_count, n_sub, node_count, start, offdiag, neighbor, corner, place, upper,
                send_0, send_1, send_2, send_3, faces, blocks, chooser, table,
                start_v, neighbor_v, corner_v, place_v, upper_v, square, small_sem, block_sem):
    sends = (send_0, send_1, send_2, send_3)
    small = [
        pltpu.make_async_copy(source, target, small_sem.at[n])
        for n, (source, target) in enumerate(
            ((start, start_v), (neighbor, neighbor_v), (corner, corner_v), (place, place_v),
             (upper, upper_v))
        )
    ]

    def block_copy(e):
        return pltpu.make_async_copy(offdiag.at[:, e], blocks.at[:, e], block_sem.at[e])

    for copy in small:
        copy.start()
    for e in range(elem_count):
        block_copy(e).start()
    faces[...] = jnp.zeros(faces.shape, f32)
    for copy in small:
        copy.wait()
    chooser[...] = sum_chooser(elem_count, n_sub, neighbor_v[...], square)
    table[...] = jnp.zeros(table.shape, f32)
    width = 3 * CORNERS * elem_count
    table[0:8, 0:width] = corner_lanes(elem_count, node_count, corner_v[...], place_v[...])
    base = 3 * (node_count + 2)
    lane, row = iota((3, 128), 1), iota((3, 128), 0)
    last = jnp.zeros((3, 128), f32)
    for a in range(3):
        column = upper_v[a][:, node_count - 1 : node_count]
        last = last + jnp.where(lane == base + 3 * a + row, column, 0.0)
    table[2:3, 0:128] = jnp.sum(last, axis=0, keepdims=True)
    face_products(elem_count, start_v, blocks, faces, before=lambda e: block_copy(e).wait())
    fill_sends(faces, sends)


def apply_inverse(elem_count, rhs, faces, arrived, chooser, inverse, carried_v, columns):
    size = rhs.shape[1]
    terms = jnp.concatenate(
        [faces[...].reshape(NF * ROWS, size)] + [a[...] for a in arrived], axis=0
    )
    carried = one_hot_dot(chooser[...].astype(bf16), terms)
    carried_v[0:elem_count, :] = rhs[...] - carried[0:elem_count, :]
    lane = iota((size, 128), 1)
    columns[...] = jnp.zeros(columns.shape, f32)

    def one_element(e, _):
        product = inverse[e] * carried_v[pl.ds(e, 1), :]
        total = jnp.sum(product, axis=1, keepdims=True)
        columns[0:size, :] = jnp.where(lane == e, total, columns[0:size, :])
        return 0

    lax.fori_loop(0, elem_count, one_element, 0)
    return columns[...].T[0:ROWS, 0:size]


def next_sweep(elem_count, rhs, faces_in, arr_0, arr_1, arr_2, arr_3, chooser, inverse, blocks,
               send_0, send_1, send_2, send_3, faces, carried_v, columns, adj_v):
    adj_v[...] = apply_inverse(
        elem_count, rhs, faces_in, (arr_0, arr_1, arr_2, arr_3), chooser, inverse, carried_v, columns
    )
    faces[...] = jnp.zeros(faces.shape, f32)
    face_products(elem_count, adj_v, blocks, faces)
    fill_sends(faces, (send_0, send_1, send_2, send_3))


def last_sweep(elem_count, n_sub, n_dev, node_count, rhs, faces_in, arr_0, arr_1, arr_2, arr_3,
               chooser, inverse, geometry, table, adjoint, out, carried_v, columns):
    rows = apply_inverse(
        elem_count, rhs, faces_in, (arr_0, arr_1, arr_2, arr_3), chooser, inverse, carried_v, columns
    )
    adjoint[...] = rows[0:elem_count, :]
    width = 3 * CORNERS * elem_count
    slots = node_count + 2
    every = dot_nt(rows.astype(bf16), geometry[...])
    offset = iota(every.shape, 1) - 3 * CORNERS * iota(every.shape, 0)
    own = (offset >= 0) & (offset < 3 * CORNERS)
    corner = jnp.sum(jnp.where(own, every, 0.0), axis=0, keepdims=True)
    parts = in_three(corner)
    owner = table[0:1, 0:width].astype(i32)
    slot = table[1:2, 0:width].astype(i32)
    lane = iota((1, width), 1)
    third = lane - 3 * jnp.floor((lane.astype(f32) + 0.5) / 3.0).astype(i32)
    is_first, is_last = slot == 0, slot == node_count - 1
    beside = jnp.where(is_first, owner - 1, jnp.where(is_last, owner + 1, -1))
    beside_slot = jnp.where(is_first, slots - 1, 0)
    total = jnp.zeros((n_dev, 128), f32)
    for target, place in ((owner, slot + 1), (beside, beside_slot)):
        goes = iota((n_dev, width), 0) == target
        left = jnp.concatenate(
            [jnp.where(goes, part.astype(f32), 0.0).astype(bf16) for part in parts], axis=0
        )
        right = jnp.where(iota((128, width), 0) == third * slots + place, 1.0, 0.0).astype(bf16)
        summed = dot_nt(left, right)
        total = total + summed[0:n_dev] + summed[n_dev : 2 * n_dev] + summed[2 * n_dev :]
    device = lax.axis_index("dom") * n_sub + lax.axis_index("sub")
    after = iota((n_dev, 128), 0) == device + 1
    out[...] = total + jnp.where(after, table[2:3, 0:128], 0.0)


def stencil(node_count, arrived, diag, upper, lower, out, shifted):
    slots = node_count + 2
    sums = jnp.broadcast_to(jnp.sum(arrived[...], axis=0, keepdims=True), (8, 128))
    lane, row = iota((8, 128), 1), iota((8, 128), 0)

    def at(a, step):
        first = a * slots + 1 + step
        return pltpu.roll(sums, (128 - first) % 128, axis=1)[0:3, 0:node_count]

    total = jnp.zeros((3, node_count), f32)
    moved = jnp.zeros((3, node_count), f32)
    edge = jnp.zeros((8, 1), f32)
    for a in range(3):
        here = at(a, 0)
        total = total + diag[a] * here + lower[a] * at(a, 1)
        moved = moved + upper[a] * here
        coupling = jnp.sum(jnp.where(lane == 3 * slots + 3 * a + row, sums, 0.0), 1, keepdims=True)
        before = jnp.sum(jnp.where(lane == a * slots, sums, 0.0), 1, keepdims=True)
        edge = edge + coupling * before
    shifted[...] = jnp.zeros(shifted.shape, f32)
    shifted[0:3, 0:node_count] = moved
    prev = jnp.where(lane == 0, edge, pltpu.roll(shifted[...], 1, axis=1))
    out[...] = total + prev[0:3, 0:node_count]


def solution(mesh):
    n_dom, n_sub = mesh.shape["dom"], mesh.shape["sub"]
    n_dev = n_dom * n_sub
    swaps = pair_swaps(n_dom, n_sub)

    def exchange(sends):
        return [lax.ppermute(send, AXES, pairs) for send, pairs in zip(sends, swaps)]

    def on_device(
        adjoint_rhs, adjoint_start, offdiag_blocks, diag_inverse, geometry_jac, neighbor,
        corner_node, deform_place, stiff_diag, stiff_upper, stiff_lower,
    ):
        elem_count, size = adjoint_rhs.shape
        node_count = stiff_diag.shape[2]
        assert elem_count <= ROWS and n_dev <= 256 and 1 < node_count <= 256
        assert 3 * (node_count + 2) + 9 <= 128
        width = 3 * CORNERS * elem_count
        slab = jax.ShapeDtypeStruct((ROWS, size), f32)
        faces_shape = jax.ShapeDtypeStruct((NF, ROWS, size), f32)
        limit = pltpu.CompilerParams(vmem_limit_bytes=16 << 20)
        column_scratch = [
            pltpu.VMEM((ROWS, size), f32),
            pltpu.VMEM((up_to(size, 128), 128), f32),
        ]

        def fixed(body, *numbers):
            def call(*refs):
                return body(*numbers, *refs)

            return call

        *sends, faces, blocks, chooser, table = pl.pallas_call(
            fixed(first_sweep, elem_count, n_sub, node_count),
            out_shape=(
                slab, slab, slab, slab, faces_shape,
                pltpu.VMEM(offdiag_blocks.shape, bf16),
                jax.ShapeDtypeStruct((ROWS, (NF + 4) * ROWS), f32),
                jax.ShapeDtypeStruct((8, up_to(width, 128)), f32),
            ),
            in_specs=[IN_HBM] * 6,
            out_specs=(IN_VMEM,) * 8,
            scratch_shapes=[
                pltpu.VMEM((elem_count, size), f32),
                pltpu.VMEM((NF, elem_count), i32),
                pltpu.VMEM((CORNERS, elem_count), i32),
                pltpu.VMEM((1, deform_place.shape[0]), i32),
                pltpu.VMEM(stiff_upper.shape, f32),
                pltpu.VMEM((128, 128), i32),
                pltpu.SemaphoreType.DMA((5,)),
                pltpu.SemaphoreType.DMA((elem_count,)),
            ],
            compiler_params=limit,
            name="first_sweep",
        )(adjoint_start, offdiag_blocks, neighbor.T, corner_node.T, deform_place[None, :],
          stiff_upper)
        diag_inverse, faces = lax.optimization_barrier((diag_inverse, faces))
        inverse = pltpu.with_memory_space_constraint(diag_inverse, pltpu.VMEM)
        arrived = exchange(sends)
        *sends, faces = pl.pallas_call(
            fixed(next_sweep, elem_count),
            out_shape=(slab, slab, slab, slab, faces_shape),
            in_specs=[IN_VMEM] * 9,
            out_specs=(IN_VMEM,) * 5,
            scratch_shapes=column_scratch + [pltpu.VMEM((ROWS, size), f32)],
            compiler_params=limit,
            name="next_sweep",
        )(adjoint_rhs, faces, *arrived, chooser, inverse, blocks)
        arrived = exchange(sends)
        adjoint, by_owner = pl.pallas_call(
            fixed(last_sweep, elem_count, n_sub, n_dev, node_count),
            out_shape=(
                jax.ShapeDtypeStruct((elem_count, size), f32),
                jax.ShapeDtypeStruct((n_dev, 128), f32),
            ),
            in_specs=[IN_VMEM] * 10,
            out_specs=(IN_VMEM,) * 2,
            scratch_shapes=column_scratch,
            compiler_params=limit,
            name="last_sweep",
        )(adjoint_rhs, faces, *arrived, chooser, inverse,
          geometry_jac.reshape(width, size), table)
        gathered = lax.all_to_all(by_owner, AXES, 0, 0, tiled=True)
        shape_grad = pl.pallas_call(
            fixed(stencil, node_count),
            out_shape=jax.ShapeDtypeStruct((3, node_count), f32),
            in_specs=[IN_VMEM] * 4,
            out_specs=IN_VMEM,
            scratch_shapes=[pltpu.VMEM((8, 128), f32)],
            compiler_params=limit,
            name="stencil",
        )(gathered, stiff_diag, stiff_upper, stiff_lower)
        return adjoint, shape_grad

    placed = (
        P(AXES, None),
        P(AXES, None),
        P(None, AXES, None, None),
        P(AXES, None, None),
        P(AXES, None, None),
        P(AXES, None),
        P(AXES, None),
        P(),
        P(None, None, AXES),
        P(None, None, AXES),
        P(None, None, AXES),
    )
    return jax.shard_map(
        on_device,
        mesh=mesh,
        in_specs=placed,
        out_specs=(P(AXES, None), P(None, AXES)),
        check_vma=False,
    )
```

time: 207 us -> 62.2 us (0.30); the launches traced: 203 us -> 61.8 us
  blocking collectives: 108 us -> 11.9 us
  matrix products: 34.2 us -> 0 us
  other arithmetic: 25.4 us -> 0.01 us
  local copies, waits for them, and re-layouts: 3.49 us -> 22 us
  starting transfers between devices: 23.6 us -> 7.86 us
  Pallas kernels: 0 us -> 14.4 us
  waiting for transfers between devices: 8.12 us -> 4.98 us
    all_gather x1 -> x0, blocking collectives: 65.2 us -> none  [on_device(): every_value = lax.all_gather(values, ('dom', 'sub'), axis=1, tiled=True)]
    unnamed x1 -> x0, blocking collectives: 42.5 us -> none
    dot_general x23 -> x0, matrix products: 34.2 us -> none  [the longest x2 17 us: on_device(): jnp.einsum('keij,ei->kej', offdiag_blocks, rounded, preferred_element_typ...]
    scatter-add x1 -> x0, other arithmetic: 21.1 us -> none  [on_device(): jax.ops.segment_sum(every_value.T, node_slot, node_count + 1)[:node_count]]
    unnamed x25 -> x28, local copies, waits for them, and re-layouts: 0.58 us -> 21.1 us
    ppermute x10 -> x8, starting transfers between devices: 23.6 us -> 7.86 us  [exchange(): lax.ppermute(send, AXES, pairs)]
    pallas_call x0 -> x4, Pallas kernels: none -> 14.4 us  [the longest x1 5.66 us: on_device(): pl.pallas_call(fixed(next_sweep, elem_count), out_shape=(slab, slab, slab...]
    all_to_all x0 -> x1, blocking collectives: none -> 11.9 us  [on_device(): gathered = lax.all_to_all(by_owner, AXES, 0, 0, tiled=True)]
  transfers between devices with their start and end apart: 10 -> 8, of which waited for: 2 -> 4; matrix products, arithmetic and copies ran while one was open for 3% -> 0% of each run, Pallas kernels for 0% -> 0%
where the time goes in v1:
time: 62.2 us; the launch traced here: 61.8 us
  local copies, waits for them, and re-layouts  22 us (35%)
  Pallas kernels  14.4 us (23%)
  blocking collectives  11.9 us (19%)
  starting transfers between devices  7.86 us (13%)
  waiting for transfers between devices  4.98 us (8%)
  between operations  0.72 us (1%)
    unnamed x28, local copies, waits for them, and re-layouts  21.1 us
    all_to_all x1, blocking collectives, on_device(): gathered = lax.all_to_all(by_owner, AXES, 0, 0, tiled=True)  11.9 us
    ppermute x8, starting transfers between devices, exchange(): lax.ppermute(send, AXES, pairs)  7.86 us
    pallas_call x1, Pallas kernels, on_device(): pl.pallas_call(fixed(next_sweep, elem_count), out_shape=(slab, slab, slab...  5.66 us
    pallas_call x1, Pallas kernels, on_device(): pl.pallas_call(fixed(first_sweep, elem_count, n_sub, node_count), out_sha...  5.65 us
    ppermute x8, waiting for transfers between devices, exchange(): lax.ppermute(send, AXES, pairs)  4.98 us
    pallas_call x1, Pallas kernels, on_device(): pl.pallas_call(fixed(last_sweep, elem_count, n_sub, n_dev, node_count), o...  2.37 us
  transfers between devices with their start and end apart: 8, of which 4 were waited for; matrix products, arithmetic and copies ran while one was open for 0% of the time, Pallas kernels for 0%

profile of v1, /device:TPU:0, one launch (start us, length us, event | category | flops | bytes accessed | tf_op | source)
XLA Modules:
  0.0 61.8 jit_solution(12476452127979734834)
XLA Ops:
  0.6 0.0 slice-start
  0.6 0.8 %broadcast_in_dim.3.refs_4_ = s32[1,567]{1,0:T(1,128)S(1)} reshape(s32[567]{0:T(1024)} %param.18) | data formatting | bytes 4536 | tf_op jit(solution)/shard_map/broadcast_in_dim | solution.py:321
  1.5 6.2 %copy-done = bf16[6,12,320,320]{3,2,1,0:T(8,128)(2,1)S(1)} copy-done((bf16[6,12,320,320]{3,2,1,0:T(8,128)(2,1)S(1)}, bf16[6,12,320,320]{3,2,1,0:T(8,128)(2,1)}, u32[]{:S(2)}) %copy-start) | copy-done | bytes 14745624
  7.7 0.7 %copy-done.5 = f32[3,3,18]{2,1,0:T(4,128)S(1)} copy-done((f32[3,3,18]{2,1,0:T(4,128)S(1)}, f32[3,3,18]{2,1,0:T(4,128)}, u32[]{:S(2)}) %copy-start.5) | copy-done | bytes 672
  8.4 0.7 %copy-done.7 = f32[12,320]{1,0:T(8,128)S(1)} copy-done((f32[12,320]{1,0:T(8,128)S(1)}, f32[12,320]{1,0:T(8,128)}, u32[]{:S(2)}) %copy-start.7) | copy-done | bytes 15384
  9.1 0.7 %copy-done.10 = s32[12,6]{0,1:T(8,128)S(1)} copy-done((s32[12,6]{0,1:T(8,128)S(1)}, s32[12,6]{0,1:T(8,128)}, u32[]{:S(2)}) %copy-start.10) | copy-done | bytes 312
  9.8 0.7 %copy-done.11 = s32[12,8]{0,1:T(8,128)S(1)} copy-done((s32[12,8]{0,1:T(8,128)S(1)}, s32[12,8]{0,1:T(8,128)}, u32[]{:S(2)}) %copy-start.11) | copy-done | bytes 408
  10.5 5.6 %first_sweep.1 = (f32[16,320]{1,0:T(8,128)S(1)}, f32[16,320]{1,0:T(8,128)S(1)}, f32[16,320]{1,0:T(8,128)S(1)}, f32[16,320]{1,0:T(8,128)S(1)}, f32[6,16,320]{2,1,...) custom-call(f32[12,320]{1,0:T(8,128)S(1)} %copy-done.7, ...), custom_call_target="tpu_custom_call" | custom-call | tf_op jit(solution)/shard_map/first_sweep/pallas_call | solution.py:299
  16.2 0.0 copy-start.1
  16.2 6.1 %copy-done.1 = bf16[6,12,320,320]{3,2,1,0:T(8,128)(2,1)} copy-done((bf16[6,12,320,320]{3,2,1,0:T(8,128)(2,1)}, bf16[6,12,320,320]{3,2,1,0:T(8,128)(2,1)S(1)}, u32[]{:S(2)}) %copy-start.1) | copy-done | bytes 14745624
  22.2 0.5 collective-permute-start
  22.7 2.6 %collective-permute-start.1 = (f32[16,320]{1,0:T(8,128)S(1)}, f32[16,320]{1,0:T(8,128)S(1)}, u32[]{:S(2)}, u32[]{:S(2)}) collective-permute-start(f32[16,320]{1,0:T(8,128)S(1)} %get-tuple-element.22), channel_id=1, source_target_pairs={{4,8},{8,4},{12,16},{16,12},{20,24},{24,20},{5,9},{9,5},{13,17},{1... | collective-permute-start | bytes 61448 | tf_op jit(solution)/shard_map/ppermute | solution.py:274
  25.3 0.1 collective-permute-start.2
  25.3 1.3 %collective-permute-start.3 = (f32[16,320]{1,0:T(8,128)S(1)}, f32[16,320]{1,0:T(8,128)S(1)}, u32[]{:S(2)}, u32[]{:S(2)}) collective-permute-start(f32[16,320]{1,0:T(8,128)S(1)} %get-tuple-element.24), channel_id=1, source_target_pairs={{1,2},{2,1},{5,6},{6,5},{9,10},{10,9},{13,14},{14,13},{17,18},{18,... | collective-permute-start | bytes 61448 | tf_op jit(solution)/shard_map/ppermute | solution.py:274
  26.6 0.0 collective-permute-done.refs_2_
  26.6 0.5 collective-permute-done.1.refs_3_
  27.1 2.0 %collective-permute-done.2.refs_4_ = f32[16,320]{1,0:T(8,128)S(1)} collective-permute-done((f32[16,320]{1,0:T(8,128)S(1)}, f32[16,320]{1,0:T(8,128)S(1)}, u32[]{:S(2)}, u32[]{:S(2)}) %collective-permute-start.2) | collective-permute-done | bytes 20512 | tf_op jit(solution)/shard_map/ppermute | solution.py:274
  29.1 0.0 collective-permute-done.3.refs_5_
  29.1 6.0 %copy-done.2 = bf16[6,12,320,320]{3,2,1,0:T(8,128)(2,1)S(1)} copy-done((bf16[6,12,320,320]{3,2,1,0:T(8,128)(2,1)S(1)}, bf16[6,12,320,320]{3,2,1,0:T(8,128)(2,1)}, u32[]{:S(2)}) %copy-start.2) | copy-done | bytes 14745624
  35.2 5.7 %next_sweep.1 = (f32[16,320]{1,0:T(8,128)S(1)}, f32[16,320]{1,0:T(8,128)S(1)}, f32[16,320]{1,0:T(8,128)S(1)}, f32[16,320]{1,0:T(8,128)S(1)}, f32[6,16,320]{2,1,0:T(8,128)S(1)}) custom-call(f32[12,320]{1,0:T(8,128)S(1)} %copy-done.4, f32[6,16,320]{2,1,0:T(8,128)S(1)} %get-tuple-element.20.refs_1_, f32[16,320]{1,0:T(8,128)S(1)} %collective-permute-done.refs_2_, ...), custom_call_target="tpu_custom_call" | custom-call | tf_op jit(solution)/shard_map/next_sweep/pallas_call | solution.py:326
  40.8 0.1 collective-permute-start.4
  40.9 2.1 %collective-permute-start.5 = (f32[16,320]{1,0:T(8,128)S(1)}, f32[16,320]{1,0:T(8,128)S(1)}, u32[]{:S(2)}, u32[]{:S(2)}) collective-permute-start(f32[16,320]{1,0:T(8,128)S(1)} %get-tuple-element.30), channel_id=1, source_target_pairs={{4,8},{8,4},{12,16},{16,12},{20,24},{24,20},{5,9},{9,5},{13,17},{1... | collective-permute-start | bytes 61448 | tf_op jit(solution)/shard_map/ppermute | solution.py:274
  43.0 0.1 collective-permute-start.6
  43.1 1.3 %collective-permute-start.7 = (f32[16,320]{1,0:T(8,128)S(1)}, f32[16,320]{1,0:T(8,128)S(1)}, u32[]{:S(2)}, u32[]{:S(2)}) collective-permute-start(f32[16,320]{1,0:T(8,128)S(1)} %get-tuple-element.32), channel_id=1, source_target_pairs={{1,2},{2,1},{5,6},{6,5},{9,10},{10,9},{13,14},{14,13},{17,18},{18,... | collective-permute-start | bytes 61448 | tf_op jit(solution)/shard_map/ppermute | solution.py:274
  44.3 0.0 collective-permute-done.4.refs_2_
  44.3 0.5 collective-permute-done.5.refs_3_
  44.8 2.0 %collective-permute-done.6.refs_4_ = f32[16,320]{1,0:T(8,128)S(1)} collective-permute-done((f32[16,320]{1,0:T(8,128)S(1)}, f32[16,320]{1,0:T(8,128)S(1)}, u32[]{:S(2)}, u32[]{:S(2)}) %collective-permute-start.6) | collective-permute-done | bytes 20512 | tf_op jit(solution)/shard_map/ppermute | solution.py:274
  46.8 0.0 collective-permute-done.7.refs_5_
  46.8 2.4 %last_sweep.1 = (f32[12,320]{1,0:T(8,128)}, f32[32,128]{1,0:T(8,128)S(1)}) custom-call(f32[12,320]{1,0:T(8,128)S(1)} %copy-done.4, f32[6,16,320]{2,1,0:T(8,128)S(1)} %get-tuple-element.28.refs_1_, f32[16,320]{1,0:T(8,128)S(1)} %collective-permute-done.4.refs_2_, f32[16,320]{1,0:T(8,128)S(1)} %collective-permute-done.5.refs_3_, ...), custom_call_target="tpu_custom_call" | custom-call | tf_op jit(solution)/shard_map/last_sweep/pallas_call | solution.py:336
  49.2 11.9 %all_to_all.11 = f32[32,1,128]{2,1,0:T(1,128)S(1)} all-to-all(f32[32,1,128]{2,1,0:T(1,128)S(1)} %bitcast.11), channel_id=1, replica_groups=mesh['dom'=8,'sub'=4] {'dom','sub'}, dimensions={0} | all-to-all | bytes 32768 | tf_op jit(solution)/shard_map/all_to_all | solution.py:349
  61.1 0.0 copy-done.6
  61.1 0.7 %stencil.1 = f32[3,18]{1,0:T(4,128)} custom-call(f32[32,128]{1,0:T(8,128)S(1)} %bitcast.10, f32[3,3,18]{2,1,0:T(4,128)S(1)} %copy-done.8, f32[3,3,18]{2,1,0:T(4,128)S(1)} %copy-done.6, f32[3,3,18]{2,1,0:T(4,128)S(1)} %copy-done.9), custom_call_target="tpu_custom_call" | custom-call | tf_op jit(solution)/shard_map/stencil/pallas_call | solution.py:350
  (19 shorter events, 0.0 us)
Async XLA Ops:
  0.6 28.5 %slice-start = ((s8[5898240]{0:T(1024)(128)(4,1)}), s8[4194304]{0:T(1024)(128)(4,1)S(1)}, s32[]{:S(2)}) async-start(s8[5898240]{0:T(1024)(128)(4,1)} %bitcast.7), calls=%async_computation.1 | async-start | bytes 8388608
  1.5 6.2 %copy-start = (bf16[6,12,320,320]{3,2,1,0:T(8,128)(2,1)S(1)}, bf16[6,12,320,320]{3,2,1,0:T(8,128)(2,1)}, u32[]{:S(2)}) copy-start(bf16[6,12,320,320]{3,2,1,0:T(8,128)(2,1)} %refs_1_.2) | copy-start | bytes 44236804
  7.7 0.7 %copy-start.5 = (f32[3,3,18]{2,1,0:T(4,128)S(1)}, f32[3,3,18]{2,1,0:T(4,128)}, u32[]{:S(2)}) copy-start(f32[3,3,18]{2,1,0:T(4,128)} %refs_2_.1) | copy-start | bytes 1948
  8.4 0.7 %copy-start.7 = (f32[12,320]{1,0:T(8,128)S(1)}, f32[12,320]{1,0:T(8,128)}, u32[]{:S(2)}) copy-start(f32[12,320]{1,0:T(8,128)} %refs_0_.3) | copy-start | bytes 46084
  9.1 0.7 %copy-start.10 = (s32[12,6]{0,1:T(8,128)S(1)}, s32[12,6]{0,1:T(8,128)}, u32[]{:S(2)}) copy-start(s32[12,6]{0,1:T(8,128)} %param.16) | copy-start | bytes 868
  9.8 0.7 %copy-start.11 = (s32[12,8]{0,1:T(8,128)S(1)}, s32[12,8]{0,1:T(8,128)}, u32[]{:S(2)}) copy-start(s32[12,8]{0,1:T(8,128)} %param.17) | copy-start | bytes 1156
  10.5 18.6 %slice-start.1 = ((s8[5898240]{0:T(1024)(128)(4,1)}), s8[1703936]{0:T(1024)(128)(4,1)S(1)}, s32[]{:S(2)}) async-start(s8[5898240]{0:T(1024)(128)(4,1)} %bitcast.7), calls=%async_computation.2 | async-start | bytes 3407872
  10.5 18.6 %copy-start.4 = (f32[12,320]{1,0:T(8,128)S(1)}, f32[12,320]{1,0:T(8,128)}, u32[]{:S(2)}) copy-start(f32[12,320]{1,0:T(8,128)} %refs_0_.5) | copy-start | bytes 46084
  10.5 36.3 %copy-start.3 = (bf16[12,24,320]{2,1,0:T(8,128)(2,1)S(1)}, bf16[12,24,320]{2,1,0:T(8,128)(2,1)}, u32[]{:S(2)}) copy-start(bf16[12,24,320]{2,1,0:T(8,128)(2,1)} %param.15) | copy-start | bytes 552964
  10.5 50.6 %copy-start.9 = (f32[3,3,18]{2,1,0:T(4,128)S(1)}, f32[3,3,18]{2,1,0:T(4,128)}, u32[]{:S(2)}) copy-start(f32[3,3,18]{2,1,0:T(4,128)} %refs_3_.1) | copy-start | bytes 1948
  16.2 6.1 %copy-start.1 = (bf16[6,12,320,320]{3,2,1,0:T(8,128)(2,1)}, bf16[6,12,320,320]{3,2,1,0:T(8,128)(2,1)S(1)}, u32[]{:S(2)}) copy-start(bf16[6,12,320,320]{3,2,1,0:T(8,128)(2,1)S(1)} %get-tuple-element.27.refs_8_) | copy-start | bytes 44236804
  22.2 38.9 %copy-start.6 = (f32[3,3,18]{2,1,0:T(4,128)S(1)}, f32[3,3,18]{2,1,0:T(4,128)}, u32[]{:S(2)}) copy-start(f32[3,3,18]{2,1,0:T(4,128)} %refs_2_.1) | copy-start | bytes 1948
  22.2 38.9 %copy-start.8 = (f32[3,3,18]{2,1,0:T(4,128)S(1)}, f32[3,3,18]{2,1,0:T(4,128)}, u32[]{:S(2)}) copy-start(f32[3,3,18]{2,1,0:T(4,128)} %refs_1_.3) | copy-start | bytes 1948
  22.2 4.4 %collective-permute-start = (f32[16,320]{1,0:T(8,128)S(1)}, f32[16,320]{1,0:T(8,128)S(1)}, u32[]{:S(2)}, u32[]{:S(2)}) collective-permute-start(f32[16,320]{1,0:T(8,128)S(1)} %get-tuple-element.21), channel_id=1, source_target_pairs={{0,4},{4,0},{8,12},{12,8},{16,20},{20,16},{24,28},{28,24},{1,5},{5... | collective-permute-start | bytes 61448 | tf_op jit(solution)/shard_map/ppermute | solution.py:274
  22.7 4.4 %collective-permute-start.1 = (f32[16,320]{1,0:T(8,128)S(1)}, f32[16,320]{1,0:T(8,128)S(1)}, u32[]{:S(2)}, u32[]{:S(2)}) collective-permute-start(f32[16,320]{1,0:T(8,128)S(1)} %get-tuple-element.22), channel_id=1, source_target_pairs={{4,8},{8,4},{12,16},{16,12},{20,24},{24,20},{5,9},{9,5},{13,17},{1... | collective-permute-start | bytes 61448 | tf_op jit(solution)/shard_map/ppermute | solution.py:274
  25.3 3.8 %collective-permute-start.2 = (f32[16,320]{1,0:T(8,128)S(1)}, f32[16,320]{1,0:T(8,128)S(1)}, u32[]{:S(2)}, u32[]{:S(2)}) collective-permute-start(f32[16,320]{1,0:T(8,128)S(1)} %get-tuple-element.23), channel_id=1, source_target_pairs={{0,1},{1,0},{2,3},{3,2},{4,5},{5,4},{6,7},{7,6},{8,9},{9,8},{10,11... | collective-permute-start | bytes 61448 | tf_op jit(solution)/shard_map/ppermute | solution.py:274
  25.3 3.8 %collective-permute-start.3 = (f32[16,320]{1,0:T(8,128)S(1)}, f32[16,320]{1,0:T(8,128)S(1)}, u32[]{:S(2)}, u32[]{:S(2)}) collective-permute-start(f32[16,320]{1,0:T(8,128)S(1)} %get-tuple-element.24), channel_id=1, source_target_pairs={{1,2},{2,1},{5,6},{6,5},{9,10},{10,9},{13,14},{14,13},{17,18},{18,... | collective-permute-start | bytes 61448 | tf_op jit(solution)/shard_map/ppermute | solution.py:274
  29.1 6.0 %copy-start.2 = (bf16[6,12,320,320]{3,2,1,0:T(8,128)(2,1)S(1)}, bf16[6,12,320,320]{3,2,1,0:T(8,128)(2,1)}, u32[]{:S(2)}) copy-start(bf16[6,12,320,320]{3,2,1,0:T(8,128)(2,1)} %copy-done.1) | copy-start | bytes 44236804
  40.8 3.5 %collective-permute-start.4 = (f32[16,320]{1,0:T(8,128)S(1)}, f32[16,320]{1,0:T(8,128)S(1)}, u32[]{:S(2)}, u32[]{:S(2)}) collective-permute-start(f32[16,320]{1,0:T(8,128)S(1)} %get-tuple-element.29), channel_id=1, source_target_pairs={{0,4},{4,0},{8,12},{12,8},{16,20},{20,16},{24,28},{28,24},{1,5},{5... | collective-permute-start | bytes 61448 | tf_op jit(solution)/shard_map/ppermute | solution.py:274
  40.9 3.9 %collective-permute-start.5 = (f32[16,320]{1,0:T(8,128)S(1)}, f32[16,320]{1,0:T(8,128)S(1)}, u32[]{:S(2)}, u32[]{:S(2)}) collective-permute-start(f32[16,320]{1,0:T(8,128)S(1)} %get-tuple-element.30), channel_id=1, source_target_pairs={{4,8},{8,4},{12,16},{16,12},{20,24},{24,20},{5,9},{9,5},{13,17},{1... | collective-permute-start | bytes 61448 | tf_op jit(solution)/shard_map/ppermute | solution.py:274
  43.0 3.8 %collective-permute-start.6 = (f32[16,320]{1,0:T(8,128)S(1)}, f32[16,320]{1,0:T(8,128)S(1)}, u32[]{:S(2)}, u32[]{:S(2)}) collective-permute-start(f32[16,320]{1,0:T(8,128)S(1)} %get-tuple-element.31), channel_id=1, source_target_pairs={{0,1},{1,0},{2,3},{3,2},{4,5},{5,4},{6,7},{7,6},{8,9},{9,8},{10,11... | collective-permute-start | bytes 61448 | tf_op jit(solution)/shard_map/ppermute | solution.py:274
  43.1 3.8 %collective-permute-start.7 = (f32[16,320]{1,0:T(8,128)S(1)}, f32[16,320]{1,0:T(8,128)S(1)}, u32[]{:S(2)}, u32[]{:S(2)}) collective-permute-start(f32[16,320]{1,0:T(8,128)S(1)} %get-tuple-element.32), channel_id=1, source_target_pairs={{1,2},{2,1},{5,6},{6,5},{9,10},{10,9},{13,14},{14,13},{17,18},{18,... | collective-permute-start | bytes 61448 | tf_op jit(solution)/shard_map/ppermute | solution.py:274

commit v2 on v1

--- a/solution.py
+++ b/solution.py
@@ -164,7 +164,7 @@
     chooser[...] = sum_chooser(elem_count, n_sub, neighbor_v[...], square)
     table[...] = jnp.zeros(table.shape, f32)
     width = 3 * CORNERS * elem_count
-    table[0:8, 0:width] = corner_lanes(elem_count, node_count, corner_v[...], place_v[...])
+    table[0:8, 0:width] = corner_lanes(elem_count, node_count, corner_v[...], place_v[...][None, :])
     base = 3 * (node_count + 2)
     lane, row = iota((3, 128), 1), iota((3, 128), 0)
     last = jnp.zeros((3, 128), f32)
@@ -284,7 +284,7 @@
         width = 3 * CORNERS * elem_count
         slab = jax.ShapeDtypeStruct((ROWS, size), f32)
         faces_shape = jax.ShapeDtypeStruct((NF, ROWS, size), f32)
-        limit = pltpu.CompilerParams(vmem_limit_bytes=16 << 20)
+        limit = pltpu.CompilerParams(vmem_limit_bytes=8 << 20)
         column_scratch = [
             pltpu.VMEM((ROWS, size), f32),
             pltpu.VMEM((up_to(size, 128), 128), f32),
@@ -310,7 +310,7 @@
                 pltpu.VMEM((elem_count, size), f32),
                 pltpu.VMEM((NF, elem_count), i32),
                 pltpu.VMEM((CORNERS, elem_count), i32),
-                pltpu.VMEM((1, deform_place.shape[0]), i32),
+                pltpu.VMEM(deform_place.shape, i32),
                 pltpu.VMEM(stiff_upper.shape, f32),
                 pltpu.VMEM((128, 128), i32),
                 pltpu.SemaphoreType.DMA((5,)),
@@ -318,8 +318,8 @@
             ],
             compiler_params=limit,
             name="first_sweep",
-        )(adjoint_start, offdiag_blocks, neighbor.T, corner_node.T, deform_place[None, :],
-          stiff_upper)
+        )(*(pltpu.with_memory_space_constraint(a, pltpu.HBM) for a in (
+            adjoint_start, offdiag_blocks, neighbor.T, corner_node.T, deform_place, stiff_upper)))
         diag_inverse, faces = lax.optimization_barrier((diag_inverse, faces))
         inverse = pltpu.with_memory_space_constraint(diag_inverse, pltpu.VMEM)
         arrived = exchange(sends)

time: 62.2 us -> 44.5 us (0.72)
  local copies, waits for them, and re-layouts: 22 us -> 0.04 us
  Pallas kernels: 14.4 us -> 18.7 us
    unnamed x28 -> x14, local copies, waits for them, and re-layouts: 21.1 us -> 0.04 us
    pallas_call x1, Pallas kernels: 5.65 us -> 9.98 us  [on_device(): pl.pallas_call(fixed(first_sweep, elem_count, n_sub, node_count), out_sha...]
    broadcast_in_dim x1 -> x0, local copies, waits for them, and re-layouts: 0.84 us -> none  [on_device(): deform_place[None, :]]
where the time goes in v2:
time: 44.5 us; the launch traced here: 44.3 us
  Pallas kernels  18.7 us (42%)
  blocking collectives  11.8 us (27%)
  starting transfers between devices  7.88 us (18%)
  waiting for transfers between devices  5.1 us (11%)
  between operations  0.74 us (2%)
    all_to_all x1, blocking collectives, on_device(): gathered = lax.all_to_all(by_owner, AXES, 0, 0, tiled=True)  11.8 us
    pallas_call x1, Pallas kernels, on_device(): pl.pallas_call(fixed(first_sweep, elem_count, n_sub, node_count), out_sha...  9.98 us
    ppermute x8, starting transfers between devices, exchange(): lax.ppermute(send, AXES, pairs)  7.88 us
    pallas_call x1, Pallas kernels, on_device(): pl.pallas_call(fixed(next_sweep, elem_count), out_shape=(slab, slab, slab...  5.66 us
    ppermute x8, waiting for transfers between devices, exchange(): lax.ppermute(send, AXES, pairs)  5.1 us
    pallas_call x1, Pallas kernels, on_device(): pl.pallas_call(fixed(last_sweep, elem_count, n_sub, n_dev, node_count), o...  2.37 us
  transfers between devices with their start and end apart: 8, of which 4 were waited for; matrix products, arithmetic and copies ran while one was open for 0% of the time, Pallas kernels for 0%

profile of v2, /device:TPU:0, one launch (start us, length us, event | category | flops | bytes accessed | tf_op | source)
XLA Modules:
  0.0 44.3 jit_solution(11314242625301056336)
XLA Ops:
  0.6 0.0 slice-start
  0.6 0.0 copy-start.1
  0.7 0.0 slice-start.1
  0.7 0.0 copy-start
  0.7 10.0 %first_sweep.1 = (f32[16,320]{1,0:T(8,128)S(1)}, f32[16,320]{1,0:T(8,128)S(1)}, f32[16,320]{1,0:T(8,128)S(1)}, f32[16,320]{1,0:T(8,128)S(1)}, f32[6,16,320]{2,1,...) custom-call(f32[12,320]{1,0:T(8,128)} %refs_0_.3, ...), custom_call_target="tpu_custom_call" | custom-call | tf_op jit(solution)/shard_map/first_sweep/pallas_call | solution.py:299
  10.7 0.0 copy-start.2
  10.7 0.0 copy-start.3
  10.7 0.0 copy-start.4
  10.7 0.5 %collective-permute-start = (f32[16,320]{1,0:T(8,128)S(1)}, f32[16,320]{1,0:T(8,128)S(1)}, u32[]{:S(2)}, u32[]{:S(2)}) collective-permute-start(f32[16,320]{1,0:T(8,128)S(1)} %get-tuple-element.21), channel_id=1, source_target_pairs={{0,4},{4,0},{8,12},{12,8},{16,20},{20,16},{24,28},{28,24},{1,5},{5... | collective-permute-start | bytes 61448 | tf_op jit(solution)/shard_map/ppermute | solution.py:274
  11.2 2.6 %collective-permute-start.1 = (f32[16,320]{1,0:T(8,128)S(1)}, f32[16,320]{1,0:T(8,128)S(1)}, u32[]{:S(2)}, u32[]{:S(2)}) collective-permute-start(f32[16,320]{1,0:T(8,128)S(1)} %get-tuple-element.22), channel_id=1, source_target_pairs={{4,8},{8,4},{12,16},{16,12},{20,24},{24,20},{5,9},{9,5},{13,17},{1... | collective-permute-start | bytes 61448 | tf_op jit(solution)/shard_map/ppermute | solution.py:274
  13.9 0.1 collective-permute-start.2
  13.9 1.2 %collective-permute-start.3 = (f32[16,320]{1,0:T(8,128)S(1)}, f32[16,320]{1,0:T(8,128)S(1)}, u32[]{:S(2)}, u32[]{:S(2)}) collective-permute-start(f32[16,320]{1,0:T(8,128)S(1)} %get-tuple-element.24), channel_id=1, source_target_pairs={{1,2},{2,1},{5,6},{6,5},{9,10},{10,9},{13,14},{14,13},{17,18},{18,... | collective-permute-start | bytes 61448 | tf_op jit(solution)/shard_map/ppermute | solution.py:274
  15.2 0.0 collective-permute-done.refs_2_
  15.2 0.5 %collective-permute-done.1.refs_3_ = f32[16,320]{1,0:T(8,128)S(1)} collective-permute-done((f32[16,320]{1,0:T(8,128)S(1)}, f32[16,320]{1,0:T(8,128)S(1)}, u32[]{:S(2)}, u32[]{:S(2)}) %collective-permute-start.1) | collective-permute-done | bytes 20512 | tf_op jit(solution)/shard_map/ppermute | solution.py:274
  15.7 2.0 %collective-permute-done.2.refs_4_ = f32[16,320]{1,0:T(8,128)S(1)} collective-permute-done((f32[16,320]{1,0:T(8,128)S(1)}, f32[16,320]{1,0:T(8,128)S(1)}, u32[]{:S(2)}, u32[]{:S(2)}) %collective-permute-start.2) | collective-permute-done | bytes 20512 | tf_op jit(solution)/shard_map/ppermute | solution.py:274
  17.7 0.0 collective-permute-done.3.refs_5_
  17.7 0.0 copy-done.1
  17.7 0.0 slice-done.1
  17.7 5.7 %next_sweep.1 = (f32[16,320]{1,0:T(8,128)S(1)}, f32[16,320]{1,0:T(8,128)S(1)}, f32[16,320]{1,0:T(8,128)S(1)}, f32[16,320]{1,0:T(8,128)S(1)}, f32[6,16,320]{2,1,0:T(8,128)S(1)}) custom-call(f32[12,320]{1,0:T(8,128)S(1)} %copy-done.1, f32[6,16,320]{2,1,0:T(8,128)S(1)} %get-tuple-element.20.refs_1_, f32[16,320]{1,0:T(8,128)S(1)} %collective-permute-done.refs_2_, ...), custom_call_target="tpu_custom_call" | custom-call | tf_op jit(solution)/shard_map/next_sweep/pallas_call | solution.py:326
  23.4 0.1 collective-permute-start.4
  23.5 2.1 %collective-permute-start.5 = (f32[16,320]{1,0:T(8,128)S(1)}, f32[16,320]{1,0:T(8,128)S(1)}, u32[]{:S(2)}, u32[]{:S(2)}) collective-permute-start(f32[16,320]{1,0:T(8,128)S(1)} %get-tuple-element.30), channel_id=1, source_target_pairs={{4,8},{8,4},{12,16},{16,12},{20,24},{24,20},{5,9},{9,5},{13,17},{1... | collective-permute-start | bytes 61448 | tf_op jit(solution)/shard_map/ppermute | solution.py:274
  25.6 0.1 collective-permute-start.6
  25.6 1.2 %collective-permute-start.7 = (f32[16,320]{1,0:T(8,128)S(1)}, f32[16,320]{1,0:T(8,128)S(1)}, u32[]{:S(2)}, u32[]{:S(2)}) collective-permute-start(f32[16,320]{1,0:T(8,128)S(1)} %get-tuple-element.32), channel_id=1, source_target_pairs={{1,2},{2,1},{5,6},{6,5},{9,10},{10,9},{13,14},{14,13},{17,18},{18,... | collective-permute-start | bytes 61448 | tf_op jit(solution)/shard_map/ppermute | solution.py:274
  26.8 0.0 collective-permute-done.4.refs_2_
  26.8 0.6 %collective-permute-done.5.refs_3_ = f32[16,320]{1,0:T(8,128)S(1)} collective-permute-done((f32[16,320]{1,0:T(8,128)S(1)}, f32[16,320]{1,0:T(8,128)S(1)}, u32[]{:S(2)}, u32[]{:S(2)}) %collective-permute-start.5) | collective-permute-done | bytes 20512 | tf_op jit(solution)/shard_map/ppermute | solution.py:274
  27.4 2.0 %collective-permute-done.6.refs_4_ = f32[16,320]{1,0:T(8,128)S(1)} collective-permute-done((f32[16,320]{1,0:T(8,128)S(1)}, f32[16,320]{1,0:T(8,128)S(1)}, u32[]{:S(2)}, u32[]{:S(2)}) %collective-permute-start.6) | collective-permute-done | bytes 20512 | tf_op jit(solution)/shard_map/ppermute | solution.py:274
  29.4 0.0 collective-permute-done.7.refs_5_
  29.4 2.4 %last_sweep.1 = (f32[12,320]{1,0:T(8,128)}, f32[32,128]{1,0:T(8,128)S(1)}) custom-call(f32[12,320]{1,0:T(8,128)S(1)} %copy-done.1, f32[6,16,320]{2,1,0:T(8,128)S(1)} %get-tuple-element.28.refs_1_, f32[16,320]{1,0:T(8,128)S(1)} %collective-permute-done.4.refs_2_, f32[16,320]{1,0:T(8,128)S(1)} %collective-permute-done.5.refs_3_, ...), custom_call_target="tpu_custom_call" | custom-call | tf_op jit(solution)/shard_map/last_sweep/pallas_call | solution.py:336
  31.8 11.8 %all_to_all.11 = f32[32,1,128]{2,1,0:T(1,128)S(1)} all-to-all(f32[32,1,128]{2,1,0:T(1,128)S(1)} %bitcast.11), channel_id=1, replica_groups=mesh['dom'=8,'sub'=4] {'dom','sub'}, dimensions={0} | all-to-all | bytes 32768 | tf_op jit(solution)/shard_map/all_to_all | solution.py:349
  43.6 0.0 copy-done.2
  43.6 0.0 copy-done.4
  43.6 0.7 %stencil.1 = f32[3,18]{1,0:T(4,128)} custom-call(f32[32,128]{1,0:T(8,128)S(1)} %bitcast.10, f32[3,3,18]{2,1,0:T(4,128)S(1)} %copy-done.3, f32[3,3,18]{2,1,0:T(4,128)S(1)} %copy-done.2, f32[3,3,18]{2,1,0:T(4,128)S(1)} %copy-done.4), custom_call_target="tpu_custom_call" | custom-call | tf_op jit(solution)/shard_map/stencil/pallas_call | solution.py:350
  (4 shorter events, 0.0 us)
Async XLA Ops:
  0.6 17.1 %slice-start = ((s8[5898240]{0:T(1024)(128)(4,1)}), s8[4194304]{0:T(1024)(128)(4,1)S(1)}, s32[]{:S(2)}) async-start(s8[5898240]{0:T(1024)(128)(4,1)} %bitcast.7), calls=%async_computation.1 | async-start | bytes 8388608
  0.6 17.1 %copy-start.1 = (f32[12,320]{1,0:T(8,128)S(1)}, f32[12,320]{1,0:T(8,128)}, u32[]{:S(2)}) copy-start(f32[12,320]{1,0:T(8,128)} %refs_0_.5) | copy-start | bytes 46084
  0.7 17.1 %slice-start.1 = ((s8[5898240]{0:T(1024)(128)(4,1)}), s8[1703936]{0:T(1024)(128)(4,1)S(1)}, s32[]{:S(2)}) async-start(s8[5898240]{0:T(1024)(128)(4,1)} %bitcast.7), calls=%async_computation.2 | async-start | bytes 3407872
  0.7 28.7 %copy-start = (bf16[12,24,320]{2,1,0:T(8,128)(2,1)S(1)}, bf16[12,24,320]{2,1,0:T(8,128)(2,1)}, u32[]{:S(2)}) copy-start(bf16[12,24,320]{2,1,0:T(8,128)(2,1)} %param.15) | copy-start | bytes 552964
  10.7 32.9 %copy-start.2 = (f32[3,3,18]{2,1,0:T(4,128)S(1)}, f32[3,3,18]{2,1,0:T(4,128)}, u32[]{:S(2)}) copy-start(f32[3,3,18]{2,1,0:T(4,128)} %refs_2_.1) | copy-start | bytes 1948
  10.7 32.9 %copy-start.3 = (f32[3,3,18]{2,1,0:T(4,128)S(1)}, f32[3,3,18]{2,1,0:T(4,128)}, u32[]{:S(2)}) copy-start(f32[3,3,18]{2,1,0:T(4,128)} %refs_1_.3) | copy-start | bytes 1948
  10.7 32.9 %copy-start.4 = (f32[3,3,18]{2,1,0:T(4,128)S(1)}, f32[3,3,18]{2,1,0:T(4,128)}, u32[]{:S(2)}) copy-start(f32[3,3,18]{2,1,0:T(4,128)} %refs_3_.1) | copy-start | bytes 1948
  10.7 4.5 %collective-permute-start = (f32[16,320]{1,0:T(8,128)S(1)}, f32[16,320]{1,0:T(8,128)S(1)}, u32[]{:S(2)}, u32[]{:S(2)}) collective-permute-start(f32[16,320]{1,0:T(8,128)S(1)} %get-tuple-element.21), channel_id=1, source_target_pairs={{0,4},{4,0},{8,12},{12,8},{16,20},{20,16},{24,28},{28,24},{1,5},{5... | collective-permute-start | bytes 61448 | tf_op jit(solution)/shard_map/ppermute | solution.py:274
  11.2 4.5 %collective-permute-start.1 = (f32[16,320]{1,0:T(8,128)S(1)}, f32[16,320]{1,0:T(8,128)S(1)}, u32[]{:S(2)}, u32[]{:S(2)}) collective-permute-start(f32[16,320]{1,0:T(8,128)S(1)} %get-tuple-element.22), channel_id=1, source_target_pairs={{4,8},{8,4},{12,16},{16,12},{20,24},{24,20},{5,9},{9,5},{13,17},{1... | collective-permute-start | bytes 61448 | tf_op jit(solution)/shard_map/ppermute | solution.py:274
  13.9 3.8 %collective-permute-start.2 = (f32[16,320]{1,0:T(8,128)S(1)}, f32[16,320]{1,0:T(8,128)S(1)}, u32[]{:S(2)}, u32[]{:S(2)}) collective-permute-start(f32[16,320]{1,0:T(8,128)S(1)} %get-tuple-element.23), channel_id=1, source_target_pairs={{0,1},{1,0},{2,3},{3,2},{4,5},{5,4},{6,7},{7,6},{8,9},{9,8},{10,11... | collective-permute-start | bytes 61448 | tf_op jit(solution)/shard_map/ppermute | solution.py:274
  13.9 3.8 %collective-permute-start.3 = (f32[16,320]{1,0:T(8,128)S(1)}, f32[16,320]{1,0:T(8,128)S(1)}, u32[]{:S(2)}, u32[]{:S(2)}) collective-permute-start(f32[16,320]{1,0:T(8,128)S(1)} %get-tuple-element.24), channel_id=1, source_target_pairs={{1,2},{2,1},{5,6},{6,5},{9,10},{10,9},{13,14},{14,13},{17,18},{18,... | collective-permute-start | bytes 61448 | tf_op jit(solution)/shard_map/ppermute | solution.py:274
  23.4 3.4 %collective-permute-start.4 = (f32[16,320]{1,0:T(8,128)S(1)}, f32[16,320]{1,0:T(8,128)S(1)}, u32[]{:S(2)}, u32[]{:S(2)}) collective-permute-start(f32[16,320]{1,0:T(8,128)S(1)} %get-tuple-element.29), channel_id=1, source_target_pairs={{0,4},{4,0},{8,12},{12,8},{16,20},{20,16},{24,28},{28,24},{1,5},{5... | collective-permute-start | bytes 61448 | tf_op jit(solution)/shard_map/ppermute | solution.py:274
  23.5 3.9 %collective-permute-start.5 = (f32[16,320]{1,0:T(8,128)S(1)}, f32[16,320]{1,0:T(8,128)S(1)}, u32[]{:S(2)}, u32[]{:S(2)}) collective-permute-start(f32[16,320]{1,0:T(8,128)S(1)} %get-tuple-element.30), channel_id=1, source_target_pairs={{4,8},{8,4},{12,16},{16,12},{20,24},{24,20},{5,9},{9,5},{13,17},{1... | collective-permute-start | bytes 61448 | tf_op jit(solution)/shard_map/ppermute | solution.py:274
  25.6 3.8 %collective-permute-start.6 = (f32[16,320]{1,0:T(8,128)S(1)}, f32[16,320]{1,0:T(8,128)S(1)}, u32[]{:S(2)}, u32[]{:S(2)}) collective-permute-start(f32[16,320]{1,0:T(8,128)S(1)} %get-tuple-element.31), channel_id=1, source_target_pairs={{0,1},{1,0},{2,3},{3,2},{4,5},{5,4},{6,7},{7,6},{8,9},{9,8},{10,11... | collective-permute-start | bytes 61448 | tf_op jit(solution)/shard_map/ppermute | solution.py:274
  25.6 3.8 %collective-permute-start.7 = (f32[16,320]{1,0:T(8,128)S(1)}, f32[16,320]{1,0:T(8,128)S(1)}, u32[]{:S(2)}, u32[]{:S(2)}) collective-permute-start(f32[16,320]{1,0:T(8,128)S(1)} %get-tuple-element.32), channel_id=1, source_target_pairs={{1,2},{2,1},{5,6},{6,5},{9,10},{10,9},{13,14},{14,13},{17,18},{18,... | collective-permute-start | bytes 61448 | tf_op jit(solution)/shard_map/ppermute | solution.py:274

commit v3 on v2

--- a/solution.py
+++ b/solution.py
@@ -8,6 +8,7 @@
 NF = 6
 CORNERS = 8
 AXES = ("dom", "sub")
+PAIR = 2
 ROWS = 16
 
 f32 = jnp.float32
@@ -20,6 +21,10 @@
 
 def iota(shape, dim):
     return lax.broadcasted_iota(i32, shape, dim)
+
+
+def in_hbm(array):
+    return pltpu.with_memory_space_constraint(array, pltpu.HBM)
 
 
 def up_to(count, multiple):
@@ -39,6 +44,17 @@
 
 def dot_nt(a, b):
     return lax.dot_general(a, b, (((1,), (1,)), ((), ())), preferred_element_type=f32)
+
+
+def grouped(count, group, one):
+    def step(index, _):
+        for offset in range(group):
+            one(index * group + offset)
+        return 0
+
+    lax.fori_loop(0, count // group, step, 0)
+    for e in range(count // group * group, count):
+        one(e)
 
 
 def pair_swaps(n_dom, n_sub):
@@ -70,16 +86,10 @@
     return swaps
 
 
-def face_products(elem_count, adj_rows, blocks, faces, before=None):
-    def one_element(e, _):
-        if before is not None:
-            before(e)
-        row = adj_rows[pl.ds(e, 1), :].astype(bf16)
-        for k in range(NF):
-            faces[k, pl.ds(e, 1), :] = jnp.dot(row, blocks[k, e], preferred_element_type=f32)
-        return 0
-
-    lax.fori_loop(0, elem_count, one_element, 0)
+def element_faces(e, adj_rows, blocks, faces):
+    row = adj_rows[pl.ds(e, 1), :].astype(bf16)
+    for k in range(NF):
+        faces[k, pl.ds(e, 1), :] = jnp.dot(row, blocks[k, e], preferred_element_type=f32)
 
 
 def fill_sends(faces, sends):
@@ -139,41 +149,47 @@
     return jnp.dot(pair, found, preferred_element_type=f32)
 
 
-def first_sweep(elem_count, n_sub, node_count, start, offdiag, neighbor, corner, place, upper,
-                send_0, send_1, send_2, send_3, faces, blocks, chooser, table,
-                start_v, neighbor_v, corner_v, place_v, upper_v, square, small_sem, block_sem):
-    sends = (send_0, send_1, send_2, send_3)
-    small = [
-        pltpu.make_async_copy(source, target, small_sem.at[n])
-        for n, (source, target) in enumerate(
-            ((start, start_v), (neighbor, neighbor_v), (corner, corner_v), (place, place_v),
-             (upper, upper_v))
+def first_sweep(elem_count, start, offdiag, send_0, send_1, send_2, send_3, faces, blocks,
+                start_v, start_sem, block_sem):
+    def block_copy(index):
+        held = pl.ds(index * PAIR, PAIR)
+        return pltpu.make_async_copy(
+            offdiag.at[:, held], blocks.at[:, held], block_sem.at[index]
         )
-    ]
-
-    def block_copy(e):
-        return pltpu.make_async_copy(offdiag.at[:, e], blocks.at[:, e], block_sem.at[e])
-
-    for copy in small:
-        copy.start()
-    for e in range(elem_count):
-        block_copy(e).start()
+
+    start_copy = pltpu.make_async_copy(start, start_v, start_sem)
+    start_copy.start()
+    for index in range(elem_count // PAIR):
+        block_copy(index).start()
     faces[...] = jnp.zeros(faces.shape, f32)
-    for copy in small:
-        copy.wait()
-    chooser[...] = sum_chooser(elem_count, n_sub, neighbor_v[...], square)
+    start_copy.wait()
+
+    def step(index, _):
+        block_copy(index).wait()
+        for offset in range(PAIR):
+            element_faces(index * PAIR + offset, start_v, blocks, faces)
+        return 0
+
+    lax.fori_loop(0, elem_count // PAIR, step, 0)
+    fill_sends(faces, (send_0, send_1, send_2, send_3))
+
+
+def fetch_and_plan(elem_count, n_sub, node_count, inverse_hbm, neighbor, corner, place, upper,
+                   after, inverse, chooser, table, square, sem):
+    copy = pltpu.make_async_copy(inverse_hbm, inverse, sem)
+    copy.start()
+    chooser[...] = sum_chooser(elem_count, n_sub, neighbor[...], square)
     table[...] = jnp.zeros(table.shape, f32)
     width = 3 * CORNERS * elem_count
-    table[0:8, 0:width] = corner_lanes(elem_count, node_count, corner_v[...], place_v[...][None, :])
+    table[0:8, 0:width] = corner_lanes(elem_count, node_count, corner[...], place[...][None, :])
     base = 3 * (node_count + 2)
     lane, row = iota((3, 128), 1), iota((3, 128), 0)
     last = jnp.zeros((3, 128), f32)
     for a in range(3):
-        column = upper_v[a][:, node_count - 1 : node_count]
+        column = upper[a][:, node_count - 1 : node_count]
         last = last + jnp.where(lane == base + 3 * a + row, column, 0.0)
     table[2:3, 0:128] = jnp.sum(last, axis=0, keepdims=True)
-    face_products(elem_count, start_v, blocks, faces, before=lambda e: block_copy(e).wait())
-    fill_sends(faces, sends)
+    copy.wait()
 
 
 def apply_inverse(elem_count, rhs, faces, arrived, chooser, inverse, carried_v, columns):
@@ -202,7 +218,7 @@
         elem_count, rhs, faces_in, (arr_0, arr_1, arr_2, arr_3), chooser, inverse, carried_v, columns
     )
     faces[...] = jnp.zeros(faces.shape, f32)
-    face_products(elem_count, adj_v, blocks, faces)
+    grouped(elem_count, 4, lambda e: element_faces(e, adj_v, blocks, faces))
     fill_sends(faces, (send_0, send_1, send_2, send_3))
 
 
@@ -279,7 +295,8 @@
     ):
         elem_count, size = adjoint_rhs.shape
         node_count = stiff_diag.shape[2]
-        assert elem_count <= ROWS and n_dev <= 256 and 1 < node_count <= 256
+        assert elem_count <= ROWS and elem_count % PAIR == 0
+        assert n_dev <= 256 and 1 < node_count <= 256
         assert 3 * (node_count + 2) + 9 <= 128
         width = 3 * CORNERS * elem_count
         slab = jax.ShapeDtypeStruct((ROWS, size), f32)
@@ -296,33 +313,38 @@
 
             return call
 
-        *sends, faces, blocks, chooser, table = pl.pallas_call(
-            fixed(first_sweep, elem_count, n_sub, node_count),
+        *sends, faces, blocks = pl.pallas_call(
+            fixed(first_sweep, elem_count),
             out_shape=(
-                slab, slab, slab, slab, faces_shape,
-                pltpu.VMEM(offdiag_blocks.shape, bf16),
+                slab, slab, slab, slab, faces_shape, pltpu.VMEM(offdiag_blocks.shape, bf16),
+            ),
+            in_specs=[IN_HBM] * 2,
+            out_specs=(IN_VMEM,) * 6,
+            scratch_shapes=[
+                pltpu.VMEM((elem_count, size), f32),
+                pltpu.SemaphoreType.DMA,
+                pltpu.SemaphoreType.DMA((elem_count // PAIR,)),
+            ],
+            compiler_params=limit,
+            name="first_sweep",
+        )(in_hbm(adjoint_start), in_hbm(offdiag_blocks))
+        arrived = exchange(sends)
+        inverse, chooser, table = pl.pallas_call(
+            fixed(fetch_and_plan, elem_count, n_sub, node_count),
+            out_shape=(
+                pltpu.VMEM(diag_inverse.shape, f32),
                 jax.ShapeDtypeStruct((ROWS, (NF + 4) * ROWS), f32),
                 jax.ShapeDtypeStruct((8, up_to(width, 128)), f32),
             ),
-            in_specs=[IN_HBM] * 6,
-            out_specs=(IN_VMEM,) * 8,
-            scratch_shapes=[
-                pltpu.VMEM((elem_count, size), f32),
-                pltpu.VMEM((NF, elem_count), i32),
-                pltpu.VMEM((CORNERS, elem_count), i32),
-                pltpu.VMEM(deform_place.shape, i32),
-                pltpu.VMEM(stiff_upper.shape, f32),
-                pltpu.VMEM((128, 128), i32),
-                pltpu.SemaphoreType.DMA((5,)),
-                pltpu.SemaphoreType.DMA((elem_count,)),
-            ],
+            in_specs=[IN_HBM] + [IN_VMEM] * 5,
+            out_specs=(IN_VMEM,) * 3,
+            scratch_shapes=[pltpu.VMEM((128, 128), i32), pltpu.SemaphoreType.DMA],
             compiler_params=limit,
-            name="first_sweep",
-        )(*(pltpu.with_memory_space_constraint(a, pltpu.HBM) for a in (
-            adjoint_start, offdiag_blocks, neighbor.T, corner_node.T, deform_place, stiff_upper)))
-        diag_inverse, faces = lax.optimization_barrier((diag_inverse, faces))
-        inverse = pltpu.with_memory_space_constraint(diag_inverse, pltpu.VMEM)
-        arrived = exchange(sends)
+            cost_estimate=pl.CostEstimate(
+                flops=0, bytes_accessed=4 * diag_inverse.size, transcendentals=0
+            ),
+            name="fetch_and_plan",
+        )(in_hbm(diag_inverse), neighbor.T, corner_node.T, deform_place, stiff_upper, faces)
         *sends, faces = pl.pallas_call(
             fixed(next_sweep, elem_count),
             out_shape=(slab, slab, slab, slab, faces_shape),

time: 44.5 us -> 40.1 us (0.901)
  waiting for transfers between devices: 5.1 us -> 2.51 us
  Pallas kernels: 18.7 us -> 17.3 us
  blocking collectives: 11.8 us -> 10.6 us
  starting transfers between devices: 7.88 us -> 8.76 us
    ppermute x8, waiting for transfers between devices: 5.1 us -> 2.51 us  [exchange(): lax.ppermute(send, AXES, pairs)]
    all_to_all x1, blocking collectives: 11.8 us -> 10.6 us  [on_device(): gathered = lax.all_to_all(by_owner, AXES, 0, 0, tiled=True)]
    pallas_call x1, Pallas kernels: 5.66 us -> 4.59 us  [on_device(): pl.pallas_call(fixed(next_sweep, elem_count), out_shape=(slab, slab, slab...]
    ppermute x8, starting transfers between devices: 7.88 us -> 8.76 us  [exchange(): lax.ppermute(send, AXES, pairs)]
    pallas_call x1 -> x2, Pallas kernels: 9.98 us -> 9.58 us  [the longest x1 6.75 us: on_device(): pl.pallas_call(fixed(first_sweep, elem_count), out_shape=(slab, slab, sla...]
  transfers between devices with their start and end apart: 8 -> 8, of which waited for: 4 -> 2; matrix products, arithmetic and copies ran while one was open for 0% -> 0% of each run, Pallas kernels for 0% -> 7%
where the time goes in v3:
time: 40.1 us; the launch traced here: 40 us
  Pallas kernels  17.3 us (43%)
  blocking collectives  10.6 us (26%)
  starting transfers between devices  8.76 us (22%)
  waiting for transfers between devices  2.51 us (6%)
  between operations  0.77 us (2%)
    all_to_all x1, blocking collectives, on_device(): gathered = lax.all_to_all(by_owner, AXES, 0, 0, tiled=True)  10.6 us
    ppermute x8, starting transfers between devices, exchange(): lax.ppermute(send, AXES, pairs)  8.76 us
    pallas_call x1, Pallas kernels, on_device(): pl.pallas_call(fixed(first_sweep, elem_count), out_shape=(slab, slab, sla...  6.75 us
    pallas_call x1, Pallas kernels, on_device(): pl.pallas_call(fixed(next_sweep, elem_count), out_shape=(slab, slab, slab...  4.59 us
    pallas_call x1, Pallas kernels, on_device(): pl.pallas_call(fixed(fetch_and_plan, elem_count, n_sub, node_count), out_...  2.83 us
    ppermute x8, waiting for transfers between devices, exchange(): lax.ppermute(send, AXES, pairs)  2.51 us
    pallas_call x1, Pallas kernels, on_device(): pl.pallas_call(fixed(last_sweep, elem_count, n_sub, n_dev, node_count), o...  2.37 us
  transfers between devices with their start and end apart: 8, of which 2 were waited for; matrix products, arithmetic and copies ran while one was open for 0% of the time, Pallas kernels for 7%

profile of v3, /device:TPU:0, one launch (start us, length us, event | category | flops | bytes accessed | tf_op | source)
XLA Modules:
  0.0 40.0 jit_solution(16526286719556761586)
XLA Ops:
  0.6 0.0 copy-start.2
  0.6 0.0 copy-start.7
  0.7 0.0 copy-start.6
  0.7 0.0 copy-start.5
  0.7 6.8 %first_sweep.1 = (f32[16,320]{1,0:T(8,128)S(1)}, f32[16,320]{1,0:T(8,128)S(1)}, f32[16,320]{1,0:T(8,128)S(1)}, f32[16,320]{1,0:T(8,128)S(1)}, f32[6,16,320]{2,1,...) custom-call(f32[12,320]{1,0:T(8,128)} %refs_0_.4, bf16[6,12,320,320]{3,2,1,0:T(8,128)(2,1)} %refs_1_.2), custom_call_target="tpu_custom_call" | custom-call | tf_op jit(solution)/shard_map/first_sweep/pallas_call | solution.py:316
  7.4 0.0 copy-start
  7.5 0.5 %collective-permute-start = (f32[16,320]{1,0:T(8,128)S(1)}, f32[16,320]{1,0:T(8,128)S(1)}, u32[]{:S(2)}, u32[]{:S(2)}) collective-permute-start(f32[16,320]{1,0:T(8,128)S(1)} %get-tuple-element.19), channel_id=1, source_target_pairs={{0,4},{4,0},{8,12},{12,8},{16,20},{20,16},{24,28},{28,24},{1,5},{5... | collective-permute-start | bytes 61448 | tf_op jit(solution)/shard_map/ppermute | solution.py:290
  8.0 2.6 %collective-permute-start.1 = (f32[16,320]{1,0:T(8,128)S(1)}, f32[16,320]{1,0:T(8,128)S(1)}, u32[]{:S(2)}, u32[]{:S(2)}) collective-permute-start(f32[16,320]{1,0:T(8,128)S(1)} %get-tuple-element.20), channel_id=1, source_target_pairs={{4,8},{8,4},{12,16},{16,12},{20,24},{24,20},{5,9},{9,5},{13,17},{1... | collective-permute-start | bytes 61448 | tf_op jit(solution)/shard_map/ppermute | solution.py:290
  10.6 0.1 collective-permute-start.2
  10.7 1.2 %collective-permute-start.3 = (f32[16,320]{1,0:T(8,128)S(1)}, f32[16,320]{1,0:T(8,128)S(1)}, u32[]{:S(2)}, u32[]{:S(2)}) collective-permute-start(f32[16,320]{1,0:T(8,128)S(1)} %get-tuple-element.22), channel_id=1, source_target_pairs={{1,2},{2,1},{5,6},{6,5},{9,10},{10,9},{13,14},{14,13},{17,18},{18,... | collective-permute-start | bytes 61448 | tf_op jit(solution)/shard_map/ppermute | solution.py:290
  12.0 0.0 copy-done.5
  12.0 0.0 copy-start.3
  12.0 0.0 copy-start.4
  12.0 2.8 %fetch_and_plan.1 = (f32[12,320,320]{2,1,0:T(8,128)S(1)}, f32[16,160]{1,0:T(8,128)S(1)}, f32[8,384]{1,0:T(8,128)S(1)}) custom-call(f32[12,320,320]{2,1,0:T(8,128)} %refs_0_.5, s32[6,12]{1,0:T(8,128)S(1)} %bitcast.10, s32[8,12]{1,0:T(8,128)S(1)} %bitcast.11, s32[567]{0:T(1024)S(1)} %copy-done.7, f32[3,3,18]{2,1,0:T(4,128)S(1)} %copy-done.2, ...), custom_call_target="tpu_custom_call" | custom-call | bytes 4915200 | tf_op jit(solution)/shard_map/fetch_and_plan/pallas_call | solution.py:332
  14.8 0.0 collective-permute-done.refs_2_
  14.8 0.0 collective-permute-done.1.refs_3_
  14.8 0.0 collective-permute-done.2.refs_4_
  14.9 0.0 collective-permute-done.3.refs_5_
  14.9 4.6 %next_sweep.1 = (f32[16,320]{1,0:T(8,128)S(1)}, f32[16,320]{1,0:T(8,128)S(1)}, f32[16,320]{1,0:T(8,128)S(1)}, f32[16,320]{1,0:T(8,128)S(1)}, f32[6,16,320]{2,1,0:T(8,128)S(1)}) custom-call(f32[12,320]{1,0:T(8,128)S(1)} %copy-done.1, f32[6,16,320]{2,1,0:T(8,128)S(1)} %get-tuple-element.18.refs_5_.refs_1_, f32[16,320]{1,0:T(8,128)S(1)} %collective-permute-done.refs_2_, ...), custom_call_target="tpu_custom_call" | custom-call | tf_op jit(solution)/shard_map/next_sweep/pallas_call | solution.py:348
  19.5 0.1 collective-permute-start.4
  19.6 2.9 %collective-permute-start.5 = (f32[16,320]{1,0:T(8,128)S(1)}, f32[16,320]{1,0:T(8,128)S(1)}, u32[]{:S(2)}, u32[]{:S(2)}) collective-permute-start(f32[16,320]{1,0:T(8,128)S(1)} %get-tuple-element.28), channel_id=1, source_target_pairs={{4,8},{8,4},{12,16},{16,12},{20,24},{24,20},{5,9},{9,5},{13,17},{1... | collective-permute-start | bytes 61448 | tf_op jit(solution)/shard_map/ppermute | solution.py:290
  22.4 0.0 collective-permute-start.6
  22.4 1.3 %collective-permute-start.7 = (f32[16,320]{1,0:T(8,128)S(1)}, f32[16,320]{1,0:T(8,128)S(1)}, u32[]{:S(2)}, u32[]{:S(2)}) collective-permute-start(f32[16,320]{1,0:T(8,128)S(1)} %get-tuple-element.30), channel_id=1, source_target_pairs={{1,2},{2,1},{5,6},{6,5},{9,10},{10,9},{13,14},{14,13},{17,18},{18,... | collective-permute-start | bytes 61448 | tf_op jit(solution)/shard_map/ppermute | solution.py:290
  23.7 0.0 collective-permute-done.4.refs_2_
  23.7 0.5 %collective-permute-done.5.refs_3_ = f32[16,320]{1,0:T(8,128)S(1)} collective-permute-done((f32[16,320]{1,0:T(8,128)S(1)}, f32[16,320]{1,0:T(8,128)S(1)}, u32[]{:S(2)}, u32[]{:S(2)}) %collective-permute-start.5) | collective-permute-done | bytes 20512 | tf_op jit(solution)/shard_map/ppermute | solution.py:290
  24.2 2.0 %collective-permute-done.6.refs_4_ = f32[16,320]{1,0:T(8,128)S(1)} collective-permute-done((f32[16,320]{1,0:T(8,128)S(1)}, f32[16,320]{1,0:T(8,128)S(1)}, u32[]{:S(2)}, u32[]{:S(2)}) %collective-permute-start.6) | collective-permute-done | bytes 20512 | tf_op jit(solution)/shard_map/ppermute | solution.py:290
  26.2 0.0 collective-permute-done.7.refs_5_
  26.2 0.0 copy-done
  26.2 2.4 %last_sweep.1 = (f32[12,320]{1,0:T(8,128)}, f32[32,128]{1,0:T(8,128)S(1)}) custom-call(f32[12,320]{1,0:T(8,128)S(1)} %copy-done.1, f32[6,16,320]{2,1,0:T(8,128)S(1)} %get-tuple-element.26.refs_1_, f32[16,320]{1,0:T(8,128)S(1)} %collective-permute-done.4.refs_2_, f32[16,320]{1,0:T(8,128)S(1)} %collective-permute-done.5.refs_3_, ...), custom_call_target="tpu_custom_call" | custom-call | tf_op jit(solution)/shard_map/last_sweep/pallas_call | solution.py:358
  28.6 10.6 %all_to_all.11 = f32[32,1,128]{2,1,0:T(1,128)S(1)} all-to-all(f32[32,1,128]{2,1,0:T(1,128)S(1)} %bitcast.9), channel_id=1, replica_groups=mesh['dom'=8,'sub'=4] {'dom','sub'}, dimensions={0} | all-to-all | bytes 32768 | tf_op jit(solution)/shard_map/all_to_all | solution.py:371
  39.2 0.0 copy-done.3
  39.2 0.7 %stencil.1 = f32[3,18]{1,0:T(4,128)} custom-call(f32[32,128]{1,0:T(8,128)S(1)} %bitcast.8, f32[3,3,18]{2,1,0:T(4,128)S(1)} %copy-done.3, f32[3,3,18]{2,1,0:T(4,128)S(1)} %copy-done.2, f32[3,3,18]{2,1,0:T(4,128)S(1)} %copy-done.4), custom_call_target="tpu_custom_call" | custom-call | tf_op jit(solution)/shard_map/stencil/pallas_call | solution.py:372
  (6 shorter events, 0.0 us)
Async XLA Ops:
  0.6 11.3 %copy-start.2 = (f32[3,3,18]{2,1,0:T(4,128)S(1)}, f32[3,3,18]{2,1,0:T(4,128)}, u32[]{:S(2)}) copy-start(f32[3,3,18]{2,1,0:T(4,128)} %refs_2_.1) | copy-start | bytes 1948
  0.6 11.3 %copy-start.7 = (s32[567]{0:T(1024)S(1)}, s32[567]{0:T(1024)}, u32[]{:S(2)}) copy-start(s32[567]{0:T(1024)} %refs_3_.2) | copy-start | bytes 6808
  0.7 11.3 %copy-start.6 = (s32[12,8]{0,1:T(8,128)S(1)}, s32[12,8]{0,1:T(8,128)}, u32[]{:S(2)}) copy-start(s32[12,8]{0,1:T(8,128)} %param.17) | copy-start | bytes 1156
  0.7 11.3 %copy-start.5 = (s32[12,6]{0,1:T(8,128)S(1)}, s32[12,6]{0,1:T(8,128)}, u32[]{:S(2)}) copy-start(s32[12,6]{0,1:T(8,128)} %param.16) | copy-start | bytes 868
  0.7 14.2 %copy-start.1 = (f32[12,320]{1,0:T(8,128)S(1)}, f32[12,320]{1,0:T(8,128)}, u32[]{:S(2)}) copy-start(f32[12,320]{1,0:T(8,128)} %refs_0_.7) | copy-start | bytes 46084
  7.4 18.8 %copy-start = (bf16[12,24,320]{2,1,0:T(8,128)(2,1)S(1)}, bf16[12,24,320]{2,1,0:T(8,128)(2,1)}, u32[]{:S(2)}) copy-start(bf16[12,24,320]{2,1,0:T(8,128)(2,1)} %param.15) | copy-start | bytes 552964
  7.5 7.4 %collective-permute-start = (f32[16,320]{1,0:T(8,128)S(1)}, f32[16,320]{1,0:T(8,128)S(1)}, u32[]{:S(2)}, u32[]{:S(2)}) collective-permute-start(f32[16,320]{1,0:T(8,128)S(1)} %get-tuple-element.19), channel_id=1, source_target_pairs={{0,4},{4,0},{8,12},{12,8},{16,20},{20,16},{24,28},{28,24},{1,5},{5... | collective-permute-start | bytes 61448 | tf_op jit(solution)/shard_map/ppermute | solution.py:290
  8.0 6.9 %collective-permute-start.1 = (f32[16,320]{1,0:T(8,128)S(1)}, f32[16,320]{1,0:T(8,128)S(1)}, u32[]{:S(2)}, u32[]{:S(2)}) collective-permute-start(f32[16,320]{1,0:T(8,128)S(1)} %get-tuple-element.20), channel_id=1, source_target_pairs={{4,8},{8,4},{12,16},{16,12},{20,24},{24,20},{5,9},{9,5},{13,17},{1... | collective-permute-start | bytes 61448 | tf_op jit(solution)/shard_map/ppermute | solution.py:290
  10.6 4.2 %collective-permute-start.2 = (f32[16,320]{1,0:T(8,128)S(1)}, f32[16,320]{1,0:T(8,128)S(1)}, u32[]{:S(2)}, u32[]{:S(2)}) collective-permute-start(f32[16,320]{1,0:T(8,128)S(1)} %get-tuple-element.21), channel_id=1, source_target_pairs={{0,1},{1,0},{2,3},{3,2},{4,5},{5,4},{6,7},{7,6},{8,9},{9,8},{10,11... | collective-permute-start | bytes 61448 | tf_op jit(solution)/shard_map/ppermute | solution.py:290
  10.7 4.2 %collective-permute-start.3 = (f32[16,320]{1,0:T(8,128)S(1)}, f32[16,320]{1,0:T(8,128)S(1)}, u32[]{:S(2)}, u32[]{:S(2)}) collective-permute-start(f32[16,320]{1,0:T(8,128)S(1)} %get-tuple-element.22), channel_id=1, source_target_pairs={{1,2},{2,1},{5,6},{6,5},{9,10},{10,9},{13,14},{14,13},{17,18},{18,... | collective-permute-start | bytes 61448 | tf_op jit(solution)/shard_map/ppermute | solution.py:290
  12.0 27.3 %copy-start.3 = (f32[3,3,18]{2,1,0:T(4,128)S(1)}, f32[3,3,18]{2,1,0:T(4,128)}, u32[]{:S(2)}) copy-start(f32[3,3,18]{2,1,0:T(4,128)} %refs_1_.3) | copy-start | bytes 1948
  12.0 27.3 %copy-start.4 = (f32[3,3,18]{2,1,0:T(4,128)S(1)}, f32[3,3,18]{2,1,0:T(4,128)}, u32[]{:S(2)}) copy-start(f32[3,3,18]{2,1,0:T(4,128)} %refs_3_.3) | copy-start | bytes 1948
  19.5 4.3 %collective-permute-start.4 = (f32[16,320]{1,0:T(8,128)S(1)}, f32[16,320]{1,0:T(8,128)S(1)}, u32[]{:S(2)}, u32[]{:S(2)}) collective-permute-start(f32[16,320]{1,0:T(8,128)S(1)} %get-tuple-element.27), channel_id=1, source_target_pairs={{0,4},{4,0},{8,12},{12,8},{16,20},{20,16},{24,28},{28,24},{1,5},{5... | collective-permute-start | bytes 61448 | tf_op jit(solution)/shard_map/ppermute | solution.py:290
  19.6 4.7 %collective-permute-start.5 = (f32[16,320]{1,0:T(8,128)S(1)}, f32[16,320]{1,0:T(8,128)S(1)}, u32[]{:S(2)}, u32[]{:S(2)}) collective-permute-start(f32[16,320]{1,0:T(8,128)S(1)} %get-tuple-element.28), channel_id=1, source_target_pairs={{4,8},{8,4},{12,16},{16,12},{20,24},{24,20},{5,9},{9,5},{13,17},{1... | collective-permute-start | bytes 61448 | tf_op jit(solution)/shard_map/ppermute | solution.py:290
  22.4 3.8 %collective-permute-start.6 = (f32[16,320]{1,0:T(8,128)S(1)}, f32[16,320]{1,0:T(8,128)S(1)}, u32[]{:S(2)}, u32[]{:S(2)}) collective-permute-start(f32[16,320]{1,0:T(8,128)S(1)} %get-tuple-element.29), channel_id=1, source_target_pairs={{0,1},{1,0},{2,3},{3,2},{4,5},{5,4},{6,7},{7,6},{8,9},{9,8},{10,11... | collective-permute-start | bytes 61448 | tf_op jit(solution)/shard_map/ppermute | solution.py:290
  22.4 3.8 %collective-permute-start.7 = (f32[16,320]{1,0:T(8,128)S(1)}, f32[16,320]{1,0:T(8,128)S(1)}, u32[]{:S(2)}, u32[]{:S(2)}) collective-permute-start(f32[16,320]{1,0:T(8,128)S(1)} %get-tuple-element.30), channel_id=1, source_target_pairs={{1,2},{2,1},{5,6},{6,5},{9,10},{10,9},{13,14},{14,13},{17,18},{18,... | collective-permute-start | bytes 61448 | tf_op jit(solution)/shard_map/ppermute | solution.py:290

commit v4 on v3

--- a/solution.py
+++ b/solution.py
@@ -9,6 +9,9 @@
 CORNERS = 8
 AXES = ("dom", "sub")
 PAIR = 2
+AHEAD = 4
+GAP_BYTES = 20_000_000
+UNROLL = 4
 ROWS = 16
 
 f32 = jnp.float32
@@ -88,8 +91,13 @@
 
 def element_faces(e, adj_rows, blocks, faces):
     row = adj_rows[pl.ds(e, 1), :].astype(bf16)
-    for k in range(NF):
+    for k in range(blocks.shape[0]):
         faces[k, pl.ds(e, 1), :] = jnp.dot(row, blocks[k, e], preferred_element_type=f32)
+
+
+def send_slots():
+    dom_odd, sub_odd = lax.axis_index("dom") % 2, lax.axis_index("sub") % 2
+    return dom_odd, 1 - dom_odd, 2 + sub_odd, 3 - sub_odd
 
 
 def fill_sends(faces, sends):
@@ -101,29 +109,28 @@
     sends[3][...] = jnp.where(sub_even, faces[3], faces[2])
 
 
-def sum_chooser(elem_count, n_sub, neighbor_rows, square):
-    dom, sub = lax.axis_index("dom"), lax.axis_index("sub")
-    device = dom * n_sub + sub
+def sum_choosers(elem_count, n_sub, neighbor_rows, square):
+    device = lax.axis_index("dom") * n_sub + lax.axis_index("sub")
     first = device * elem_count
     square[...] = jnp.zeros(square.shape, i32)
     square[0:NF, 0:elem_count] = neighbor_rows
     by_element = square[...].T[0:ROWS, :]
-    dom_odd, sub_odd = dom % 2, sub % 2
-    slots = (dom_odd, 1 - dom_odd, 2 + sub_odd, 3 - sub_odd)
+    slots = send_slots() + (4, 5)
     offsets = (n_sub, -n_sub, 1, -1)
-    columns = iota((ROWS, (NF + 4) * ROWS), 1)
+    near, far = iota((ROWS, NF * ROWS), 1), iota((ROWS, 4 * ROWS), 1)
     live = iota((ROWS, 1), 0) < elem_count
-    total = jnp.zeros(columns.shape, f32)
+    near_total, far_total = jnp.zeros(near.shape, f32), jnp.zeros(far.shape, f32)
     for k in range(NF):
         ids = by_element[:, k : k + 1]
+        valid = live & (ids >= 0)
         inside = (ids >= first) & (ids < first + elem_count)
-        column = (k ^ 1) * ROWS + ids - first
+        column = jnp.where(valid & inside, slots[k ^ 1] * ROWS + ids - first, -1)
+        near_total = near_total + jnp.where(near == column, 1.0, 0.0)
         if k < 4:
-            away = (NF + slots[k]) * ROWS + ids - first - offsets[k] * elem_count
-            column = jnp.where(inside, column, away)
-        column = jnp.where(live & (ids >= 0), column, -1)
-        total = total + jnp.where(columns == column, 1.0, 0.0)
-    return total
+            column = slots[k] * ROWS + ids - first - offsets[k] * elem_count
+            column = jnp.where(valid & jnp.logical_not(inside), column, -1)
+            far_total = far_total + jnp.where(far == column, 1.0, 0.0)
+    return near_total, far_total
 
 
 def corner_lanes(elem_count, node_count, corner_rows, place_row):
@@ -149,36 +156,75 @@
     return jnp.dot(pair, found, preferred_element_type=f32)
 
 
-def first_sweep(elem_count, start, offdiag, send_0, send_1, send_2, send_3, faces, blocks,
-                start_v, start_sem, block_sem):
-    def block_copy(index):
+def block_copies(offdiag, first_face, blocks, sems):
+    faces = pl.ds(first_face, blocks.shape[0])
+
+    def copy(index):
         held = pl.ds(index * PAIR, PAIR)
-        return pltpu.make_async_copy(
-            offdiag.at[:, held], blocks.at[:, held], block_sem.at[index]
-        )
-
+        return pltpu.make_async_copy(offdiag.at[faces, held], blocks.at[:, held], sems.at[index])
+
+    return copy
+
+
+def start_copies(elem_count, block_copy):
+    for index in range(min(AHEAD, elem_count // PAIR)):
+        block_copy(index).start()
+
+
+def streamed_faces(elem_count, adj_rows, block_copy, blocks, faces):
+    def step(index, _):
+        block_copy(index).wait()
+
+        @pl.when(index + AHEAD < elem_count // PAIR)
+        def _():
+            block_copy(index + AHEAD).start()
+
+        for offset in range(PAIR):
+            element_faces(index * PAIR + offset, adj_rows, blocks, faces)
+        return 0
+
+    lax.fori_loop(0, elem_count // PAIR, step, 0)
+
+
+def first_sweep(elem_count, start, offdiag, send_0, send_1, send_2, send_3, blocks,
+                start_v, faces, start_sem, block_sem):
     start_copy = pltpu.make_async_copy(start, start_v, start_sem)
+    block_copy = block_copies(offdiag, 0, blocks, block_sem)
     start_copy.start()
-    for index in range(elem_count // PAIR):
-        block_copy(index).start()
+    start_copies(elem_count, block_copy)
     faces[...] = jnp.zeros(faces.shape, f32)
     start_copy.wait()
-
-    def step(index, _):
-        block_copy(index).wait()
-        for offset in range(PAIR):
-            element_faces(index * PAIR + offset, start_v, blocks, faces)
-        return 0
-
-    lax.fori_loop(0, elem_count // PAIR, step, 0)
+    streamed_faces(elem_count, start_v, block_copy, blocks, faces)
     fill_sends(faces, (send_0, send_1, send_2, send_3))
 
 
-def fetch_and_plan(elem_count, n_sub, node_count, inverse_hbm, neighbor, corner, place, upper,
-                   after, inverse, chooser, table, square, sem):
-    copy = pltpu.make_async_copy(inverse_hbm, inverse, sem)
-    copy.start()
-    chooser[...] = sum_chooser(elem_count, n_sub, neighbor[...], square)
+def local_rest(elem_count, rhs, sends, faces, near):
+    terms = jnp.concatenate([send[...] for send in sends] + [faces[0], faces[1]], axis=0)
+    own = one_hot_dot(near[...].astype(bf16), terms)
+    return rhs[...] - own[0:elem_count, :]
+
+
+def first_gap(elem_count, n_sub, offdiag, start, rhs, neighbor, send_0, send_1, send_2, send_3,
+              blocks, near, far, rest, faces, square, block_sem):
+    block_copy = block_copies(offdiag, 4, blocks, block_sem)
+    start_copies(elem_count, block_copy)
+    faces[...] = jnp.zeros(faces.shape, f32)
+    near[...], far[...] = sum_choosers(elem_count, n_sub, neighbor[...], square)
+    streamed_faces(elem_count, start, block_copy, blocks, faces)
+    rest[...] = jnp.zeros(rest.shape, f32)
+    rest[0:elem_count, :] = local_rest(
+        elem_count, rhs, (send_0, send_1, send_2, send_3), faces, near
+    )
+
+
+def second_gap(elem_count, node_count, adj, rhs, near, blocks, corner, place, upper,
+               send_0, send_1, send_2, send_3, rest, table, faces):
+    faces[...] = jnp.zeros(faces.shape, f32)
+    grouped(elem_count, 4, lambda e: element_faces(e, adj, blocks, faces))
+    rest[...] = jnp.zeros(rest.shape, f32)
+    rest[0:elem_count, :] = local_rest(
+        elem_count, rhs, (send_0, send_1, send_2, send_3), faces, near
+    )
     table[...] = jnp.zeros(table.shape, f32)
     width = 3 * CORNERS * elem_count
     table[0:8, 0:width] = corner_lanes(elem_count, node_count, corner[...], place[...][None, :])
@@ -189,43 +235,42 @@
         column = upper[a][:, node_count - 1 : node_count]
         last = last + jnp.where(lane == base + 3 * a + row, column, 0.0)
     table[2:3, 0:128] = jnp.sum(last, axis=0, keepdims=True)
-    copy.wait()
-
-
-def apply_inverse(elem_count, rhs, faces, arrived, chooser, inverse, carried_v, columns):
-    size = rhs.shape[1]
-    terms = jnp.concatenate(
-        [faces[...].reshape(NF * ROWS, size)] + [a[...] for a in arrived], axis=0
-    )
-    carried = one_hot_dot(chooser[...].astype(bf16), terms)
-    carried_v[0:elem_count, :] = rhs[...] - carried[0:elem_count, :]
+
+
+def apply_inverse(elem_count, rest, arrived, far, inverse, rest_v, columns):
+    size = rest.shape[1]
+    terms = jnp.concatenate([a[...] for a in arrived], axis=0)
+    rest_v[...] = rest[...] - one_hot_dot(far[...].astype(bf16), terms)
     lane = iota((size, 128), 1)
     columns[...] = jnp.zeros(columns.shape, f32)
 
-    def one_element(e, _):
-        product = inverse[e] * carried_v[pl.ds(e, 1), :]
-        total = jnp.sum(product, axis=1, keepdims=True)
-        columns[0:size, :] = jnp.where(lane == e, total, columns[0:size, :])
+    def some_elements(index, _):
+        total = columns[0:size, :]
+        for e in range(UNROLL):
+            e = index * UNROLL + e
+            product = inverse[e] * rest_v[pl.ds(e, 1), :]
+            total = jnp.where(lane == e, jnp.sum(product, axis=1, keepdims=True), total)
+        columns[0:size, :] = total
         return 0
 
-    lax.fori_loop(0, elem_count, one_element, 0)
+    lax.fori_loop(0, elem_count // UNROLL, some_elements, 0)
     return columns[...].T[0:ROWS, 0:size]
 
 
-def next_sweep(elem_count, rhs, faces_in, arr_0, arr_1, arr_2, arr_3, chooser, inverse, blocks,
-               send_0, send_1, send_2, send_3, faces, carried_v, columns, adj_v):
-    adj_v[...] = apply_inverse(
-        elem_count, rhs, faces_in, (arr_0, arr_1, arr_2, arr_3), chooser, inverse, carried_v, columns
+def next_sweep(elem_count, rest, arr_0, arr_1, arr_2, arr_3, far, inverse, blocks,
+               send_0, send_1, send_2, send_3, adj, rest_v, columns, faces):
+    adj[...] = apply_inverse(
+        elem_count, rest, (arr_0, arr_1, arr_2, arr_3), far, inverse, rest_v, columns
     )
     faces[...] = jnp.zeros(faces.shape, f32)
-    grouped(elem_count, 4, lambda e: element_faces(e, adj_v, blocks, faces))
+    grouped(elem_count, 4, lambda e: element_faces(e, adj, blocks, faces))
     fill_sends(faces, (send_0, send_1, send_2, send_3))
 
 
-def last_sweep(elem_count, n_sub, n_dev, node_count, rhs, faces_in, arr_0, arr_1, arr_2, arr_3,
-               chooser, inverse, geometry, table, adjoint, out, carried_v, columns):
+def last_sweep(elem_count, n_sub, n_dev, node_count, rest, arr_0, arr_1, arr_2, arr_3,
+               far, inverse, geometry, table, adjoint, out, rest_v, columns):
     rows = apply_inverse(
-        elem_count, rhs, faces_in, (arr_0, arr_1, arr_2, arr_3), chooser, inverse, carried_v, columns
+        elem_count, rest, (arr_0, arr_1, arr_2, arr_3), far, inverse, rest_v, columns
     )
     adjoint[...] = rows[0:elem_count, :]
     width = 3 * CORNERS * elem_count
@@ -296,78 +341,97 @@
         elem_count, size = adjoint_rhs.shape
         node_count = stiff_diag.shape[2]
         assert elem_count <= ROWS and elem_count % PAIR == 0
+        assert elem_count % UNROLL == 0
         assert n_dev <= 256 and 1 < node_count <= 256
         assert 3 * (node_count + 2) + 9 <= 128
         width = 3 * CORNERS * elem_count
         slab = jax.ShapeDtypeStruct((ROWS, size), f32)
-        faces_shape = jax.ShapeDtypeStruct((NF, ROWS, size), f32)
+        near = jax.ShapeDtypeStruct((ROWS, NF * ROWS), f32)
+        far = jax.ShapeDtypeStruct((ROWS, 4 * ROWS), f32)
         limit = pltpu.CompilerParams(vmem_limit_bytes=8 << 20)
         column_scratch = [
             pltpu.VMEM((ROWS, size), f32),
             pltpu.VMEM((up_to(size, 128), 128), f32),
         ]
 
+        def blocks_of(faces):
+            return pltpu.VMEM((faces,) + offdiag_blocks.shape[1:], bf16)
+
+        def faces_of(faces):
+            return pltpu.VMEM((faces, ROWS, size), f32)
+
         def fixed(body, *numbers):
             def call(*refs):
                 return body(*numbers, *refs)
 
             return call
 
-        *sends, faces, blocks = pl.pallas_call(
+        offdiag = in_hbm(offdiag_blocks)
+        inverse = pltpu.with_memory_space_constraint(diag_inverse, pltpu.VMEM)
+        copies = elem_count // PAIR
+        *sends, blocks = pl.pallas_call(
             fixed(first_sweep, elem_count),
-            out_shape=(
-                slab, slab, slab, slab, faces_shape, pltpu.VMEM(offdiag_blocks.shape, bf16),
-            ),
+            out_shape=(slab, slab, slab, slab, blocks_of(4)),
             in_specs=[IN_HBM] * 2,
-            out_specs=(IN_VMEM,) * 6,
+            out_specs=(IN_VMEM,) * 5,
             scratch_shapes=[
                 pltpu.VMEM((elem_count, size), f32),
+                faces_of(4),
                 pltpu.SemaphoreType.DMA,
-                pltpu.SemaphoreType.DMA((elem_count // PAIR,)),
+                pltpu.SemaphoreType.DMA((copies,)),
             ],
             compiler_params=limit,
             name="first_sweep",
-        )(in_hbm(adjoint_start), in_hbm(offdiag_blocks))
+        )(in_hbm(adjoint_start), offdiag)
         arrived = exchange(sends)
-        inverse, chooser, table = pl.pallas_call(
-            fixed(fetch_and_plan, elem_count, n_sub, node_count),
-            out_shape=(
-                pltpu.VMEM(diag_inverse.shape, f32),
-                jax.ShapeDtypeStruct((ROWS, (NF + 4) * ROWS), f32),
-                jax.ShapeDtypeStruct((8, up_to(width, 128)), f32),
+        more_blocks, near, far, rest = pl.pallas_call(
+            fixed(first_gap, elem_count, n_sub),
+            out_shape=(blocks_of(2), near, far, slab),
+            in_specs=[IN_HBM] + [IN_VMEM] * 7,
+            out_specs=(IN_VMEM,) * 4,
+            scratch_shapes=[
+                faces_of(2), pltpu.VMEM((128, 128), i32), pltpu.SemaphoreType.DMA((copies,)),
+            ],
+            compiler_params=limit,
+            cost_estimate=pl.CostEstimate(
+                flops=0, bytes_accessed=GAP_BYTES, transcendentals=0
             ),
-            in_specs=[IN_HBM] + [IN_VMEM] * 5,
-            out_specs=(IN_VMEM,) * 3,
-            scratch_shapes=[pltpu.VMEM((128, 128), i32), pltpu.SemaphoreType.DMA],
+            name="first_gap",
+        )(offdiag, adjoint_start, adjoint_rhs, neighbor.T, *sends)
+        *sends, adj = pl.pallas_call(
+            fixed(next_sweep, elem_count),
+            out_shape=(slab,) * 5,
+            in_specs=[IN_VMEM] * 8,
+            out_specs=(IN_VMEM,) * 5,
+            scratch_shapes=column_scratch + [faces_of(4)],
+            compiler_params=limit,
+            name="next_sweep",
+        )(rest, *arrived, far, inverse, blocks)
+        arrived = exchange(sends)
+        rest, table = pl.pallas_call(
+            fixed(second_gap, elem_count, node_count),
+            out_shape=(slab, jax.ShapeDtypeStruct((8, up_to(width, 128)), f32)),
+            in_specs=[IN_VMEM] * 11,
+            out_specs=(IN_VMEM,) * 2,
+            scratch_shapes=[faces_of(2)],
             compiler_params=limit,
             cost_estimate=pl.CostEstimate(
-                flops=0, bytes_accessed=4 * diag_inverse.size, transcendentals=0
+                flops=0, bytes_accessed=GAP_BYTES, transcendentals=0
             ),
-            name="fetch_and_plan",
-        )(in_hbm(diag_inverse), neighbor.T, corner_node.T, deform_place, stiff_upper, faces)
-        *sends, faces = pl.pallas_call(
-            fixed(next_sweep, elem_count),
-            out_shape=(slab, slab, slab, slab, faces_shape),
-            in_specs=[IN_VMEM] * 9,
-            out_specs=(IN_VMEM,) * 5,
-            scratch_shapes=column_scratch + [pltpu.VMEM((ROWS, size), f32)],
-            compiler_params=limit,
-            name="next_sweep",
-        )(adjoint_rhs, faces, *arrived, chooser, inverse, blocks)
-        arrived = exchange(sends)
+            name="second_gap",
+        )(adj, adjoint_rhs, near, more_blocks, corner_node.T, deform_place, stiff_upper, *sends)
         adjoint, by_owner = pl.pallas_call(
             fixed(last_sweep, elem_count, n_sub, n_dev, node_count),
             out_shape=(
-                jax.ShapeDtypeStruct((elem_count, size), f32),
+                pltpu.VMEM((elem_count, size), f32),
                 jax.ShapeDtypeStruct((n_dev, 128), f32),
             ),
-            in_specs=[IN_VMEM] * 10,
+            in_specs=[IN_VMEM] * 9,
             out_specs=(IN_VMEM,) * 2,
             scratch_shapes=column_scratch,
             compiler_params=limit,
             name="last_sweep",
-        )(adjoint_rhs, faces, *arrived, chooser, inverse,
-          geometry_jac.reshape(width, size), table)
+        )(rest, *arrived, far, inverse, geometry_jac.reshape(width, size), table)
         gathered = lax.all_to_all(by_owner, AXES, 0, 0, tiled=True)
         shape_grad = pl.pallas_call(
             fixed(stencil, node_count),

time: 40.1 us -> 37.8 us (0.943)
  blocking collectives: 10.6 us -> 0 us
  waiting for transfers between devices: 2.51 us -> 7.51 us
  starting transfers between devices: 8.76 us -> 12.1 us
  Pallas kernels: 17.3 us -> 16.6 us
  local copies, waits for them, and re-layouts: 0.04 us -> 0.67 us
    all_to_all x1 -> x0, blocking collectives: 10.6 us -> none  [on_device(): gathered = lax.all_to_all(by_owner, AXES, 0, 0, tiled=True)]
    all_to_all x0 -> x1, waiting for transfers between devices: none -> 6.56 us  [on_device(): gathered = lax.all_to_all(by_owner, AXES, 0, 0, tiled=True)]
    all_to_all x0 -> x1, starting transfers between devices: none -> 3.32 us  [on_device(): gathered = lax.all_to_all(by_owner, AXES, 0, 0, tiled=True)]
    ppermute x8, waiting for transfers between devices: 2.51 us -> 0.95 us  [exchange(): lax.ppermute(send, AXES, pairs)]
    pallas_call x1, Pallas kernels: 6.75 us -> 5.77 us  [on_device(): pl.pallas_call(fixed(first_sweep, elem_count), out_shape=(slab, slab, sla...]
    pallas_call x2 -> x3, Pallas kernels: 7.42 us -> 8.08 us  [the longest x1 3.5 us: on_device(): pl.pallas_call(fixed(first_gap, elem_count, n_sub), out_shape=(blocks_of(...]
    unnamed x16 -> x23, local copies, waits for them, and re-layouts: 0.04 us -> 0.67 us
    pallas_call x1, Pallas kernels: 2.37 us -> 1.97 us  [on_device(): pl.pallas_call(fixed(last_sweep, elem_count, n_sub, n_dev, node_count), o...]
  transfers between devices with their start and end apart: 8 -> 9, of which waited for: 2 -> 2; matrix products, arithmetic and copies ran while one was open for 0% -> 2% of each run, Pallas kernels for 7% -> 13%
where the time goes in v4:
time: 37.8 us; the launch traced here: 37.6 us
  Pallas kernels  16.6 us (44%)
  starting transfers between devices  12.1 us (32%)
  waiting for transfers between devices  7.51 us (20%)
  between operations  0.81 us (2%)
  local copies, waits for them, and re-layouts  0.67 us (2%)
    ppermute x8, starting transfers between devices, exchange(): lax.ppermute(send, AXES, pairs)  8.76 us
    all_to_all x1, waiting for transfers between devices, on_device(): gathered = lax.all_to_all(by_owner, AXES, 0, 0, tiled=True)  6.56 us
    pallas_call x1, Pallas kernels, on_device(): pl.pallas_call(fixed(first_sweep, elem_count), out_shape=(slab, slab, sla...  5.77 us
    pallas_call x1, Pallas kernels, on_device(): pl.pallas_call(fixed(first_gap, elem_count, n_sub), out_shape=(blocks_of(...  3.5 us
    all_to_all x1, starting transfers between devices, on_device(): gathered = lax.all_to_all(by_owner, AXES, 0, 0, tiled=True)  3.32 us
    pallas_call x1, Pallas kernels, on_device(): pl.pallas_call(fixed(next_sweep, elem_count), out_shape=(slab,) * 5, in_s...  3.04 us
    pallas_call x1, Pallas kernels, on_device(): pl.pallas_call(fixed(last_sweep, elem_count, n_sub, n_dev, node_count), o...  1.97 us
    pallas_call x1, Pallas kernels, on_device(): pl.pallas_call(fixed(second_gap, elem_count, node_count), out_shape=(slab...  1.55 us
  transfers between devices with their start and end apart: 9, of which 2 were waited for; matrix products, arithmetic and copies ran while one was open for 2% of the time, Pallas kernels for 13%

profile of v4, /device:TPU:0, one launch (start us, length us, event | category | flops | bytes accessed | tf_op | source)
XLA Modules:
  0.0 37.6 jit_solution(533384480103856316)
XLA Ops:
  0.7 5.8 %first_sweep.1 = (f32[16,320]{1,0:T(8,128)S(1)}, f32[16,320]{1,0:T(8,128)S(1)}, f32[16,320]{1,0:T(8,128)S(1)}, f32[16,320]{1,0:T(8,128)S(1)}, bf16[4,12,320,320]{3,2,1,0:T(8,128)(2,1)S(1)}) custom-call(f32[12,320]{1,0:T(8,128)} %refs_1_.5, bf16[6,12,320,320]{3,2,1,0:T(8,128)(2,1)} %refs_0_.3), custom_call_target="tpu_custom_call" | custom-call | tf_op jit(solution)/shard_map/first_sweep/pallas_call | solution.py:372
  6.4 0.0 slice-start
  6.4 0.5 %collective-permute-start = (f32[16,320]{1,0:T(8,128)S(1)}, f32[16,320]{1,0:T(8,128)S(1)}, u32[]{:S(2)}, u32[]{:S(2)}) collective-permute-start(f32[16,320]{1,0:T(8,128)S(1)} %get-tuple-element.20.refs_4_), channel_id=1, source_target_pairs={{0,4},{4,0},{8,12},{12,8},{16,20},{20,16},{24,28},{28,24},{1,5},{5... | collective-permute-start | bytes 61448 | tf_op jit(solution)/shard_map/ppermute | solution.py:335
  7.0 2.6 %collective-permute-start.1 = (f32[16,320]{1,0:T(8,128)S(1)}, f32[16,320]{1,0:T(8,128)S(1)}, u32[]{:S(2)}, u32[]{:S(2)}) collective-permute-start(f32[16,320]{1,0:T(8,128)S(1)} %get-tuple-element.21.refs_5_), channel_id=1, source_target_pairs={{4,8},{8,4},{12,16},{16,12},{20,24},{24,20},{5,9},{9,5},{13,17},{1... | collective-permute-start | bytes 61448 | tf_op jit(solution)/shard_map/ppermute | solution.py:335
  9.6 0.1 collective-permute-start.2
  9.7 1.2 %collective-permute-start.3 = (f32[16,320]{1,0:T(8,128)S(1)}, f32[16,320]{1,0:T(8,128)S(1)}, u32[]{:S(2)}, u32[]{:S(2)}) collective-permute-start(f32[16,320]{1,0:T(8,128)S(1)} %get-tuple-element.23.refs_7_), channel_id=1, source_target_pairs={{1,2},{2,1},{5,6},{6,5},{9,10},{10,9},{13,14},{14,13},{17,18},{18,... | collective-permute-start | bytes 61448 | tf_op jit(solution)/shard_map/ppermute | solution.py:335
  11.0 3.5 %first_gap.1 = (bf16[2,12,320,320]{3,2,1,0:T(8,128)(2,1)S(1)}, f32[16,96]{1,0:T(8,128)S(1)}, f32[16,64]{1,0:T(8,128)S(1)}, f32[16,320]{1,0:T(8,128)S(1)}) custom-call(bf16[6,12,320,320]{3,2,1,0:T(8,128)(2,1)} %refs_0_.3, f32[12,320]{1,0:T(8,128)S(1)} %copy-done.1, f32[12,320]{1,0:T(8,128)S(1)} %copy-done.2, s32[6,12]{1,0:T(8,128)S(1)} %bitcast.12, ...), custom_call_target="tpu_custom_call" | custom-call | bytes 20000000 | tf_op jit(solution)/shard_map/first_gap/pallas_call | solution.py:387
  14.5 0.0 copy-start.3
  14.5 0.0 copy-start.6
  14.5 0.0 copy-start.7
  14.5 0.0 collective-permute-done.refs_1_
  14.5 0.0 collective-permute-done.1.refs_2_
  14.5 0.0 collective-permute-done.2.refs_3_
  14.5 0.0 collective-permute-done.3.refs_4_
  14.6 0.0 copy-start
  14.6 0.0 copy-start.4
  14.6 0.0 copy-start.5
  14.6 3.0 %next_sweep.1 = (f32[16,320]{1,0:T(8,128)S(1)}, f32[16,320]{1,0:T(8,128)S(1)}, f32[16,320]{1,0:T(8,128)S(1)}, f32[16,320]{1,0:T(8,128)S(1)}, f32[16,320]{1,0:T(8,128)S(1)}) custom-call(f32[16,320]{1,0:T(8,128)S(1)} %get-tuple-element.24.refs_0_, f32[16,320]{1,0:T(8,128)S(1)} %collective-permute-done.refs_1_, f32[16,320]{1,0:T(8,128)S(1)} %collective-permute-done.1.refs_2_, ...), custom_call_target="tpu_custom_call" | custom-call | tf_op jit(solution)/shard_map/next_sweep/pallas_call | solution.py:401
  17.7 0.1 collective-permute-start.4
  17.7 2.9 %collective-permute-start.5 = (f32[16,320]{1,0:T(8,128)S(1)}, f32[16,320]{1,0:T(8,128)S(1)}, u32[]{:S(2)}, u32[]{:S(2)}) collective-permute-start(f32[16,320]{1,0:T(8,128)S(1)} %get-tuple-element.31.refs_8_), channel_id=1, source_target_pairs={{4,8},{8,4},{12,16},{16,12},{20,24},{24,20},{5,9},{9,5},{13,17},{1... | collective-permute-start | bytes 61448 | tf_op jit(solution)/shard_map/ppermute | solution.py:335
  20.6 0.0 collective-permute-start.6
  20.6 1.3 %collective-permute-start.7 = (f32[16,320]{1,0:T(8,128)S(1)}, f32[16,320]{1,0:T(8,128)S(1)}, u32[]{:S(2)}, u32[]{:S(2)}) collective-permute-start(f32[16,320]{1,0:T(8,128)S(1)} %get-tuple-element.33.refs_10_), channel_id=1, source_target_pairs={{1,2},{2,1},{5,6},{6,5},{9,10},{10,9},{13,14},{14,13},{17,18},{18,... | collective-permute-start | bytes 61448 | tf_op jit(solution)/shard_map/ppermute | solution.py:335
  21.9 1.5 %second_gap.1 = (f32[16,320]{1,0:T(8,128)S(1)}, f32[8,384]{1,0:T(8,128)S(1)}) custom-call(f32[16,320]{1,0:T(8,128)S(1)} %get-tuple-element.27.refs_0_, f32[12,320]{1,0:T(8,128)S(1)} %copy-done.2, f32[16,96]{1,0:T(8,128)S(1)} %get-tuple-element.28.refs_2_, bf16[2,12,320,320]{3,2,1,0:T(8,128)(2,1)S(1)} %get-tuple-element.29.refs_3_, s32[8,12]{1,0:T(8,128)S(1)} %bitcast.11, ...), custom_call_target="tpu_custom_call" | custom-call | bytes 20000000 | tf_op jit(solution)/shard_map/second_gap/pallas_call | solution.py:411
  23.5 0.0 collective-permute-done.4.refs_1_
  23.5 0.0 collective-permute-done.5.refs_2_
  23.5 0.9 %collective-permute-done.6.refs_3_ = f32[16,320]{1,0:T(8,128)S(1)} collective-permute-done((f32[16,320]{1,0:T(8,128)S(1)}, f32[16,320]{1,0:T(8,128)S(1)}, u32[]{:S(2)}, u32[]{:S(2)}) %collective-permute-start.6) | collective-permute-done | bytes 20512 | tf_op jit(solution)/shard_map/ppermute | solution.py:335
  24.4 0.0 collective-permute-done.7.refs_4_
  24.4 2.0 %last_sweep.1 = (f32[12,320]{1,0:T(8,128)S(1)}, f32[32,128]{1,0:T(8,128)}) custom-call(f32[16,320]{1,0:T(8,128)S(1)} %get-tuple-element.34.refs_0_, f32[16,320]{1,0:T(8,128)S(1)} %collective-permute-done.4.refs_1_, f32[16,320]{1,0:T(8,128)S(1)} %collective-permute-done.5.refs_2_, f32[16,320]{1,0:T(8,128)S(1)} %collective-permute-done.6.refs_3_, ...), custom_call_target="tpu_custom_call" | custom-call | tf_op jit(solution)/shard_map/last_sweep/pallas_call | solution.py:423
  26.4 3.3 %all-to-all-start = ((f32[32,1,128]{2,1,0:T(1,128)}), f32[32,1,128]{2,1,0:T(1,128)S(1)}, u32[]{:S(2)}, u32[]{:S(2)}) async-start(f32[32,1,128]{2,1,0:T(1,128)} %bitcast.4), calls=%async_computation | async-start | bytes 32768 | tf_op jit(solution)/shard_map/all_to_all | solution.py:435
  29.7 0.6 %copy.14 = f32[12,320]{1,0:T(8,128)} copy(f32[12,320]{1,0:T(8,128)S(1)} %get-tuple-element.38) | data formatting | bytes 30720
  30.3 6.6 %all-to-all-done = f32[32,1,128]{2,1,0:T(1,128)S(1)} async-done(((f32[32,1,128]{2,1,0:T(1,128)}), f32[32,1,128]{2,1,0:T(1,128)S(1)}, u32[]{:S(2)}, u32[]{:S(2)}) %all-to-all-start) | async-done | bytes 16416 | tf_op jit(solution)/shard_map/all_to_all | solution.py:435
  36.9 0.7 %stencil.1 = f32[3,18]{1,0:T(4,128)} custom-call(f32[32,128]{1,0:T(8,128)S(1)} %bitcast.10, f32[3,3,18]{2,1,0:T(4,128)S(1)} %copy-done.4, f32[3,3,18]{2,1,0:T(4,128)S(1)} %copy-done.3, f32[3,3,18]{2,1,0:T(4,128)S(1)} %copy-done.5), custom_call_target="tpu_custom_call" | custom-call | tf_op jit(solution)/shard_map/stencil/pallas_call | solution.py:436
  (16 shorter events, 0.0 us)
Async XLA Ops:
  0.6 10.3 %copy-start.1 = (f32[12,320]{1,0:T(8,128)S(1)}, f32[12,320]{1,0:T(8,128)}, u32[]{:S(2)}) copy-start(f32[12,320]{1,0:T(8,128)} %refs_1_.5) | copy-start | bytes 46084
  0.6 10.3 %copy-start.2 = (f32[12,320]{1,0:T(8,128)S(1)}, f32[12,320]{1,0:T(8,128)}, u32[]{:S(2)}) copy-start(f32[12,320]{1,0:T(8,128)} %refs_1_.6) | copy-start | bytes 46084
  0.6 10.3 %copy-start.8 = (s32[12,6]{0,1:T(8,128)S(1)}, s32[12,6]{0,1:T(8,128)}, u32[]{:S(2)}) copy-start(s32[12,6]{0,1:T(8,128)} %param.16) | copy-start | bytes 868
  6.4 8.1 %slice-start = ((s8[5898240]{0:T(1024)(128)(4,1)}), s8[4194304]{0:T(1024)(128)(4,1)S(1)}, s32[]{:S(2)}) async-start(s8[5898240]{0:T(1024)(128)(4,1)} %bitcast.7), calls=%async_computation.1 | async-start | bytes 8388608
  6.4 8.1 %collective-permute-start = (f32[16,320]{1,0:T(8,128)S(1)}, f32[16,320]{1,0:T(8,128)S(1)}, u32[]{:S(2)}, u32[]{:S(2)}) collective-permute-start(f32[16,320]{1,0:T(8,128)S(1)} %get-tuple-element.20.refs_4_), channel_id=1, source_target_pairs={{0,4},{4,0},{8,12},{12,8},{16,20},{20,16},{24,28},{28,24},{1,5},{5... | collective-permute-start | bytes 61448 | tf_op jit(solution)/shard_map/ppermute | solution.py:335
  7.0 7.5 %collective-permute-start.1 = (f32[16,320]{1,0:T(8,128)S(1)}, f32[16,320]{1,0:T(8,128)S(1)}, u32[]{:S(2)}, u32[]{:S(2)}) collective-permute-start(f32[16,320]{1,0:T(8,128)S(1)} %get-tuple-element.21.refs_5_), channel_id=1, source_target_pairs={{4,8},{8,4},{12,16},{16,12},{20,24},{24,20},{5,9},{9,5},{13,17},{1... | collective-permute-start | bytes 61448 | tf_op jit(solution)/shard_map/ppermute | solution.py:335
  9.6 4.9 %collective-permute-start.2 = (f32[16,320]{1,0:T(8,128)S(1)}, f32[16,320]{1,0:T(8,128)S(1)}, u32[]{:S(2)}, u32[]{:S(2)}) collective-permute-start(f32[16,320]{1,0:T(8,128)S(1)} %get-tuple-element.22.refs_6_), channel_id=1, source_target_pairs={{0,1},{1,0},{2,3},{3,2},{4,5},{5,4},{6,7},{7,6},{8,9},{9,8},{10,11... | collective-permute-start | bytes 61448 | tf_op jit(solution)/shard_map/ppermute | solution.py:335
  9.7 4.8 %collective-permute-start.3 = (f32[16,320]{1,0:T(8,128)S(1)}, f32[16,320]{1,0:T(8,128)S(1)}, u32[]{:S(2)}, u32[]{:S(2)}) collective-permute-start(f32[16,320]{1,0:T(8,128)S(1)} %get-tuple-element.23.refs_7_), channel_id=1, source_target_pairs={{1,2},{2,1},{5,6},{6,5},{9,10},{10,9},{13,14},{14,13},{17,18},{18,... | collective-permute-start | bytes 61448 | tf_op jit(solution)/shard_map/ppermute | solution.py:335
  11.0 3.6 %slice-start.1 = ((s8[5898240]{0:T(1024)(128)(4,1)}), s8[1703936]{0:T(1024)(128)(4,1)S(1)}, s32[]{:S(2)}) async-start(s8[5898240]{0:T(1024)(128)(4,1)} %bitcast.7), calls=%async_computation.2 | async-start | bytes 3407872
  14.5 7.5 %copy-start.3 = (f32[3,3,18]{2,1,0:T(4,128)S(1)}, f32[3,3,18]{2,1,0:T(4,128)}, u32[]{:S(2)}) copy-start(f32[3,3,18]{2,1,0:T(4,128)} %refs_2_.3) | copy-start | bytes 1948
  14.5 7.4 %copy-start.6 = (s32[12,8]{0,1:T(8,128)S(1)}, s32[12,8]{0,1:T(8,128)}, u32[]{:S(2)}) copy-start(s32[12,8]{0,1:T(8,128)} %param.17) | copy-start | bytes 1156
  14.5 7.4 %copy-start.7 = (s32[567]{0:T(1024)S(1)}, s32[567]{0:T(1024)}, u32[]{:S(2)}) copy-start(s32[567]{0:T(1024)} %refs_5_.1) | copy-start | bytes 6808
  14.6 9.9 %copy-start = (bf16[12,24,320]{2,1,0:T(8,128)(2,1)S(1)}, bf16[12,24,320]{2,1,0:T(8,128)(2,1)}, u32[]{:S(2)}) copy-start(bf16[12,24,320]{2,1,0:T(8,128)(2,1)} %param.15) | copy-start | bytes 552964
  14.6 22.3 %copy-start.4 = (f32[3,3,18]{2,1,0:T(4,128)S(1)}, f32[3,3,18]{2,1,0:T(4,128)}, u32[]{:S(2)}) copy-start(f32[3,3,18]{2,1,0:T(4,128)} %refs_1_.7) | copy-start | bytes 1948
  14.6 22.3 %copy-start.5 = (f32[3,3,18]{2,1,0:T(4,128)S(1)}, f32[3,3,18]{2,1,0:T(4,128)}, u32[]{:S(2)}) copy-start(f32[3,3,18]{2,1,0:T(4,128)} %refs_3_.1) | copy-start | bytes 1948
  17.7 5.8 %collective-permute-start.4 = (f32[16,320]{1,0:T(8,128)S(1)}, f32[16,320]{1,0:T(8,128)S(1)}, u32[]{:S(2)}, u32[]{:S(2)}) collective-permute-start(f32[16,320]{1,0:T(8,128)S(1)} %get-tuple-element.30.refs_7_), channel_id=1, source_target_pairs={{0,4},{4,0},{8,12},{12,8},{16,20},{20,16},{24,28},{28,24},{1,5},{5... | collective-permute-start | bytes 61448 | tf_op jit(solution)/shard_map/ppermute | solution.py:335
  17.7 5.7 %collective-permute-start.5 = (f32[16,320]{1,0:T(8,128)S(1)}, f32[16,320]{1,0:T(8,128)S(1)}, u32[]{:S(2)}, u32[]{:S(2)}) collective-permute-start(f32[16,320]{1,0:T(8,128)S(1)} %get-tuple-element.31.refs_8_), channel_id=1, source_target_pairs={{4,8},{8,4},{12,16},{16,12},{20,24},{24,20},{5,9},{9,5},{13,17},{1... | collective-permute-start | bytes 61448 | tf_op jit(solution)/shard_map/ppermute | solution.py:335
  20.6 3.8 %collective-permute-start.6 = (f32[16,320]{1,0:T(8,128)S(1)}, f32[16,320]{1,0:T(8,128)S(1)}, u32[]{:S(2)}, u32[]{:S(2)}) collective-permute-start(f32[16,320]{1,0:T(8,128)S(1)} %get-tuple-element.32.refs_9_), channel_id=1, source_target_pairs={{0,1},{1,0},{2,3},{3,2},{4,5},{5,4},{6,7},{7,6},{8,9},{9,8},{10,11... | collective-permute-start | bytes 61448 | tf_op jit(solution)/shard_map/ppermute | solution.py:335
  20.6 3.8 %collective-permute-start.7 = (f32[16,320]{1,0:T(8,128)S(1)}, f32[16,320]{1,0:T(8,128)S(1)}, u32[]{:S(2)}, u32[]{:S(2)}) collective-permute-start(f32[16,320]{1,0:T(8,128)S(1)} %get-tuple-element.33.refs_10_), channel_id=1, source_target_pairs={{1,2},{2,1},{5,6},{6,5},{9,10},{10,9},{13,14},{14,13},{17,18},{18,... | collective-permute-start | bytes 61448 | tf_op jit(solution)/shard_map/ppermute | solution.py:335
  26.4 10.5 %all-to-all-start = ((f32[32,1,128]{2,1,0:T(1,128)}), f32[32,1,128]{2,1,0:T(1,128)S(1)}, u32[]{:S(2)}, u32[]{:S(2)}) async-start(f32[32,1,128]{2,1,0:T(1,128)} %bitcast.4), calls=%async_computation | async-start | bytes 32768 | tf_op jit(solution)/shard_map/all_to_all | solution.py:435

commit v5 on v4

--- a/solution.py
+++ b/solution.py
@@ -10,8 +10,7 @@
 AXES = ("dom", "sub")
 PAIR = 2
 AHEAD = 4
-GAP_BYTES = 20_000_000
-UNROLL = 4
+UNROLL = 12
 ROWS = 16
 
 f32 = jnp.float32
@@ -204,27 +203,13 @@
     return rhs[...] - own[0:elem_count, :]
 
 
-def first_gap(elem_count, n_sub, offdiag, start, rhs, neighbor, send_0, send_1, send_2, send_3,
-              blocks, near, far, rest, faces, square, block_sem):
+def first_gap(elem_count, n_sub, node_count, offdiag, start, rhs, neighbor, corner, place, upper,
+              send_0, send_1, send_2, send_3, blocks, near, far, rest, table,
+              faces, square, block_sem):
     block_copy = block_copies(offdiag, 4, blocks, block_sem)
     start_copies(elem_count, block_copy)
     faces[...] = jnp.zeros(faces.shape, f32)
     near[...], far[...] = sum_choosers(elem_count, n_sub, neighbor[...], square)
-    streamed_faces(elem_count, start, block_copy, blocks, faces)
-    rest[...] = jnp.zeros(rest.shape, f32)
-    rest[0:elem_count, :] = local_rest(
-        elem_count, rhs, (send_0, send_1, send_2, send_3), faces, near
-    )
-
-
-def second_gap(elem_count, node_count, adj, rhs, near, blocks, corner, place, upper,
-               send_0, send_1, send_2, send_3, rest, table, faces):
-    faces[...] = jnp.zeros(faces.shape, f32)
-    grouped(elem_count, 4, lambda e: element_faces(e, adj, blocks, faces))
-    rest[...] = jnp.zeros(rest.shape, f32)
-    rest[0:elem_count, :] = local_rest(
-        elem_count, rhs, (send_0, send_1, send_2, send_3), faces, near
-    )
     table[...] = jnp.zeros(table.shape, f32)
     width = 3 * CORNERS * elem_count
     table[0:8, 0:width] = corner_lanes(elem_count, node_count, corner[...], place[...][None, :])
@@ -235,6 +220,20 @@
         column = upper[a][:, node_count - 1 : node_count]
         last = last + jnp.where(lane == base + 3 * a + row, column, 0.0)
     table[2:3, 0:128] = jnp.sum(last, axis=0, keepdims=True)
+    streamed_faces(elem_count, start, block_copy, blocks, faces)
+    rest[...] = jnp.zeros(rest.shape, f32)
+    rest[0:elem_count, :] = local_rest(
+        elem_count, rhs, (send_0, send_1, send_2, send_3), faces, near
+    )
+
+
+def second_gap(elem_count, adj, rhs, near, blocks, send_0, send_1, send_2, send_3, rest, faces):
+    faces[...] = jnp.zeros(faces.shape, f32)
+    grouped(elem_count, 12, lambda e: element_faces(e, adj, blocks, faces))
+    rest[...] = jnp.zeros(rest.shape, f32)
+    rest[0:elem_count, :] = local_rest(
+        elem_count, rhs, (send_0, send_1, send_2, send_3), faces, near
+    )
 
 
 def apply_inverse(elem_count, rest, arrived, far, inverse, rest_v, columns):
@@ -263,7 +262,7 @@
         elem_count, rest, (arr_0, arr_1, arr_2, arr_3), far, inverse, rest_v, columns
     )
     faces[...] = jnp.zeros(faces.shape, f32)
-    grouped(elem_count, 4, lambda e: element_faces(e, adj, blocks, faces))
+    grouped(elem_count, 12, lambda e: element_faces(e, adj, blocks, faces))
     fill_sends(faces, (send_0, send_1, send_2, send_3))
 
 
@@ -384,20 +383,24 @@
             name="first_sweep",
         )(in_hbm(adjoint_start), offdiag)
         arrived = exchange(sends)
-        more_blocks, near, far, rest = pl.pallas_call(
-            fixed(first_gap, elem_count, n_sub),
-            out_shape=(blocks_of(2), near, far, slab),
-            in_specs=[IN_HBM] + [IN_VMEM] * 7,
-            out_specs=(IN_VMEM,) * 4,
+        more_blocks, near, far, rest, table = pl.pallas_call(
+            fixed(first_gap, elem_count, n_sub, node_count),
+            out_shape=(
+                blocks_of(2), near, far, slab,
+                jax.ShapeDtypeStruct((8, up_to(width, 128)), f32),
+            ),
+            in_specs=[IN_HBM] + [IN_VMEM] * 10,
+            out_specs=(IN_VMEM,) * 5,
             scratch_shapes=[
                 faces_of(2), pltpu.VMEM((128, 128), i32), pltpu.SemaphoreType.DMA((copies,)),
             ],
             compiler_params=limit,
             cost_estimate=pl.CostEstimate(
-                flops=0, bytes_accessed=GAP_BYTES, transcendentals=0
+                flops=0, bytes_accessed=2 * elem_count * size * size * 2, transcendentals=0
             ),
             name="first_gap",
-        )(offdiag, adjoint_start, adjoint_rhs, neighbor.T, *sends)
+        )(offdiag, adjoint_start, adjoint_rhs, neighbor.T, corner_node.T, deform_place, stiff_upper,
+          *sends)
         *sends, adj = pl.pallas_call(
             fixed(next_sweep, elem_count),
             out_shape=(slab,) * 5,
@@ -408,23 +411,23 @@
             name="next_sweep",
         )(rest, *arrived, far, inverse, blocks)
         arrived = exchange(sends)
-        rest, table = pl.pallas_call(
-            fixed(second_gap, elem_count, node_count),
-            out_shape=(slab, jax.ShapeDtypeStruct((8, up_to(width, 128)), f32)),
-            in_specs=[IN_VMEM] * 11,
-            out_specs=(IN_VMEM,) * 2,
+        rest = pl.pallas_call(
+            fixed(second_gap, elem_count),
+            out_shape=slab,
+            in_specs=[IN_VMEM] * 8,
+            out_specs=IN_VMEM,
             scratch_shapes=[faces_of(2)],
             compiler_params=limit,
             cost_estimate=pl.CostEstimate(
-                flops=0, bytes_accessed=GAP_BYTES, transcendentals=0
+                flops=0, bytes_accessed=2 * elem_count * size * size * 2, transcendentals=0
             ),
             name="second_gap",
-        )(adj, adjoint_rhs, near, more_blocks, corner_node.T, deform_place, stiff_upper, *sends)
+        )(adj, adjoint_rhs, near, more_blocks, *sends)
         adjoint, by_owner = pl.pallas_call(
             fixed(last_sweep, elem_count, n_sub, n_dev, node_count),
             out_shape=(
-                pltpu.VMEM((elem_count, size), f32),
-                jax.ShapeDtypeStruct((n_dev, 128), f32),
+                jax.ShapeDtypeStruct((elem_count, size), f32),
+                pltpu.VMEM((n_dev, 128), f32),
             ),
             in_specs=[IN_VMEM] * 9,
             out_specs=(IN_VMEM,) * 2,

time: 37.8 us -> 36.6 us (0.968)
  blocking collectives: 0 us -> 10.3 us
  waiting for transfers between devices: 7.51 us -> 1.42 us
  starting transfers between devices: 12.1 us -> 8.75 us
  Pallas kernels: 16.6 us -> 15.1 us
  local copies, waits for them, and re-layouts: 0.67 us -> 0.06 us
    all_to_all x0 -> x1, blocking collectives: none -> 10.3 us  [on_device(): gathered = lax.all_to_all(by_owner, AXES, 0, 0, tiled=True)]
    all_to_all x1 -> x0, waiting for transfers between devices: 6.56 us -> none  [on_device(): gathered = lax.all_to_all(by_owner, AXES, 0, 0, tiled=True)]
    all_to_all x1 -> x0, starting transfers between devices: 3.32 us -> none  [on_device(): gathered = lax.all_to_all(by_owner, AXES, 0, 0, tiled=True)]
    unnamed x23 -> x22, local copies, waits for them, and re-layouts: 0.67 us -> 0.06 us
    pallas_call x1, Pallas kernels: 1.97 us -> 1.42 us  [on_device(): pl.pallas_call(fixed(last_sweep, elem_count, n_sub, n_dev, node_count), o...]
    pallas_call x1, Pallas kernels: 3.04 us -> 2.55 us  [on_device(): pl.pallas_call(fixed(next_sweep, elem_count), out_shape=(slab,) * 5, in_s...]
    ppermute x8, waiting for transfers between devices: 0.95 us -> 1.42 us  [exchange(): lax.ppermute(send, AXES, pairs)]
    pallas_call x2, Pallas kernels: 5.05 us -> 4.6 us  [the longest x1 3.51 us: on_device(): pl.pallas_call(fixed(first_gap, elem_count, n_sub, node_count), out_shape...]
  transfers between devices with their start and end apart: 9 -> 8, of which waited for: 2 -> 1; matrix products, arithmetic and copies ran while one was open for 2% -> 0% of each run, Pallas kernels for 13% -> 13%
where the time goes in v5:
time: 36.6 us; the launch traced here: 36.4 us
  Pallas kernels  15.1 us (41%)
  blocking collectives  10.3 us (28%)
  starting transfers between devices  8.75 us (24%)
  waiting for transfers between devices  1.42 us (4%)
  between operations  0.83 us (2%)
    all_to_all x1, blocking collectives, on_device(): gathered = lax.all_to_all(by_owner, AXES, 0, 0, tiled=True)  10.3 us
    ppermute x8, starting transfers between devices, exchange(): lax.ppermute(send, AXES, pairs)  8.75 us
    pallas_call x1, Pallas kernels, on_device(): pl.pallas_call(fixed(first_sweep, elem_count), out_shape=(slab, slab, sla...  5.77 us
    pallas_call x1, Pallas kernels, on_device(): pl.pallas_call(fixed(first_gap, elem_count, n_sub, node_count), out_shape...  3.51 us
    pallas_call x1, Pallas kernels, on_device(): pl.pallas_call(fixed(next_sweep, elem_count), out_shape=(slab,) * 5, in_s...  2.55 us
    pallas_call x1, Pallas kernels, on_device(): pl.pallas_call(fixed(last_sweep, elem_count, n_sub, n_dev, node_count), o...  1.42 us
    ppermute x8, waiting for transfers between devices, exchange(): lax.ppermute(send, AXES, pairs)  1.42 us
    pallas_call x1, Pallas kernels, on_device(): pl.pallas_call(fixed(second_gap, elem_count), out_shape=slab, in_specs=[I...  1.09 us
  transfers between devices with their start and end apart: 8, of which 1 were waited for; matrix products, arithmetic and copies ran while one was open for 0% of the time, Pallas kernels for 13%

profile of v5, /device:TPU:0, one launch (start us, length us, event | category | flops | bytes accessed | tf_op | source)
XLA Modules:
  0.0 36.4 jit_solution(13598087653810842587)
XLA Ops:
  0.6 0.0 copy-start.1
  0.7 5.8 %first_sweep.1 = (f32[16,320]{1,0:T(8,128)S(1)}, f32[16,320]{1,0:T(8,128)S(1)}, f32[16,320]{1,0:T(8,128)S(1)}, f32[16,320]{1,0:T(8,128)S(1)}, bf16[4,12,320,320]{3,2,1,0:T(8,128)(2,1)S(1)}) custom-call(f32[12,320]{1,0:T(8,128)} %refs_1_.5, bf16[6,12,320,320]{3,2,1,0:T(8,128)(2,1)} %refs_0_.3), custom_call_target="tpu_custom_call" | custom-call | tf_op jit(solution)/shard_map/first_sweep/pallas_call | solution.py:371
  6.5 0.0 slice-start
  6.5 0.5 %collective-permute-start = (f32[16,320]{1,0:T(8,128)S(1)}, f32[16,320]{1,0:T(8,128)S(1)}, u32[]{:S(2)}, u32[]{:S(2)}) collective-permute-start(f32[16,320]{1,0:T(8,128)S(1)} %get-tuple-element.19.refs_7_), channel_id=1, source_target_pairs={{0,4},{4,0},{8,12},{12,8},{16,20},{20,16},{24,28},{28,24},{1,5},{5... | collective-permute-start | bytes 61448 | tf_op jit(solution)/shard_map/ppermute | solution.py:334
  7.0 2.6 %collective-permute-start.1 = (f32[16,320]{1,0:T(8,128)S(1)}, f32[16,320]{1,0:T(8,128)S(1)}, u32[]{:S(2)}, u32[]{:S(2)}) collective-permute-start(f32[16,320]{1,0:T(8,128)S(1)} %get-tuple-element.20.refs_8_), channel_id=1, source_target_pairs={{4,8},{8,4},{12,16},{16,12},{20,24},{24,20},{5,9},{9,5},{13,17},{1... | collective-permute-start | bytes 61448 | tf_op jit(solution)/shard_map/ppermute | solution.py:334
  9.6 0.1 collective-permute-start.2
  9.7 1.2 %collective-permute-start.3 = (f32[16,320]{1,0:T(8,128)S(1)}, f32[16,320]{1,0:T(8,128)S(1)}, u32[]{:S(2)}, u32[]{:S(2)}) collective-permute-start(f32[16,320]{1,0:T(8,128)S(1)} %get-tuple-element.22.refs_10_), channel_id=1, source_target_pairs={{1,2},{2,1},{5,6},{6,5},{9,10},{10,9},{13,14},{14,13},{17,18},{18,... | collective-permute-start | bytes 61448 | tf_op jit(solution)/shard_map/ppermute | solution.py:334
  11.0 0.0 copy-done.1
  11.0 0.0 copy-done.7
  11.0 0.0 copy-done.6
  11.0 0.0 slice-start.1
  11.0 3.5 %first_gap.1 = (bf16[2,12,320,320]{3,2,1,0:T(8,128)(2,1)S(1)}, f32[16,96]{1,0:T(8,128)S(1)}, f32[16,64]{1,0:T(8,128)S(1)}, f32[16,320]{1,0:T(8,128)S(1)}, f32[8,384]{1,0:T(8,128)S(1)}) custom-call(bf16[6,12,320,320]{3,2,1,0:T(8,128)(2,1)} %refs_0_.3, f32[12,320]{1,0:T(8,128)S(1)} %copy-done.1, f32[12,320]{1,0:T(8,128)S(1)} %copy-done.2, ...), custom_call_target="tpu_custom_call" | custom-call | bytes 4915200 | tf_op jit(solution)/shard_map/first_gap/pallas_call | solution.py:386
  14.5 0.0 collective-permute-done.refs_1_
  14.5 0.0 collective-permute-done.1.refs_2_
  14.6 0.0 collective-permute-done.2.refs_3_
  14.6 0.0 collective-permute-done.3.refs_4_
  14.6 0.0 copy-start
  14.6 0.0 copy-start.4
  14.6 0.0 copy-start.5
  14.6 2.5 %next_sweep.1 = (f32[16,320]{1,0:T(8,128)S(1)}, f32[16,320]{1,0:T(8,128)S(1)}, f32[16,320]{1,0:T(8,128)S(1)}, f32[16,320]{1,0:T(8,128)S(1)}, f32[16,320]{1,0:T(8,128)S(1)}) custom-call(f32[16,320]{1,0:T(8,128)S(1)} %get-tuple-element.23.refs_0_, f32[16,320]{1,0:T(8,128)S(1)} %collective-permute-done.refs_1_, f32[16,320]{1,0:T(8,128)S(1)} %collective-permute-done.1.refs_2_, ...), custom_call_target="tpu_custom_call" | custom-call | tf_op jit(solution)/shard_map/next_sweep/pallas_call | solution.py:404
  17.2 0.1 collective-permute-start.4
  17.3 2.9 %collective-permute-start.5 = (f32[16,320]{1,0:T(8,128)S(1)}, f32[16,320]{1,0:T(8,128)S(1)}, u32[]{:S(2)}, u32[]{:S(2)}) collective-permute-start(f32[16,320]{1,0:T(8,128)S(1)} %get-tuple-element.30.refs_5_), channel_id=1, source_target_pairs={{4,8},{8,4},{12,16},{16,12},{20,24},{24,20},{5,9},{9,5},{13,17},{1... | collective-permute-start | bytes 61448 | tf_op jit(solution)/shard_map/ppermute | solution.py:334
  20.1 0.0 collective-permute-start.6
  20.2 1.3 %collective-permute-start.7 = (f32[16,320]{1,0:T(8,128)S(1)}, f32[16,320]{1,0:T(8,128)S(1)}, u32[]{:S(2)}, u32[]{:S(2)}) collective-permute-start(f32[16,320]{1,0:T(8,128)S(1)} %get-tuple-element.32.refs_7_), channel_id=1, source_target_pairs={{1,2},{2,1},{5,6},{6,5},{9,10},{10,9},{13,14},{14,13},{17,18},{18,... | collective-permute-start | bytes 61448 | tf_op jit(solution)/shard_map/ppermute | solution.py:334
  21.4 1.1 %second_gap.1.refs_0_ = f32[16,320]{1,0:T(8,128)S(1)} custom-call(f32[16,320]{1,0:T(8,128)S(1)} %get-tuple-element.26.refs_0_, f32[12,320]{1,0:T(8,128)S(1)} %copy-done.2, f32[16,96]{1,0:T(8,128)S(1)} %get-tuple-element.27.refs_2_, bf16[2,12,320,320]{3,2,1,0:T(8,128)(2,1)S(1)} %get-tuple-element.28.refs_3_, f32[16,320]{1,0:T(8,128)S(1)} %get-tuple-element.29.refs_4_, ...), custom_call_target="tpu_custom_call" | custom-call | bytes 4915200 | tf_op jit(solution)/shard_map/second_gap/pallas_call | solution.py:414
  22.5 0.0 collective-permute-done.4.refs_1_
  22.5 0.0 collective-permute-done.5.refs_2_
  22.6 1.4 %collective-permute-done.6.refs_3_ = f32[16,320]{1,0:T(8,128)S(1)} collective-permute-done((f32[16,320]{1,0:T(8,128)S(1)}, f32[16,320]{1,0:T(8,128)S(1)}, u32[]{:S(2)}, u32[]{:S(2)}) %collective-permute-start.6) | collective-permute-done | bytes 20512 | tf_op jit(solution)/shard_map/ppermute | solution.py:334
  23.9 0.0 collective-permute-done.7.refs_4_
  24.0 1.4 %last_sweep.1 = (f32[12,320]{1,0:T(8,128)}, f32[32,128]{1,0:T(8,128)S(1)}) custom-call(f32[16,320]{1,0:T(8,128)S(1)} %second_gap.1.refs_0_, f32[16,320]{1,0:T(8,128)S(1)} %collective-permute-done.4.refs_1_, f32[16,320]{1,0:T(8,128)S(1)} %collective-permute-done.5.refs_2_, f32[16,320]{1,0:T(8,128)S(1)} %collective-permute-done.6.refs_3_, ...), custom_call_target="tpu_custom_call" | custom-call | tf_op jit(solution)/shard_map/last_sweep/pallas_call | solution.py:426
  25.4 10.3 %all_to_all.11 = f32[32,1,128]{2,1,0:T(1,128)S(1)} all-to-all(f32[32,1,128]{2,1,0:T(1,128)S(1)} %bitcast.11), channel_id=1, replica_groups=mesh['dom'=8,'sub'=4] {'dom','sub'}, dimensions={0} | all-to-all | bytes 32768 | tf_op jit(solution)/shard_map/all_to_all | solution.py:438
  35.7 0.7 %stencil.1 = f32[3,18]{1,0:T(4,128)} custom-call(f32[32,128]{1,0:T(8,128)S(1)} %bitcast.10, f32[3,3,18]{2,1,0:T(4,128)S(1)} %copy-done.4, f32[3,3,18]{2,1,0:T(4,128)S(1)} %copy-done.3, f32[3,3,18]{2,1,0:T(4,128)S(1)} %copy-done.5), custom_call_target="tpu_custom_call" | custom-call | tf_op jit(solution)/shard_map/stencil/pallas_call | solution.py:439
  (14 shorter events, 0.0 us)
Async XLA Ops:
  0.6 10.3 %copy-start.1 = (f32[12,320]{1,0:T(8,128)S(1)}, f32[12,320]{1,0:T(8,128)}, u32[]{:S(2)}) copy-start(f32[12,320]{1,0:T(8,128)} %refs_1_.5) | copy-start | bytes 46084
  0.6 10.3 %copy-start.3 = (f32[3,3,18]{2,1,0:T(4,128)S(1)}, f32[3,3,18]{2,1,0:T(4,128)}, u32[]{:S(2)}) copy-start(f32[3,3,18]{2,1,0:T(4,128)} %refs_2_.3) | copy-start | bytes 1948
  0.7 10.3 %copy-start.2 = (f32[12,320]{1,0:T(8,128)S(1)}, f32[12,320]{1,0:T(8,128)}, u32[]{:S(2)}) copy-start(f32[12,320]{1,0:T(8,128)} %refs_1_.6) | copy-start | bytes 46084
  0.7 10.3 %copy-start.8 = (s32[567]{0:T(1024)S(1)}, s32[567]{0:T(1024)}, u32[]{:S(2)}) copy-start(s32[567]{0:T(1024)} %refs_5_.1) | copy-start | bytes 6808
  0.7 10.3 %copy-start.7 = (s32[12,8]{0,1:T(8,128)S(1)}, s32[12,8]{0,1:T(8,128)}, u32[]{:S(2)}) copy-start(s32[12,8]{0,1:T(8,128)} %param.17) | copy-start | bytes 1156
  0.7 10.3 %copy-start.6 = (s32[12,6]{0,1:T(8,128)S(1)}, s32[12,6]{0,1:T(8,128)}, u32[]{:S(2)}) copy-start(s32[12,6]{0,1:T(8,128)} %param.16) | copy-start | bytes 868
  6.5 8.1 %slice-start = ((s8[5898240]{0:T(1024)(128)(4,1)}), s8[4194304]{0:T(1024)(128)(4,1)S(1)}, s32[]{:S(2)}) async-start(s8[5898240]{0:T(1024)(128)(4,1)} %bitcast.7), calls=%async_computation.1 | async-start | bytes 8388608
  6.5 8.1 %collective-permute-start = (f32[16,320]{1,0:T(8,128)S(1)}, f32[16,320]{1,0:T(8,128)S(1)}, u32[]{:S(2)}, u32[]{:S(2)}) collective-permute-start(f32[16,320]{1,0:T(8,128)S(1)} %get-tuple-element.19.refs_7_), channel_id=1, source_target_pairs={{0,4},{4,0},{8,12},{12,8},{16,20},{20,16},{24,28},{28,24},{1,5},{5... | collective-permute-start | bytes 61448 | tf_op jit(solution)/shard_map/ppermute | solution.py:334
  7.0 7.5 %collective-permute-start.1 = (f32[16,320]{1,0:T(8,128)S(1)}, f32[16,320]{1,0:T(8,128)S(1)}, u32[]{:S(2)}, u32[]{:S(2)}) collective-permute-start(f32[16,320]{1,0:T(8,128)S(1)} %get-tuple-element.20.refs_8_), channel_id=1, source_target_pairs={{4,8},{8,4},{12,16},{16,12},{20,24},{24,20},{5,9},{9,5},{13,17},{1... | collective-permute-start | bytes 61448 | tf_op jit(solution)/shard_map/ppermute | solution.py:334
  9.6 4.9 %collective-permute-start.2 = (f32[16,320]{1,0:T(8,128)S(1)}, f32[16,320]{1,0:T(8,128)S(1)}, u32[]{:S(2)}, u32[]{:S(2)}) collective-permute-start(f32[16,320]{1,0:T(8,128)S(1)} %get-tuple-element.21.refs_9_), channel_id=1, source_target_pairs={{0,1},{1,0},{2,3},{3,2},{4,5},{5,4},{6,7},{7,6},{8,9},{9,8},{10,11... | collective-permute-start | bytes 61448 | tf_op jit(solution)/shard_map/ppermute | solution.py:334
  9.7 4.8 %collective-permute-start.3 = (f32[16,320]{1,0:T(8,128)S(1)}, f32[16,320]{1,0:T(8,128)S(1)}, u32[]{:S(2)}, u32[]{:S(2)}) collective-permute-start(f32[16,320]{1,0:T(8,128)S(1)} %get-tuple-element.22.refs_10_), channel_id=1, source_target_pairs={{1,2},{2,1},{5,6},{6,5},{9,10},{10,9},{13,14},{14,13},{17,18},{18,... | collective-permute-start | bytes 61448 | tf_op jit(solution)/shard_map/ppermute | solution.py:334
  11.0 3.6 %slice-start.1 = ((s8[5898240]{0:T(1024)(128)(4,1)}), s8[1703936]{0:T(1024)(128)(4,1)S(1)}, s32[]{:S(2)}) async-start(s8[5898240]{0:T(1024)(128)(4,1)} %bitcast.7), calls=%async_computation.2 | async-start | bytes 3407872
  14.6 9.4 %copy-start = (bf16[12,24,320]{2,1,0:T(8,128)(2,1)S(1)}, bf16[12,24,320]{2,1,0:T(8,128)(2,1)}, u32[]{:S(2)}) copy-start(bf16[12,24,320]{2,1,0:T(8,128)(2,1)} %param.15) | copy-start | bytes 552964
  14.6 21.0 %copy-start.4 = (f32[3,3,18]{2,1,0:T(4,128)S(1)}, f32[3,3,18]{2,1,0:T(4,128)}, u32[]{:S(2)}) copy-start(f32[3,3,18]{2,1,0:T(4,128)} %refs_1_.7) | copy-start | bytes 1948
  14.6 21.0 %copy-start.5 = (f32[3,3,18]{2,1,0:T(4,128)S(1)}, f32[3,3,18]{2,1,0:T(4,128)}, u32[]{:S(2)}) copy-start(f32[3,3,18]{2,1,0:T(4,128)} %refs_3_.1) | copy-start | bytes 1948
  17.2 5.4 %collective-permute-start.4 = (f32[16,320]{1,0:T(8,128)S(1)}, f32[16,320]{1,0:T(8,128)S(1)}, u32[]{:S(2)}, u32[]{:S(2)}) collective-permute-start(f32[16,320]{1,0:T(8,128)S(1)} %get-tuple-element.29.refs_4_), channel_id=1, source_target_pairs={{0,4},{4,0},{8,12},{12,8},{16,20},{20,16},{24,28},{28,24},{1,5},{5... | collective-permute-start | bytes 61448 | tf_op jit(solution)/shard_map/ppermute | solution.py:334
  17.3 5.3 %collective-permute-start.5 = (f32[16,320]{1,0:T(8,128)S(1)}, f32[16,320]{1,0:T(8,128)S(1)}, u32[]{:S(2)}, u32[]{:S(2)}) collective-permute-start(f32[16,320]{1,0:T(8,128)S(1)} %get-tuple-element.30.refs_5_), channel_id=1, source_target_pairs={{4,8},{8,4},{12,16},{16,12},{20,24},{24,20},{5,9},{9,5},{13,17},{1... | collective-permute-start | bytes 61448 | tf_op jit(solution)/shard_map/ppermute | solution.py:334
  20.1 3.8 %collective-permute-start.6 = (f32[16,320]{1,0:T(8,128)S(1)}, f32[16,320]{1,0:T(8,128)S(1)}, u32[]{:S(2)}, u32[]{:S(2)}) collective-permute-start(f32[16,320]{1,0:T(8,128)S(1)} %get-tuple-element.31.refs_6_), channel_id=1, source_target_pairs={{0,1},{1,0},{2,3},{3,2},{4,5},{5,4},{6,7},{7,6},{8,9},{9,8},{10,11... | collective-permute-start | bytes 61448 | tf_op jit(solution)/shard_map/ppermute | solution.py:334
  20.2 3.8 %collective-permute-start.7 = (f32[16,320]{1,0:T(8,128)S(1)}, f32[16,320]{1,0:T(8,128)S(1)}, u32[]{:S(2)}, u32[]{:S(2)}) collective-permute-start(f32[16,320]{1,0:T(8,128)S(1)} %get-tuple-element.32.refs_7_), channel_id=1, source_target_pairs={{1,2},{2,1},{5,6},{6,5},{9,10},{10,9},{13,14},{14,13},{17,18},{18,... | collective-permute-start | bytes 61448 | tf_op jit(solution)/shard_map/ppermute | solution.py:334

commit v6 on v5

--- a/solution.py
+++ b/solution.py
@@ -9,7 +9,8 @@
 CORNERS = 8
 AXES = ("dom", "sub")
 PAIR = 2
-AHEAD = 4
+SWEEP_AHEAD = 4
+GAP_AHEAD = 6
 UNROLL = 12
 ROWS = 16
 
@@ -165,18 +166,18 @@
     return copy
 
 
-def start_copies(elem_count, block_copy):
-    for index in range(min(AHEAD, elem_count // PAIR)):
+def start_copies(elem_count, block_copy, ahead):
+    for index in range(min(ahead, elem_count // PAIR)):
         block_copy(index).start()
 
 
-def streamed_faces(elem_count, adj_rows, block_copy, blocks, faces):
+def streamed_faces(elem_count, adj_rows, block_copy, blocks, faces, ahead):
     def step(index, _):
         block_copy(index).wait()
 
-        @pl.when(index + AHEAD < elem_count // PAIR)
+        @pl.when(index + ahead < elem_count // PAIR)
         def _():
-            block_copy(index + AHEAD).start()
+            block_copy(index + ahead).start()
 
         for offset in range(PAIR):
             element_faces(index * PAIR + offset, adj_rows, blocks, faces)
@@ -190,10 +191,10 @@
     start_copy = pltpu.make_async_copy(start, start_v, start_sem)
     block_copy = block_copies(offdiag, 0, blocks, block_sem)
     start_copy.start()
-    start_copies(elem_count, block_copy)
+    start_copies(elem_count, block_copy, SWEEP_AHEAD)
     faces[...] = jnp.zeros(faces.shape, f32)
     start_copy.wait()
-    streamed_faces(elem_count, start_v, block_copy, blocks, faces)
+    streamed_faces(elem_count, start_v, block_copy, blocks, faces, SWEEP_AHEAD)
     fill_sends(faces, (send_0, send_1, send_2, send_3))
 
 
@@ -207,7 +208,7 @@
               send_0, send_1, send_2, send_3, blocks, near, far, rest, table,
               faces, square, block_sem):
     block_copy = block_copies(offdiag, 4, blocks, block_sem)
-    start_copies(elem_count, block_copy)
+    start_copies(elem_count, block_copy, GAP_AHEAD)
     faces[...] = jnp.zeros(faces.shape, f32)
     near[...], far[...] = sum_choosers(elem_count, n_sub, neighbor[...], square)
     table[...] = jnp.zeros(table.shape, f32)
@@ -220,7 +221,7 @@
         column = upper[a][:, node_count - 1 : node_count]
         last = last + jnp.where(lane == base + 3 * a + row, column, 0.0)
     table[2:3, 0:128] = jnp.sum(last, axis=0, keepdims=True)
-    streamed_faces(elem_count, start, block_copy, blocks, faces)
+    streamed_faces(elem_count, start, block_copy, blocks, faces, GAP_AHEAD)
     rest[...] = jnp.zeros(rest.shape, f32)
     rest[0:elem_count, :] = local_rest(
         elem_count, rhs, (send_0, send_1, send_2, send_3), faces, near

time: 36.6 us -> 36.4 us (level)
  transfers between devices with their start and end apart: 8 -> 8, of which waited for: 1 -> 1; matrix products, arithmetic and copies ran while one was open for 0% -> 0% of each run, Pallas kernels for 13% -> 12%
where the time goes in v6:
time: 36.4 us; the launch traced here: 36.2 us
  Pallas kernels  14.9 us (41%)
  blocking collectives  10.3 us (28%)
  starting transfers between devices  8.76 us (24%)
  waiting for transfers between devices  1.42 us (4%)
  between operations  0.83 us (2%)
    all_to_all x1, blocking collectives, on_device(): gathered = lax.all_to_all(by_owner, AXES, 0, 0, tiled=True)  10.3 us
    ppermute x8, starting transfers between devices, exchange(): lax.ppermute(send, AXES, pairs)  8.76 us
    pallas_call x1, Pallas kernels, on_device(): pl.pallas_call(fixed(first_sweep, elem_count), out_shape=(slab, slab, sla...  5.77 us
    pallas_call x1, Pallas kernels, on_device(): pl.pallas_call(fixed(first_gap, elem_count, n_sub, node_count), out_shape...  3.32 us
    pallas_call x1, Pallas kernels, on_device(): pl.pallas_call(fixed(next_sweep, elem_count), out_shape=(slab,) * 5, in_s...  2.55 us
    pallas_call x1, Pallas kernels, on_device(): pl.pallas_call(fixed(last_sweep, elem_count, n_sub, n_dev, node_count), o...  1.42 us
    ppermute x8, waiting for transfers between devices, exchange(): lax.ppermute(send, AXES, pairs)  1.42 us
    pallas_call x1, Pallas kernels, on_device(): pl.pallas_call(fixed(second_gap, elem_count), out_shape=slab, in_specs=[I...  1.09 us
  transfers between devices with their start and end apart: 8, of which 1 were waited for; matrix products, arithmetic and copies ran while one was open for 0% of the time, Pallas kernels for 12%

profile of v6, /device:TPU:0, one launch (start us, length us, event | category | flops | bytes accessed | tf_op | source)
XLA Modules:
  0.0 36.2 jit_solution(7003891510243320182)
XLA Ops:
  0.7 5.8 %first_sweep.1 = (f32[16,320]{1,0:T(8,128)S(1)}, f32[16,320]{1,0:T(8,128)S(1)}, f32[16,320]{1,0:T(8,128)S(1)}, f32[16,320]{1,0:T(8,128)S(1)}, bf16[4,12,320,320]{3,2,1,0:T(8,128)(2,1)S(1)}) custom-call(f32[12,320]{1,0:T(8,128)} %refs_1_.5, bf16[6,12,320,320]{3,2,1,0:T(8,128)(2,1)} %refs_0_.3), custom_call_target="tpu_custom_call" | custom-call | tf_op jit(solution)/shard_map/first_sweep/pallas_call | solution.py:372
  6.5 0.0 slice-start
  6.5 0.5 %collective-permute-start = (f32[16,320]{1,0:T(8,128)S(1)}, f32[16,320]{1,0:T(8,128)S(1)}, u32[]{:S(2)}, u32[]{:S(2)}) collective-permute-start(f32[16,320]{1,0:T(8,128)S(1)} %get-tuple-element.19.refs_7_), channel_id=1, source_target_pairs={{0,4},{4,0},{8,12},{12,8},{16,20},{20,16},{24,28},{28,24},{1,5},{5... | collective-permute-start | bytes 61448 | tf_op jit(solution)/shard_map/ppermute | solution.py:335
  7.0 2.6 %collective-permute-start.1 = (f32[16,320]{1,0:T(8,128)S(1)}, f32[16,320]{1,0:T(8,128)S(1)}, u32[]{:S(2)}, u32[]{:S(2)}) collective-permute-start(f32[16,320]{1,0:T(8,128)S(1)} %get-tuple-element.20.refs_8_), channel_id=1, source_target_pairs={{4,8},{8,4},{12,16},{16,12},{20,24},{24,20},{5,9},{9,5},{13,17},{1... | collective-permute-start | bytes 61448 | tf_op jit(solution)/shard_map/ppermute | solution.py:335
  9.6 0.1 collective-permute-start.2
  9.7 1.2 %collective-permute-start.3 = (f32[16,320]{1,0:T(8,128)S(1)}, f32[16,320]{1,0:T(8,128)S(1)}, u32[]{:S(2)}, u32[]{:S(2)}) collective-permute-start(f32[16,320]{1,0:T(8,128)S(1)} %get-tuple-element.22.refs_10_), channel_id=1, source_target_pairs={{1,2},{2,1},{5,6},{6,5},{9,10},{10,9},{13,14},{14,13},{17,18},{18,... | collective-permute-start | bytes 61448 | tf_op jit(solution)/shard_map/ppermute | solution.py:335
  11.0 0.0 copy-done.1
  11.0 0.0 copy-done.7
  11.0 0.0 copy-done.6
  11.0 0.0 slice-start.1
  11.0 3.3 %first_gap.1 = (bf16[2,12,320,320]{3,2,1,0:T(8,128)(2,1)S(1)}, f32[16,96]{1,0:T(8,128)S(1)}, f32[16,64]{1,0:T(8,128)S(1)}, f32[16,320]{1,0:T(8,128)S(1)}, f32[8,384]{1,0:T(8,128)S(1)}) custom-call(bf16[6,12,320,320]{3,2,1,0:T(8,128)(2,1)} %refs_0_.3, f32[12,320]{1,0:T(8,128)S(1)} %copy-done.1, f32[12,320]{1,0:T(8,128)S(1)} %copy-done.2, ...), custom_call_target="tpu_custom_call" | custom-call | bytes 4915200 | tf_op jit(solution)/shard_map/first_gap/pallas_call | solution.py:387
  14.4 0.0 collective-permute-done.refs_1_
  14.4 0.0 collective-permute-done.1.refs_2_
  14.4 0.0 collective-permute-done.2.refs_3_
  14.4 0.0 collective-permute-done.3.refs_4_
  14.4 0.0 slice-done
  14.4 0.0 copy-start
  14.4 0.0 copy-start.4
  14.4 0.0 copy-start.5
  14.5 2.5 %next_sweep.1 = (f32[16,320]{1,0:T(8,128)S(1)}, f32[16,320]{1,0:T(8,128)S(1)}, f32[16,320]{1,0:T(8,128)S(1)}, f32[16,320]{1,0:T(8,128)S(1)}, f32[16,320]{1,0:T(8,128)S(1)}) custom-call(f32[16,320]{1,0:T(8,128)S(1)} %get-tuple-element.23.refs_0_, f32[16,320]{1,0:T(8,128)S(1)} %collective-permute-done.refs_1_, f32[16,320]{1,0:T(8,128)S(1)} %collective-permute-done.1.refs_2_, ...), custom_call_target="tpu_custom_call" | custom-call | tf_op jit(solution)/shard_map/next_sweep/pallas_call | solution.py:405
  17.0 0.1 collective-permute-start.4
  17.1 2.9 %collective-permute-start.5 = (f32[16,320]{1,0:T(8,128)S(1)}, f32[16,320]{1,0:T(8,128)S(1)}, u32[]{:S(2)}, u32[]{:S(2)}) collective-permute-start(f32[16,320]{1,0:T(8,128)S(1)} %get-tuple-element.30.refs_5_), channel_id=1, source_target_pairs={{4,8},{8,4},{12,16},{16,12},{20,24},{24,20},{5,9},{9,5},{13,17},{1... | collective-permute-start | bytes 61448 | tf_op jit(solution)/shard_map/ppermute | solution.py:335
  19.9 0.0 collective-permute-start.6
  20.0 1.3 %collective-permute-start.7 = (f32[16,320]{1,0:T(8,128)S(1)}, f32[16,320]{1,0:T(8,128)S(1)}, u32[]{:S(2)}, u32[]{:S(2)}) collective-permute-start(f32[16,320]{1,0:T(8,128)S(1)} %get-tuple-element.32.refs_7_), channel_id=1, source_target_pairs={{1,2},{2,1},{5,6},{6,5},{9,10},{10,9},{13,14},{14,13},{17,18},{18,... | collective-permute-start | bytes 61448 | tf_op jit(solution)/shard_map/ppermute | solution.py:335
  21.3 1.1 %second_gap.1.refs_0_ = f32[16,320]{1,0:T(8,128)S(1)} custom-call(f32[16,320]{1,0:T(8,128)S(1)} %get-tuple-element.26.refs_0_, f32[12,320]{1,0:T(8,128)S(1)} %copy-done.2, f32[16,96]{1,0:T(8,128)S(1)} %get-tuple-element.27.refs_2_, bf16[2,12,320,320]{3,2,1,0:T(8,128)(2,1)S(1)} %get-tuple-element.28.refs_3_, f32[16,320]{1,0:T(8,128)S(1)} %get-tuple-element.29.refs_4_, ...), custom_call_target="tpu_custom_call" | custom-call | bytes 4915200 | tf_op jit(solution)/shard_map/second_gap/pallas_call | solution.py:415
  22.4 0.0 collective-permute-done.4.refs_1_
  22.4 0.0 collective-permute-done.5.refs_2_
  22.4 1.4 %collective-permute-done.6.refs_3_ = f32[16,320]{1,0:T(8,128)S(1)} collective-permute-done((f32[16,320]{1,0:T(8,128)S(1)}, f32[16,320]{1,0:T(8,128)S(1)}, u32[]{:S(2)}, u32[]{:S(2)}) %collective-permute-start.6) | collective-permute-done | bytes 20512 | tf_op jit(solution)/shard_map/ppermute | solution.py:335
  23.8 0.0 collective-permute-done.7.refs_4_
  23.8 1.4 %last_sweep.1 = (f32[12,320]{1,0:T(8,128)}, f32[32,128]{1,0:T(8,128)S(1)}) custom-call(f32[16,320]{1,0:T(8,128)S(1)} %second_gap.1.refs_0_, f32[16,320]{1,0:T(8,128)S(1)} %collective-permute-done.4.refs_1_, f32[16,320]{1,0:T(8,128)S(1)} %collective-permute-done.5.refs_2_, f32[16,320]{1,0:T(8,128)S(1)} %collective-permute-done.6.refs_3_, ...), custom_call_target="tpu_custom_call" | custom-call | tf_op jit(solution)/shard_map/last_sweep/pallas_call | solution.py:427
  25.2 10.3 %all_to_all.11 = f32[32,1,128]{2,1,0:T(1,128)S(1)} all-to-all(f32[32,1,128]{2,1,0:T(1,128)S(1)} %bitcast.11), channel_id=1, replica_groups=mesh['dom'=8,'sub'=4] {'dom','sub'}, dimensions={0} | all-to-all | bytes 32768 | tf_op jit(solution)/shard_map/all_to_all | solution.py:439
  35.5 0.7 %stencil.1 = f32[3,18]{1,0:T(4,128)} custom-call(f32[32,128]{1,0:T(8,128)S(1)} %bitcast.10, f32[3,3,18]{2,1,0:T(4,128)S(1)} %copy-done.4, f32[3,3,18]{2,1,0:T(4,128)S(1)} %copy-done.3, f32[3,3,18]{2,1,0:T(4,128)S(1)} %copy-done.5), custom_call_target="tpu_custom_call" | custom-call | tf_op jit(solution)/shard_map/stencil/pallas_call | solution.py:440
  (14 shorter events, 0.0 us)
Async XLA Ops:
  0.6 10.3 %copy-start.1 = (f32[12,320]{1,0:T(8,128)S(1)}, f32[12,320]{1,0:T(8,128)}, u32[]{:S(2)}) copy-start(f32[12,320]{1,0:T(8,128)} %refs_1_.5) | copy-start | bytes 46084
  0.6 10.3 %copy-start.3 = (f32[3,3,18]{2,1,0:T(4,128)S(1)}, f32[3,3,18]{2,1,0:T(4,128)}, u32[]{:S(2)}) copy-start(f32[3,3,18]{2,1,0:T(4,128)} %refs_2_.3) | copy-start | bytes 1948
  0.7 10.3 %copy-start.2 = (f32[12,320]{1,0:T(8,128)S(1)}, f32[12,320]{1,0:T(8,128)}, u32[]{:S(2)}) copy-start(f32[12,320]{1,0:T(8,128)} %refs_1_.6) | copy-start | bytes 46084
  0.7 10.3 %copy-start.8 = (s32[567]{0:T(1024)S(1)}, s32[567]{0:T(1024)}, u32[]{:S(2)}) copy-start(s32[567]{0:T(1024)} %refs_5_.1) | copy-start | bytes 6808
  0.7 10.3 %copy-start.7 = (s32[12,8]{0,1:T(8,128)S(1)}, s32[12,8]{0,1:T(8,128)}, u32[]{:S(2)}) copy-start(s32[12,8]{0,1:T(8,128)} %param.17) | copy-start | bytes 1156
  0.7 10.3 %copy-start.6 = (s32[12,6]{0,1:T(8,128)S(1)}, s32[12,6]{0,1:T(8,128)}, u32[]{:S(2)}) copy-start(s32[12,6]{0,1:T(8,128)} %param.16) | copy-start | bytes 868
  6.5 7.9 %slice-start = ((s8[5898240]{0:T(1024)(128)(4,1)}), s8[4194304]{0:T(1024)(128)(4,1)S(1)}, s32[]{:S(2)}) async-start(s8[5898240]{0:T(1024)(128)(4,1)} %bitcast.7), calls=%async_computation.1 | async-start | bytes 8388608
  6.5 7.9 %collective-permute-start = (f32[16,320]{1,0:T(8,128)S(1)}, f32[16,320]{1,0:T(8,128)S(1)}, u32[]{:S(2)}, u32[]{:S(2)}) collective-permute-start(f32[16,320]{1,0:T(8,128)S(1)} %get-tuple-element.19.refs_7_), channel_id=1, source_target_pairs={{0,4},{4,0},{8,12},{12,8},{16,20},{20,16},{24,28},{28,24},{1,5},{5... | collective-permute-start | bytes 61448 | tf_op jit(solution)/shard_map/ppermute | solution.py:335
  7.0 7.4 %collective-permute-start.1 = (f32[16,320]{1,0:T(8,128)S(1)}, f32[16,320]{1,0:T(8,128)S(1)}, u32[]{:S(2)}, u32[]{:S(2)}) collective-permute-start(f32[16,320]{1,0:T(8,128)S(1)} %get-tuple-element.20.refs_8_), channel_id=1, source_target_pairs={{4,8},{8,4},{12,16},{16,12},{20,24},{24,20},{5,9},{9,5},{13,17},{1... | collective-permute-start | bytes 61448 | tf_op jit(solution)/shard_map/ppermute | solution.py:335
  9.6 4.7 %collective-permute-start.2 = (f32[16,320]{1,0:T(8,128)S(1)}, f32[16,320]{1,0:T(8,128)S(1)}, u32[]{:S(2)}, u32[]{:S(2)}) collective-permute-start(f32[16,320]{1,0:T(8,128)S(1)} %get-tuple-element.21.refs_9_), channel_id=1, source_target_pairs={{0,1},{1,0},{2,3},{3,2},{4,5},{5,4},{6,7},{7,6},{8,9},{9,8},{10,11... | collective-permute-start | bytes 61448 | tf_op jit(solution)/shard_map/ppermute | solution.py:335
  9.7 4.7 %collective-permute-start.3 = (f32[16,320]{1,0:T(8,128)S(1)}, f32[16,320]{1,0:T(8,128)S(1)}, u32[]{:S(2)}, u32[]{:S(2)}) collective-permute-start(f32[16,320]{1,0:T(8,128)S(1)} %get-tuple-element.22.refs_10_), channel_id=1, source_target_pairs={{1,2},{2,1},{5,6},{6,5},{9,10},{10,9},{13,14},{14,13},{17,18},{18,... | collective-permute-start | bytes 61448 | tf_op jit(solution)/shard_map/ppermute | solution.py:335
  11.0 3.4 %slice-start.1 = ((s8[5898240]{0:T(1024)(128)(4,1)}), s8[1703936]{0:T(1024)(128)(4,1)S(1)}, s32[]{:S(2)}) async-start(s8[5898240]{0:T(1024)(128)(4,1)} %bitcast.7), calls=%async_computation.2 | async-start | bytes 3407872
  14.4 9.4 %copy-start = (bf16[12,24,320]{2,1,0:T(8,128)(2,1)S(1)}, bf16[12,24,320]{2,1,0:T(8,128)(2,1)}, u32[]{:S(2)}) copy-start(bf16[12,24,320]{2,1,0:T(8,128)(2,1)} %param.15) | copy-start | bytes 552964
  14.4 21.1 %copy-start.4 = (f32[3,3,18]{2,1,0:T(4,128)S(1)}, f32[3,3,18]{2,1,0:T(4,128)}, u32[]{:S(2)}) copy-start(f32[3,3,18]{2,1,0:T(4,128)} %refs_1_.7) | copy-start | bytes 1948
  14.4 21.0 %copy-start.5 = (f32[3,3,18]{2,1,0:T(4,128)S(1)}, f32[3,3,18]{2,1,0:T(4,128)}, u32[]{:S(2)}) copy-start(f32[3,3,18]{2,1,0:T(4,128)} %refs_3_.1) | copy-start | bytes 1948
  17.0 5.4 %collective-permute-start.4 = (f32[16,320]{1,0:T(8,128)S(1)}, f32[16,320]{1,0:T(8,128)S(1)}, u32[]{:S(2)}, u32[]{:S(2)}) collective-permute-start(f32[16,320]{1,0:T(8,128)S(1)} %get-tuple-element.29.refs_4_), channel_id=1, source_target_pairs={{0,4},{4,0},{8,12},{12,8},{16,20},{20,16},{24,28},{28,24},{1,5},{5... | collective-permute-start | bytes 61448 | tf_op jit(solution)/shard_map/ppermute | solution.py:335
  17.1 5.3 %collective-permute-start.5 = (f32[16,320]{1,0:T(8,128)S(1)}, f32[16,320]{1,0:T(8,128)S(1)}, u32[]{:S(2)}, u32[]{:S(2)}) collective-permute-start(f32[16,320]{1,0:T(8,128)S(1)} %get-tuple-element.30.refs_5_), channel_id=1, source_target_pairs={{4,8},{8,4},{12,16},{16,12},{20,24},{24,20},{5,9},{9,5},{13,17},{1... | collective-permute-start | bytes 61448 | tf_op jit(solution)/shard_map/ppermute | solution.py:335
  19.9 3.8 %collective-permute-start.6 = (f32[16,320]{1,0:T(8,128)S(1)}, f32[16,320]{1,0:T(8,128)S(1)}, u32[]{:S(2)}, u32[]{:S(2)}) collective-permute-start(f32[16,320]{1,0:T(8,128)S(1)} %get-tuple-element.31.refs_6_), channel_id=1, source_target_pairs={{0,1},{1,0},{2,3},{3,2},{4,5},{5,4},{6,7},{7,6},{8,9},{9,8},{10,11... | collective-permute-start | bytes 61448 | tf_op jit(solution)/shard_map/ppermute | solution.py:335
  20.0 3.8 %collective-permute-start.7 = (f32[16,320]{1,0:T(8,128)S(1)}, f32[16,320]{1,0:T(8,128)S(1)}, u32[]{:S(2)}, u32[]{:S(2)}) collective-permute-start(f32[16,320]{1,0:T(8,128)S(1)} %get-tuple-element.32.refs_7_), channel_id=1, source_target_pairs={{1,2},{2,1},{5,6},{6,5},{9,10},{10,9},{13,14},{14,13},{17,18},{18,... | collective-permute-start | bytes 61448 | tf_op jit(solution)/shard_map/ppermute | solution.py:335
